TPU v7x, 32 devices: a whole 2x2x4 slice. The times are simulated.
32 devices in a mesh: dom: 16 (over z, y, core), orb: 2 (over x).
Axes of the slice: x: 2, y: 2, z: 4, core: 2. Of those that a mesh axis runs over, the one named last changes fastest.
Arguments:
- orbitals: float32 [6144, 1024], P('dom', 'orb'), may hold values from -6 to 6
- cell_mats: float32 [16, 512, 512], P('dom'), as said below
- cell_map: int32 [16, 512], P('dom'), may hold values from 0 to 511, as said below
Outputs:
- rotated: float32 [6144, 1024], P(('dom', 'orb'))
Inputs may be any that keep to these rules, and one draw needn't show every extreme that they name: `cell_map`: cell c belongs to domain c. Its 512 entries are distinct. Entries below 384 name the domain's own nodes, each used by some cell of the domain; an entry j >= 384 names own node j - 384 of the next domain, and every such j is used by some cell of the domain. `cell_mats`: each cell matrix is symmetric.
All inputs are finite; a program needn't handle non-finite values.
Results may differ from a plain program's by a relative error of at most 0.00013.
Values sent between devices are 32-bit elements; how exact they have to be, the bound alone decides.
No kernel may reach another device: no remote copies, remote signals or barrier semaphores. Data moves between devices by JAX's collectives and lax.ppermute only.
A program may use at most 64 MiB of HBM per device.

v0:
```python
import jax
import jax.numpy as jnp
from jax import lax
from jax.sharding import PartitionSpec as P

DEGREE = 5
HALO = 128


filter_center = 2.0
filter_half = 3.5


def shifted(block, axis, distance):
    devices = range(lax.axis_size(axis))
    route = [((i - distance) % len(devices), i) for i in devices]
    return lax.ppermute(block, axis, route)


def apply_local(vectors, cell_mats, cell_map):
    own_count = vectors.shape[0]
    borrowed = shifted(vectors[:HALO], "dom", -1)
    extended = jnp.concatenate([vectors, borrowed], axis=0)
    summed = jnp.zeros(extended.shape, jnp.float32)
    node_idx = cell_map[0]
    gathered = jnp.take(extended, node_idx, axis=0)
    product = jnp.dot(
        cell_mats[0], gathered, precision=lax.Precision.HIGHEST, preferred_element_type=jnp.float32
    )
    summed = summed.at[node_idx].add(product)
    returned = shifted(summed[own_count:], "dom", 1)
    return jnp.concatenate([summed[:HALO] + returned, summed[HALO:own_count]], axis=0)


def body(orbitals, cell_mats, cell_map):
    own_count = orbitals.shape[0]
    node_total = own_count * lax.axis_size("dom")
    previous = orbitals
    current = (apply_local(orbitals, cell_mats, cell_map) - filter_center * orbitals) / filter_half
    for order in range(1, DEGREE):
        advanced = (
            2.0
            * (apply_local(current, cell_mats, cell_map) - filter_center * current)
            / filter_half
            - previous
        )
        previous, current = (current, advanced)
    regrouped = lax.all_to_all(current, "orb", split_axis=0, concat_axis=1, tiled=True)
    local_gram = jnp.einsum("nk,nj->kj", regrouped, regrouped, precision=lax.Precision.HIGHEST)
    gram = lax.psum(local_gram, ("dom", "orb"))
    gram = gram / node_total
    lower = jnp.linalg.cholesky(gram)
    solved = lax.linalg.triangular_solve(lower, regrouped.T, left_side=True, lower=True)
    return solved.T


def solution(mesh):
    placed = (P("dom", "orb"), P("dom", None, None), P("dom", None))
    return jax.shard_map(
        body, mesh=mesh, in_specs=placed, out_specs=P(("dom", "orb"), None), check_vma=False
    )
```

profile of v0, /device:TPU:0, one launch (start us, length us, event | category | flops | bytes accessed | tf_op | source)
XLA Modules:
  0.0 657.8 jit_solution(3789338286109253911)
XLA Ops:
  7.6 5.5 collective-permute-start
  18.2 2.3 gather_fusion
  20.6 4.9 convolution_bitcast_fusion.4
  26.8 4.5 scatter_custom_fusion
  31.4 8.7 %collective-permute-done.1 = f32[128,512]{1,0:T(8,128)S(1)} collective-permute-done((f32[128,512]{1,0:T(8,128)S(1)}, f32[128,512]{1,0:T(8,128)S(1)}, u32[]{:S(2)}, u32[]{:S(2)}) %collective-permute-start.1) | collective-permute-done | bytes 262176 | tf_op jit(solution)/shard_map/ppermute | solution.py:17
  41.0 3.9 collective-permute-done.2
  44.9 2.3 gather_fusion.1
  47.3 4.8 convolution_bitcast_fusion.3
  53.4 4.5 scatter_custom_fusion.1
  58.1 8.7 %collective-permute-done.3 = f32[128,512]{1,0:T(8,128)S(1)} collective-permute-done((f32[128,512]{1,0:T(8,128)S(1)}, f32[128,512]{1,0:T(8,128)S(1)}, u32[]{:S(2)}, u32[]{:S(2)}) %collective-permute-start.3) | collective-permute-done | bytes 262176 | tf_op jit(solution)/shard_map/ppermute | solution.py:17
  68.3 3.9 collective-permute-done.4
  73.9 4.5 convolution_bitcast_fusion.2
  78.5 2.6 copy.21
  81.0 4.5 scatter_custom_fusion.2
  85.7 8.7 %collective-permute-done.5 = f32[128,512]{1,0:T(8,128)S(1)} collective-permute-done((f32[128,512]{1,0:T(8,128)S(1)}, f32[128,512]{1,0:T(8,128)S(1)}, u32[]{:S(2)}, u32[]{:S(2)}) %collective-permute-start.5) | collective-permute-done | bytes 262176 | tf_op jit(solution)/shard_map/ppermute | solution.py:17
  96.2 3.9 collective-permute-done.6
  100.1 2.3 gather_fusion.3
  102.5 5.8 convolution_bitcast_fusion.1
  108.3 2.6 copy.22
  110.9 5.3 scatter_custom_fusion.3
  118.3 7.7 %collective-permute-done.7 = f32[128,512]{1,0:T(8,128)S(1)} collective-permute-done((f32[128,512]{1,0:T(8,128)S(1)}, f32[128,512]{1,0:T(8,128)S(1)}, u32[]{:S(2)}, u32[]{:S(2)}) %collective-permute-start.7) | collective-permute-done | bytes 262176 | tf_op jit(solution)/shard_map/ppermute | solution.py:17
  127.8 3.9 collective-permute-done.8
  131.7 2.3 gather_fusion.4
  134.1 5.8 convolution_bitcast_fusion
  139.9 2.6 copy.23
  142.5 4.5 scatter_custom_fusion.4
  147.2 8.6 %collective-permute-done.9 = f32[128,512]{1,0:T(8,128)S(1)} collective-permute-done((f32[128,512]{1,0:T(8,128)S(1)}, f32[128,512]{1,0:T(8,128)S(1)}, u32[]{:S(2)}, u32[]{:S(2)}) %collective-permute-start.9) | collective-permute-done | bytes 262176 | tf_op jit(solution)/shard_map/ppermute | solution.py:17
  156.1 10.5 %all_to_all.19 = f32[2,192,512]{2,1,0:T(8,128)S(1)} all-to-all(f32[2,192,512]{2,1,0:T(8,128)S(1)} %bitcast.145), channel_id=1, replica_groups=mesh['dom'=16,'orb'=2] {'orb'}, dimensions={0} | all-to-all | bytes 1572864 | tf_op jit(solution)/shard_map/all_to_all | solution.py:48
  166.7 5.1 fusion.106
  171.8 139.4 %all-reduce.3.cloned.1.call-done = f32[1024,1024]{0,1:T(8,128)} async-done(((f32[1024,1024]{0,1:T(8,128)}), f32[1024,1024]{0,1:T(8,128)}) %all-reduce.3.cloned.1.call-update) | async-done | bytes 4194320 | tf_op jit(solution)/shard_map/psum | solution.py:50
  311.2 5.1 broadcast_multiply_fusion
  316.3 5.5 copy.26
  321.8 4.5 fusion
  328.2 11.7 %cholesky.223 = f32[128,128]{1,0:T(8,128)S(1)} custom-call(f32[128,128]{1,0:T(8,128)S(1)} %cholesky.580), custom_call_target="Cholesky" | custom-call | tf_op jit(solution)/shard_map/jit(cholesky)/cholesky | solution.py:52
  339.9 2.5 cholesky.255
  342.4 9.8 %custom-call.62 = f32[1,128,128]{1,2,0:T(8,128)S(1)} custom-call(f32[1,128,128]{2,1,0:T(8,128)S(1)} %get-tuple-element.70), custom_call_target="InvertDiagBlocksLowerTriangular" | custom-call | tf_op jit(solution)/shard_map/jit(cholesky)/cholesky | solution.py:52
  352.2 2.4 constant_dynamic-update-slice_fusion.31
  356.2 11.9 %cholesky.244 = f32[128,128]{1,0:T(8,128)S(1)} custom-call(f32[128,128]{1,0:T(8,128)S(1)} %cholesky.584), custom_call_target="Cholesky" | custom-call | tf_op jit(solution)/shard_map/jit(cholesky)/cholesky | solution.py:52
  368.7 9.8 %custom-call.63 = f32[1,128,128]{1,2,0:T(8,128)S(1)} custom-call(f32[1,128,128]{2,1,0:T(8,128)S(1)} %get-tuple-element.67), custom_call_target="InvertDiagBlocksLowerTriangular" | custom-call | tf_op jit(solution)/shard_map/jit(cholesky)/cholesky | solution.py:52
  381.9 11.7 %cholesky.468 = f32[128,128]{1,0:T(8,128)S(1)} custom-call(f32[128,128]{1,0:T(8,128)S(1)} %cholesky.589), custom_call_target="Cholesky" | custom-call | tf_op jit(solution)/shard_map/jit(cholesky)/cholesky | solution.py:52
  394.8 9.8 %custom-call.64 = f32[1,128,128]{1,2,0:T(8,128)S(1)} custom-call(f32[1,128,128]{2,1,0:T(8,128)S(1)} %get-tuple-element.64), custom_call_target="InvertDiagBlocksLowerTriangular" | custom-call | tf_op jit(solution)/shard_map/jit(cholesky)/cholesky | solution.py:52
  405.8 2.3 convolution_subtract_fusion.2
  408.2 12.1 %cholesky.487 = f32[128,128]{1,0:T(8,128)S(1)} custom-call(f32[128,128]{1,0:T(8,128)S(1)} %cholesky.594), custom_call_target="Cholesky" | custom-call | tf_op jit(solution)/shard_map/jit(cholesky)/cholesky | solution.py:52
  421.6 9.8 %custom-call.65 = f32[1,128,128]{1,2,0:T(8,128)S(1)} custom-call(f32[1,128,128]{2,1,0:T(8,128)S(1)} %get-tuple-element.61), custom_call_target="InvertDiagBlocksLowerTriangular" | custom-call | tf_op jit(solution)/shard_map/jit(cholesky)/cholesky | solution.py:52
  432.5 2.3 convolution_subtract_fusion.3
  434.8 11.7 %cholesky.506 = f32[128,128]{1,0:T(8,128)S(1)} custom-call(f32[128,128]{1,0:T(8,128)S(1)} %cholesky.599), custom_call_target="Cholesky" | custom-call | tf_op jit(solution)/shard_map/jit(cholesky)/cholesky | solution.py:52
  447.8 10.0 %custom-call.66 = f32[1,128,128]{1,2,0:T(8,128)S(1)} custom-call(f32[1,128,128]{2,1,0:T(8,128)S(1)} %get-tuple-element.58), custom_call_target="InvertDiagBlocksLowerTriangular" | custom-call | tf_op jit(solution)/shard_map/jit(cholesky)/cholesky | solution.py:52
  458.8 2.3 convolution_subtract_fusion.4
  461.1 11.7 %cholesky.526 = f32[128,128]{1,0:T(8,128)S(1)} custom-call(f32[128,128]{1,0:T(8,128)S(1)} %cholesky.604), custom_call_target="Cholesky" | custom-call | tf_op jit(solution)/shard_map/jit(cholesky)/cholesky | solution.py:52
  474.1 9.8 %custom-call.67 = f32[1,128,128]{1,2,0:T(8,128)S(1)} custom-call(f32[1,128,128]{2,1,0:T(8,128)S(1)} %get-tuple-element.55), custom_call_target="InvertDiagBlocksLowerTriangular" | custom-call | tf_op jit(solution)/shard_map/jit(cholesky)/cholesky | solution.py:52
  486.9 11.9 %cholesky.546 = f32[128,128]{1,0:T(8,128)S(1)} custom-call(f32[128,128]{1,0:T(8,128)S(1)} %cholesky.609), custom_call_target="Cholesky" | custom-call | tf_op jit(solution)/shard_map/jit(cholesky)/cholesky | solution.py:52
  500.1 9.8 %custom-call.68 = f32[1,128,128]{1,2,0:T(8,128)S(1)} custom-call(f32[1,128,128]{2,1,0:T(8,128)S(1)} %get-tuple-element.52), custom_call_target="InvertDiagBlocksLowerTriangular" | custom-call | tf_op jit(solution)/shard_map/jit(cholesky)/cholesky | solution.py:52
  512.5 11.7 %cholesky.564 = f32[128,128]{1,0:T(8,128)S(1)} custom-call(f32[128,128]{1,0:T(8,128)S(1)} %convolution_subtract_fusion.13), custom_call_target="Cholesky" | custom-call | tf_op jit(solution)/shard_map/jit(cholesky)/cholesky | solution.py:52
  531.1 4.8 select_select_fusion
  535.9 22.8 %while.1 = (s32[]{:T(128)}, f32[1024,1024]{1,0:T(8,128)}, s32[8,2]{0,1:T(2,128)S(1)}, f32[8,128,128]{2,1,0:T(8,128)S(1)}, s32[]{:T(128)}) while((s32[]{:T(128)}, f32[1024,1024]{1,0:T(8,128)}, s32[8,2]{0,1:T(2,128)S(1)}, f32[8,128,128]{2,1,0:T(8,128)S(1)}, s32[]{:T(128)}) %tuple.58), condition=%wide.while_cond, body=%wide.while_body.sunk | while | flops 2 | bytes 131181 | solution.py:53
  536.5 2.2 bitcast_dynamic-update-slice_fusion.2
  539.3 2.2 bitcast_dynamic-update-slice_fusion.2
  542.2 2.2 bitcast_dynamic-update-slice_fusion.2
  545.1 2.2 bitcast_dynamic-update-slice_fusion.2
  547.9 2.2 bitcast_dynamic-update-slice_fusion.2
  550.8 2.2 bitcast_dynamic-update-slice_fusion.2
  553.7 2.2 bitcast_dynamic-update-slice_fusion.2
  556.5 2.2 bitcast_dynamic-update-slice_fusion.2
  558.7 78.8 %custom-call.69 = f32[8,128,128]{1,2,0:T(8,128)S(1)} custom-call(f32[8,128,128]{2,1,0:T(8,128)S(1)} %get-tuple-element.13), custom_call_target="InvertDiagBlocksLowerTriangular" | custom-call | tf_op jit(solution)/shard_map/triangular_solve | solution.py:53
  (140 shorter events, 62.3 us)
Async XLA Ops:
  6.5 14.0 %copy-start = (f32[1,512,512]{2,1,0:T(8,128)S(1)}, f32[1,512,512]{2,1,0:T(8,128)}, u32[]{:S(2)}) copy-start(f32[1,512,512]{2,1,0:T(8,128)} %param.6) | copy-start | bytes 3145732
  6.5 304.6 %all-reduce.3.cloned.1.call-start = ((), (), s32[]{:S(2)}) async-start(), calls=%async_computation.1 | async-start | bytes 8388608 | tf_op jit(solution)/shard_map/psum | solution.py:50
  7.6 9.4 %collective-permute-start = (f32[128,512]{1,0:T(8,128)S(1)}, f32[128,512]{1,0:T(8,128)S(1)}, u32[]{:S(2)}, u32[]{:S(2)}) collective-permute-start(f32[128,512]{1,0:T(8,128)S(1)} %slice.283), channel_id=1, source_target_pairs={{2,0},{4,2},{6,4},{8,6},{10,8},{12,10},{14,12},{16,14},{18,16},{20... | collective-permute-start | bytes 786440 | tf_op jit(solution)/shard_map/ppermute | solution.py:17
  20.6 19.6 %copy-start.6 = (f32[384,512]{1,0:T(8,128)S(1)}, f32[384,512]{1,0:T(8,128)}, u32[]{:S(2)}) copy-start(f32[384,512]{1,0:T(8,128)} %param.5) | copy-start | bytes 2359300
  31.3 8.8 %collective-permute-start.1 = (f32[128,512]{1,0:T(8,128)S(1)}, f32[128,512]{1,0:T(8,128)S(1)}, u32[]{:S(2)}, u32[]{:S(2)}) collective-permute-start(f32[128,512]{1,0:T(8,128)S(1)} %slice.325), channel_id=1, source_target_pairs={{30,0},{0,2},{2,4},{4,6},{6,8},{8,10},{10,12},{12,14},{14,16},{16,... | collective-permute-start | bytes 786440 | tf_op jit(solution)/shard_map/ppermute | solution.py:17
  40.2 0.8 copy-start.10
  40.4 4.5 copy-start.7
  40.4 4.5 collective-permute-start.2
  57.9 8.8 %collective-permute-start.3 = (f32[128,512]{1,0:T(8,128)S(1)}, f32[128,512]{1,0:T(8,128)S(1)}, u32[]{:S(2)}, u32[]{:S(2)}) collective-permute-start(f32[128,512]{1,0:T(8,128)S(1)} %slice.329), channel_id=1, source_target_pairs={{30,0},{0,2},{2,4},{4,6},{6,8},{8,10},{10,12},{12,14},{14,16},{16,... | collective-permute-start | bytes 786440 | tf_op jit(solution)/shard_map/ppermute | solution.py:17
  68.0 4.2 copy-start.2
  68.1 4.1 collective-permute-start.4
  73.9 20.6 %copy-start.3 = (f32[384,512]{1,0:T(8,128)S(1)}, f32[384,512]{1,0:T(8,128)}, u32[]{:S(2)}) copy-start(f32[384,512]{1,0:T(8,128)} %copy-done.2) | copy-start | bytes 2359300
  85.6 8.8 %collective-permute-start.5 = (f32[128,512]{1,0:T(8,128)S(1)}, f32[128,512]{1,0:T(8,128)S(1)}, u32[]{:S(2)}, u32[]{:S(2)}) collective-permute-start(f32[128,512]{1,0:T(8,128)S(1)} %slice.333), channel_id=1, source_target_pairs={{30,0},{0,2},{2,4},{4,6},{6,8},{8,10},{10,12},{12,14},{14,16},{16,... | collective-permute-start | bytes 786440 | tf_op jit(solution)/shard_map/ppermute | solution.py:17
  95.9 4.2 collective-permute-start.6
  102.5 24.5 %copy-start.4 = (f32[384,512]{1,0:T(8,128)S(1)}, f32[384,512]{1,0:T(8,128)}, u32[]{:S(2)}) copy-start(f32[384,512]{1,0:T(8,128)} %copy-done.2) | copy-start | bytes 2359300
  117.2 8.8 %collective-permute-start.7 = (f32[128,512]{1,0:T(8,128)S(1)}, f32[128,512]{1,0:T(8,128)S(1)}, u32[]{:S(2)}, u32[]{:S(2)}) collective-permute-start(f32[128,512]{1,0:T(8,128)S(1)} %slice.337), channel_id=1, source_target_pairs={{30,0},{0,2},{2,4},{4,6},{6,8},{8,10},{10,12},{12,14},{14,16},{16,... | collective-permute-start | bytes 786440 | tf_op jit(solution)/shard_map/ppermute | solution.py:17
  127.2 4.4 copy-start.8
  127.3 4.4 collective-permute-start.8
  134.1 21.7 %copy-start.9 = (f32[384,512]{1,0:T(8,128)S(1)}, f32[384,512]{1,0:T(8,128)}, u32[]{:S(2)}) copy-start(f32[384,512]{1,0:T(8,128)} %copy-done.8) | copy-start | bytes 2359300
  147.0 8.7 %collective-permute-start.9 = (f32[128,512]{1,0:T(8,128)S(1)}, f32[128,512]{1,0:T(8,128)S(1)}, u32[]{:S(2)}, u32[]{:S(2)}) collective-permute-start(f32[128,512]{1,0:T(8,128)S(1)} %slice.341), channel_id=1, source_target_pairs={{30,0},{0,2},{2,4},{4,6},{6,8},{8,10},{10,12},{12,14},{14,16},{16,... | collective-permute-start | bytes 786440 | tf_op jit(solution)/shard_map/ppermute | solution.py:17
  326.2 1.9 copy-start.5
  639.2 11.5 %copy-start.1 = (f32[1,512,512]{2,1,0:T(8,128)S(1)}, f32[1,512,512]{2,1,0:T(8,128)}, u32[]{:S(2)}) copy-start(f32[1,512,512]{2,1,0:T(8,128)} %param.6) | copy-start | bytes 3145732
  649.8 0.9 copy-start.11
Sparse Core Ops, SparseCore 0:
  171.9 139.2 all-reduce.2
where the time goes:
time: 666 us; the launch traced here: 658 us
  other arithmetic  297 us (45%)
  waiting for transfers between devices  199 us (30%)
  matrix products  66.2 us (10%)
  local copies, waits for them, and re-layouts  58.5 us (9%)
  between operations  19.2 us (3%)
  blocking collectives  10.5 us (2%)
  starting transfers between devices  7.36 us (1%)
    another operation x30, other arithmetic, body(): lower = jnp.linalg.cholesky(gram)  172 us
    psum x1, waiting for transfers between devices, body(): gram = lax.psum(local_gram, ('dom', 'orb'))  139 us
    another operation x3, other arithmetic, body(): lax.linalg.triangular_solve(lower, regrouped.T, left_side=True, lower=True)  83.6 us
    ppermute x10, waiting for transfers between devices, shifted(): return lax.ppermute(block, axis, route)  59.7 us
    dot_general x5, matrix products, apply_local(): jnp.dot(cell_mats[0], gathered, precision=lax.Precision.HIGHEST, preferre...  25.9 us
    scatter-add x5, other arithmetic, apply_local(): summed = summed.at[node_idx].add(product)  23.3 us
    another operation x14, matrix products, body(): lower = jnp.linalg.cholesky(gram)  23.1 us
    another operation x24, local copies, waits for them, and re-layouts  22.7 us
  transfers between devices with their start and end apart: 11, of which 11 were waited for; matrix products, arithmetic and copies ran while one was open for 1% of the time, Pallas kernels for 0%

commit v1 on v0

v1 whole, which is shorter than its diff:
```python
import jax
import jax.numpy as jnp
from jax import lax
from jax.experimental import pallas as pl
from jax.experimental.pallas import tpu as pltpu
from jax.sharding import PartitionSpec as P

DEGREE = 5

filter_center = 2.0
filter_half = 3.5

F32, BF16 = jnp.float32, jnp.bfloat16
LANES, SUB = 128, 8
VMEM_BYTES = 48 << 20


def kernel_call(body, out_shape, scratch=()):
    return pl.pallas_call(
        body,
        out_shape=out_shape,
        scratch_shapes=list(scratch),
        compiler_params=pltpu.CompilerParams(vmem_limit_bytes=VMEM_BYTES),
    )


def f32(*shape):
    return jax.ShapeDtypeStruct(shape, F32)


def bf16(*shape):
    return jax.ShapeDtypeStruct(shape, BF16)


def split(v):
    hi = v.astype(BF16)
    return hi, (v - hi.astype(F32)).astype(BF16)


def contract(a, b, dims):
    return lax.dot_general(a, b, (dims, ((), ())), preferred_element_type=F32)


def product(a, b, dims):
    (a_hi, a_lo), (b_hi, b_lo) = a, b
    return contract(a_hi, b_hi, dims) + (contract(a_hi, b_lo, dims) + contract(a_lo, b_hi, dims))


NN = ((1,), (0,))
NT = ((1,), (1,))


def order_kernel(map_ref, cell_ref, hi_ref, lo_ref):
    size = cell_ref.shape[1]
    node = lax.broadcasted_iota(jnp.int32, (size, size), 0)
    pick = jnp.where(node == map_ref[...], 1.0, 0.0).astype(BF16)
    for half, out_ref in zip(split(cell_ref[0]), (hi_ref, lo_ref)):
        rows = contract(pick, half, NN).astype(BF16)
        out_ref[...] = contract(rows, pick, NT).astype(BF16)


def step_kernel(order, own, hi_ref, lo_ref, *refs):
    size = hi_ref.shape[0]
    halo = size - own
    if order == 0:
        own_ref, bottom_ref = refs[:2]
        vec = jnp.concatenate([own_ref[...], bottom_ref[...]], axis=0)
        outs = refs[2:]
    else:
        part_ref, top_ref, bottom_ref = refs[:3]
        vec = jnp.concatenate(
            [
                part_ref[:halo, :] + top_ref[...],
                part_ref[halo:own, :],
                part_ref[own:, :] + bottom_ref[...],
            ],
            axis=0,
        )
        outs = refs[3:]
    if order > 0:
        before_ref, outs = outs[0], outs[1:]
    scale = (1.0 if order == 0 else 2.0) / filter_half
    applied = product((hi_ref[...], lo_ref[...]), split(vec), NN) * scale
    part = applied - (filter_center * scale) * vec
    if order > 0:
        part = part - before_ref[...]
    if order == DEGREE - 1:
        next_ref, down_ref = outs
        next_ref[...] = part[:own]
    else:
        now_ref, next_ref, up_ref, down_ref = outs
        now_ref[...] = vec
        next_ref[...] = part
        up_ref[...] = applied[:halo]
    down_ref[...] = applied[own:]


def shifted(block, axis, distance):
    count = lax.axis_size(axis)
    route = [((i - distance) % count, i) for i in range(count)]
    return lax.ppermute(block, axis, route)


def filtered_columns(orbitals, matrix):
    own, cols = orbitals.shape
    size = matrix[0].shape[0]
    halo = size - own
    bottom = shifted(orbitals[:halo], "dom", -1)
    state = (orbitals, bottom)
    for order in range(DEGREE):
        last = order == DEGREE - 1
        outs = [f32(own if last else size, cols)]
        if not last:
            outs = [f32(size, cols)] + outs + [f32(halo, cols)]
        outs.append(f32(halo, cols))
        body = lambda *refs, order=order: step_kernel(order, own, *refs)
        got = kernel_call(body, outs)(*matrix, *state)
        if last:
            part, down = got
            top = shifted(down, "dom", 1)
            return jnp.concatenate([part[:halo] + top, part[halo:]], axis=0)
        now, part, up, down = got
        top = shifted(down, "dom", 1)
        bottom = shifted(up, "dom", -1)
        state = (part, top, bottom, now)


def gram_kernel(rows_ref, out_ref):
    hi, lo = split(rows_ref[...].T)
    panels = hi.shape[0] // LANES
    at = 0
    for p in range(panels):
        cut = slice(p * LANES, (p + 1) * LANES)
        below = hi.shape[0] - p * LANES
        out_ref[at : at + below, :] = product((hi[p * LANES :], lo[p * LANES :]), (hi[cut], lo[cut]), NT)
        at += below


def exchanged(block, axis, bit):
    route = [(i, i ^ bit) for i in range(lax.axis_size(axis))]
    return lax.ppermute(block, axis, route)


def summed(block, stages):
    for axis, bit in stages:
        half = block.shape[0] // 2
        upper = (lax.axis_index(axis) & bit) != 0
        pair = block.reshape(2, half, block.shape[1])
        keep = jnp.where(upper, pair[1], pair[0])
        send = jnp.where(upper, pair[0], pair[1])
        block = keep + exchanged(send, axis, bit)
    for axis, bit in reversed(stages):
        upper = (lax.axis_index(axis) & bit) != 0
        other = exchanged(block, axis, bit)
        block = jnp.concatenate([jnp.where(upper, other, block), jnp.where(upper, block, other)], axis=0)
    return block


def bits(axis):
    count = lax.axis_size(axis)
    return [(axis, 1 << i) for i in range(count.bit_length() - 1)]


def inverse_factor(block, out_ref):
    size = block.shape[0]
    rows = [block[t : t + SUB] for t in range(0, size, SUB)]
    sub = lax.broadcasted_iota(jnp.int32, (SUB, size), 0)
    lane = lax.broadcasted_iota(jnp.int32, (SUB, size), 1)
    for b in range(size // SUB):
        at = b * SUB
        here = (lane >= at) & (lane < at + SUB)
        top = rows[b]
        cols = [jnp.broadcast_to(top[:, at + k : at + k + 1], (SUB, size)) for k in range(SUB)]
        top = jnp.where(here, jnp.where(lane - at == sub, 1.0, 0.0), top)
        scale = jnp.zeros((SUB, size), F32)
        done = jnp.zeros((SUB, size), F32)
        for k in range(SUB):
            pivot = jnp.broadcast_to(cols[k][k : k + 1], (SUB, size))
            inverse = 1.0 / pivot
            row = jnp.broadcast_to(top[k : k + 1], (SUB, size))
            done = jnp.where(sub == k, row * lax.rsqrt(pivot), done)
            scale = jnp.where(sub == k, inverse, scale)
            ratio = jnp.where(sub == k, 0.0, cols[k] * inverse)
            top = top - ratio * row
            for m in range(k + 1, SUB):
                cols[m] = cols[m] - ratio * jnp.broadcast_to(cols[m][k : k + 1], (SUB, size))
        out_ref[at : at + SUB, :] = jnp.where(lane < at + SUB, done, 0.0)
        top = top * scale
        for t in range(b + 1, size // SUB):
            left = rows[t]
            kept = jnp.where(here, 0.0, left)
            for k in range(SUB):
                column = jnp.broadcast_to(left[:, at + k : at + k + 1], (SUB, size))
                kept = kept - column * jnp.broadcast_to(top[k : k + 1], (SUB, size))
            rows[t] = kept


def factor_kernel(scale, gram_ref, rows_ref, out_ref, work_ref, hi_ref, lo_ref, inverse_ref):
    panels, total = work_ref.shape[:2]
    size = panels * LANES
    at = 0
    for p in range(panels):
        below = size - p * LANES
        work_ref[p, size - below : size, :] = gram_ref[at : at + below, :] * scale
        work_ref[p, size:, :] = rows_ref[:, p * LANES : (p + 1) * LANES]
        if p > 0:
            work_ref[p, : size - below, :] = jnp.zeros((size - below, LANES), F32)
        at += below

    def panel(p, carry):
        offset = pl.multiple_of(p * LANES, LANES)

        def update(k, inner):
            mine = pl.ds(offset, LANES)
            pair = (hi_ref[k, mine, :], lo_ref[k, mine, :])
            work_ref[p] = work_ref[p] - product((hi_ref[k], lo_ref[k]), pair, NT)
            return inner

        lax.fori_loop(0, p, update, 0)
        inverse_factor(work_ref[p, pl.ds(offset, LANES), :], inverse_ref)
        solved = product(split(work_ref[p]), split(inverse_ref[...]), NT)
        hi_ref[p], lo_ref[p] = split(solved)
        work_ref[p] = solved
        return carry

    lax.fori_loop(0, panels, panel, 0)
    for p in range(panels):
        out_ref[:, p * LANES : (p + 1) * LANES] = work_ref[p, size:, :]


def body(orbitals, cell_mats, cell_map):
    own, cols = orbitals.shape
    size = cell_mats.shape[1]
    node_total = own * lax.axis_size("dom")
    matrix = kernel_call(order_kernel, [bf16(size, size)] * 2)(cell_map, cell_mats)
    current = filtered_columns(orbitals, matrix)
    regrouped = lax.all_to_all(current, "orb", split_axis=0, concat_axis=1, tiled=True)
    count, width = regrouped.shape
    panels = width // LANES
    packed = LANES * panels * (panels + 1) // 2
    gram = kernel_call(gram_kernel, f32(packed, LANES))(regrouped)
    dom = bits("dom")
    gram = summed(gram, dom[:1] + bits("orb") + dom[1:])
    scratch = [
        pltpu.VMEM((panels, width + count, LANES), F32),
        pltpu.VMEM((panels, width + count, LANES), BF16),
        pltpu.VMEM((panels, width + count, LANES), BF16),
        pltpu.VMEM((LANES, LANES), F32),
    ]
    factor = lambda *refs: factor_kernel(1.0 / node_total, *refs)
    return kernel_call(factor, f32(count, width), scratch)(gram, regrouped)


def solution(mesh):
    placed = (P("dom", "orb"), P("dom", None, None), P("dom", None))
    return jax.shard_map(
        body, mesh=mesh, in_specs=placed, out_specs=P(("dom", "orb"), None), check_vma=False
    )
```

time: 666 us -> 209 us (0.31); the launches traced: 658 us -> 208 us
  other arithmetic: 297 us -> 5.74 us
  waiting for transfers between devices: 199 us -> 101 us
  matrix products: 66.2 us -> 0 us
  Pallas kernels: 0 us -> 65.6 us
  local copies, waits for them, and re-layouts: 58.5 us -> 7 us
  starting transfers between devices: 7.36 us -> 28.4 us
  between operations: 19.2 us -> 0.33 us
  blocking collectives: 10.5 us -> 0 us
    another operation x33 -> x0, other arithmetic: 256 us -> none  [the longest x30 172 us: body(): lower = jnp.linalg.cholesky(gram)]
    psum x1 -> x0, waiting for transfers between devices: 139 us -> none  [body(): gram = lax.psum(local_gram, ('dom', 'orb'))]
    ppermute x0 -> x10, waiting for transfers between devices: none -> 68.1 us  [exchanged(): return lax.ppermute(block, axis, route)]
    pallas_call x0 -> x8, Pallas kernels: none -> 65.6 us  [the longest x1 53.3 us: body(): return kernel_call(factor, f32(count, width), scratch)(gram, regrouped)]
    another operation x29 -> x0, matrix products: 35.2 us -> none  [the longest x14 23.1 us: body(): lower = jnp.linalg.cholesky(gram)]
    ppermute x10, waiting for transfers between devices: 59.7 us -> 25.5 us  [shifted(): return lax.ppermute(block, axis, route)]
    dot_general x6 -> x0, matrix products: 31 us -> none  [the longest x5 25.9 us: apply_local(): jnp.dot(cell_mats[0], gathered, precision=lax.Precision.HIGHEST, preferre...]
    another operation x33 -> x0, local copies, waits for them, and re-layouts: 25.2 us -> none
  transfers between devices with their start and end apart: 11 -> 21, of which waited for: 11 -> 17; matrix products, arithmetic and copies ran while one was open for 1% -> 0% of each run, Pallas kernels for 0% -> 1%
where the time goes in v1:
time: 209 us; the launch traced here: 208 us
  waiting for transfers between devices  101 us (48%)
  Pallas kernels  65.6 us (31%)
  starting transfers between devices  28.4 us (14%)
  local copies, waits for them, and re-layouts  7 us (3%)
  other arithmetic  5.74 us (3%)
    ppermute x10, waiting for transfers between devices, exchanged(): return lax.ppermute(block, axis, route)  68.1 us
    pallas_call x1, Pallas kernels, body(): return kernel_call(factor, f32(count, width), scratch)(gram, regrouped)  53.3 us
    ppermute x10, waiting for transfers between devices, shifted(): return lax.ppermute(block, axis, route)  25.5 us
    ppermute x10, starting transfers between devices, shifted(): return lax.ppermute(block, axis, route)  23.6 us
    pallas_call x5, Pallas kernels, filtered_columns(): got = kernel_call(body, outs)(*matrix, *state)  8.93 us
    all_to_all x1, waiting for transfers between devices, body(): lax.all_to_all(current, 'orb', split_axis=0, concat_axis=1, tiled=True)  7.78 us
    unnamed x14, local copies, waits for them, and re-layouts  5.87 us
  transfers between devices with their start and end apart: 21, of which 17 were waited for; matrix products, arithmetic and copies ran while one was open for 0% of the time, Pallas kernels for 1%

profile of v1, /device:TPU:0, one launch (start us, length us, event | category | flops | bytes accessed | tf_op | source)
XLA Modules:
  0.0 208.5 jit_solution(13298865499319195548)
XLA Ops:
  0.0 1.0 slice.59
  1.0 5.5 %collective-permute-start = (f32[128,512]{1,0:T(8,128)S(1)}, f32[128,512]{1,0:T(8,128)S(1)}, u32[]{:S(2)}, u32[]{:S(2)}) collective-permute-start(f32[128,512]{1,0:T(8,128)S(1)} %slice.59), channel_id=1, source_target_pairs={{2,0},{4,2},{6,4},{8,6},{10,8},{12,10},{14,12},{16,14},{18,16},{20... | collective-permute-start | bytes 786440 | tf_op jit(solution)/shard_map/ppermute | solution.py:101
  6.6 1.2 copy-done.4
  7.8 0.7 copy-done.5
  8.5 1.3 shard_map.37
  9.7 0.7 collective-permute-done.refs_3_
  10.5 1.0 shard_map.38
  11.5 1.0 copy-done.3
  12.5 0.0 collective-permute-start.1
  12.5 4.6 %collective-permute-start.2 = (f32[128,512]{1,0:T(8,128)S(1)}, f32[128,512]{1,0:T(8,128)S(1)}, u32[]{:S(2)}, u32[]{:S(2)}) collective-permute-start(f32[128,512]{1,0:T(8,128)S(1)} %get-tuple-element.29), channel_id=1, source_target_pairs={{2,0},{4,2},{6,4},{8,6},{10,8},{12,10},{14,12},{16,14},{18,16},{20... | collective-permute-start | bytes 786440 | tf_op jit(solution)/shard_map/ppermute | solution.py:101
  17.1 4.1 %collective-permute-done.1.refs_3_ = f32[128,512]{1,0:T(8,128)S(1)} collective-permute-done((f32[128,512]{1,0:T(8,128)S(1)}, f32[128,512]{1,0:T(8,128)S(1)}, u32[]{:S(2)}, u32[]{:S(2)}) %collective-permute-start.1) | collective-permute-done | bytes 262176 | tf_op jit(solution)/shard_map/ppermute | solution.py:101
  21.1 0.0 collective-permute-done.2.refs_4_
  21.1 2.3 %shard_map.39 = (f32[512,512]{1,0:T(8,128)S(1)}, f32[512,512]{1,0:T(8,128)S(1)}, f32[128,512]{1,0:T(8,128)S(1)}, f32[128,512]{1,0:T(8,128)S(1)}) custom-call(bf16[512,512]{1,0:T(8,128)(2,1)S(1)} %get-tuple-element.25.refs_0_, bf16[512,512]{1,0:T(8,128)(2,1)S(1)} %get-tuple-element.26.refs_1_, f32[512,512]{1,0:T(8,128)S(1)} %get-tuple-element.27.refs_2_, ...), custom_call_target="tpu_custom_call" | custom-call | tf_op jit(solution)/shard_map/pallas_call | solution.py:117
  23.4 1.0 copy-done.1
  24.4 0.0 collective-permute-start.3
  24.4 4.4 %collective-permute-start.4 = (f32[128,512]{1,0:T(8,128)S(1)}, f32[128,512]{1,0:T(8,128)S(1)}, u32[]{:S(2)}, u32[]{:S(2)}) collective-permute-start(f32[128,512]{1,0:T(8,128)S(1)} %get-tuple-element.33), channel_id=1, source_target_pairs={{2,0},{4,2},{6,4},{8,6},{10,8},{12,10},{14,12},{16,14},{18,16},{20... | collective-permute-start | bytes 786440 | tf_op jit(solution)/shard_map/ppermute | solution.py:101
  28.9 4.1 %collective-permute-done.3.refs_3_ = f32[128,512]{1,0:T(8,128)S(1)} collective-permute-done((f32[128,512]{1,0:T(8,128)S(1)}, f32[128,512]{1,0:T(8,128)S(1)}, u32[]{:S(2)}, u32[]{:S(2)}) %collective-permute-start.3) | collective-permute-done | bytes 262176 | tf_op jit(solution)/shard_map/ppermute | solution.py:101
  32.9 0.0 collective-permute-done.4.refs_4_
  32.9 2.3 %shard_map.40 = (f32[512,512]{1,0:T(8,128)S(1)}, f32[512,512]{1,0:T(8,128)S(1)}, f32[128,512]{1,0:T(8,128)S(1)}, f32[128,512]{1,0:T(8,128)S(1)}) custom-call(bf16[512,512]{1,0:T(8,128)(2,1)S(1)} %get-tuple-element.25.refs_0_, bf16[512,512]{1,0:T(8,128)(2,1)S(1)} %get-tuple-element.26.refs_1_, f32[512,512]{1,0:T(8,128)S(1)} %get-tuple-element.31.refs_2_, ...), custom_call_target="tpu_custom_call" | custom-call | tf_op jit(solution)/shard_map/pallas_call | solution.py:117
  35.2 1.0 copy-done.2
  36.2 4.4 %collective-permute-start.6 = (f32[128,512]{1,0:T(8,128)S(1)}, f32[128,512]{1,0:T(8,128)S(1)}, u32[]{:S(2)}, u32[]{:S(2)}) collective-permute-start(f32[128,512]{1,0:T(8,128)S(1)} %get-tuple-element.37), channel_id=1, source_target_pairs={{2,0},{4,2},{6,4},{8,6},{10,8},{12,10},{14,12},{16,14},{18,16},{20... | collective-permute-start | bytes 786440 | tf_op jit(solution)/shard_map/ppermute | solution.py:101
  40.6 4.1 %collective-permute-done.5.refs_3_ = f32[128,512]{1,0:T(8,128)S(1)} collective-permute-done((f32[128,512]{1,0:T(8,128)S(1)}, f32[128,512]{1,0:T(8,128)S(1)}, u32[]{:S(2)}, u32[]{:S(2)}) %collective-permute-start.5) | collective-permute-done | bytes 262176 | tf_op jit(solution)/shard_map/ppermute | solution.py:101
  44.8 0.0 collective-permute-done.6.refs_4_
  44.8 2.3 %shard_map.41 = (f32[512,512]{1,0:T(8,128)S(1)}, f32[512,512]{1,0:T(8,128)S(1)}, f32[128,512]{1,0:T(8,128)S(1)}, f32[128,512]{1,0:T(8,128)S(1)}) custom-call(bf16[512,512]{1,0:T(8,128)(2,1)S(1)} %get-tuple-element.25.refs_0_, bf16[512,512]{1,0:T(8,128)(2,1)S(1)} %get-tuple-element.26.refs_1_, f32[512,512]{1,0:T(8,128)S(1)} %get-tuple-element.35.refs_2_, ...), custom_call_target="tpu_custom_call" | custom-call | tf_op jit(solution)/shard_map/pallas_call | solution.py:117
  47.1 0.1 collective-permute-start.7
  47.2 4.4 %collective-permute-start.8 = (f32[128,512]{1,0:T(8,128)S(1)}, f32[128,512]{1,0:T(8,128)S(1)}, u32[]{:S(2)}, u32[]{:S(2)}) collective-permute-start(f32[128,512]{1,0:T(8,128)S(1)} %get-tuple-element.41), channel_id=1, source_target_pairs={{2,0},{4,2},{6,4},{8,6},{10,8},{12,10},{14,12},{16,14},{18,16},{20... | collective-permute-start | bytes 786440 | tf_op jit(solution)/shard_map/ppermute | solution.py:101
  51.6 4.1 %collective-permute-done.7.refs_3_ = f32[128,512]{1,0:T(8,128)S(1)} collective-permute-done((f32[128,512]{1,0:T(8,128)S(1)}, f32[128,512]{1,0:T(8,128)S(1)}, u32[]{:S(2)}, u32[]{:S(2)}) %collective-permute-start.7) | collective-permute-done | bytes 262176 | tf_op jit(solution)/shard_map/ppermute | solution.py:101
  55.7 1.0 shard_map.42
  56.7 0.1 collective-permute-start.9
  56.8 8.5 %collective-permute-done.9 = f32[128,512]{1,0:T(8,128)S(1)} collective-permute-done((f32[128,512]{1,0:T(8,128)S(1)}, f32[128,512]{1,0:T(8,128)S(1)}, u32[]{:S(2)}, u32[]{:S(2)}) %collective-permute-start.9) | collective-permute-done | bytes 262176 | tf_op jit(solution)/shard_map/ppermute | solution.py:101
  65.3 0.9 pad_maximum_fusion.2
  66.3 3.7 %all-to-all-start = ((f32[2,192,512]{2,1,0:T(8,128)}), f32[2,192,512]{2,1,0:T(8,128)S(1)}, u32[]{:S(2)}, u32[]{:S(2)}) async-start(f32[2,192,512]{2,1,0:T(8,128)} %bitcast), calls=%async_computation | async-start | bytes 1572864 | tf_op jit(solution)/shard_map/all_to_all | solution.py:237
  70.0 7.8 %all-to-all-done = f32[2,192,512]{2,1,0:T(8,128)S(1)} async-done(((f32[2,192,512]{2,1,0:T(8,128)}), f32[2,192,512]{2,1,0:T(8,128)S(1)}, u32[]{:S(2)}, u32[]{:S(2)}) %all-to-all-start) | async-done | bytes 786464 | tf_op jit(solution)/shard_map/all_to_all | solution.py:237
  77.8 0.1 copy.6
  77.8 2.1 %shard_map.43 = f32[4608,128]{1,0:T(8,128)S(1)} custom-call(f32[192,1024]{1,0:T(8,128)S(1)} %bitcast.4), custom_call_target="tpu_custom_call" | custom-call | tf_op jit(solution)/shard_map/pallas_call | solution.py:241
  80.0 1.2 slice_select_fusion
  81.1 3.2 %collective-permute-done.10 = f32[2304,128]{1,0:T(8,128)} collective-permute-done((f32[2304,128]{1,0:T(8,128)}, f32[2304,128]{1,0:T(8,128)}, u32[]{:S(2)}, u32[]{:S(2)}) %collective-permute-start.10) | collective-permute-done | bytes 1179680 | tf_op jit(solution)/shard_map/ppermute | solution.py:141
  84.3 1.4 select_add_fusion
  85.8 1.0 copy-done.6
  86.8 0.1 slice_select_fusion.1
  86.9 0.3 collective-permute-start.11
  87.1 15.2 %collective-permute-done.11 = f32[1152,128]{1,0:T(8,128)S(1)} collective-permute-done((f32[1152,128]{1,0:T(8,128)S(1)}, f32[1152,128]{1,0:T(8,128)S(1)}, u32[]{:S(2)}, u32[]{:S(2)}) %collective-permute-start.11) | collective-permute-done | bytes 589856 | tf_op jit(solution)/shard_map/ppermute | solution.py:141
  102.3 1.3 select_add_fusion.1
  103.7 0.1 collective-permute-start.12
  103.8 8.2 %collective-permute-done.12 = f32[576,128]{1,0:T(8,128)S(1)} collective-permute-done((f32[576,128]{1,0:T(8,128)S(1)}, f32[576,128]{1,0:T(8,128)S(1)}, u32[]{:S(2)}, u32[]{:S(2)}) %collective-permute-start.12) | collective-permute-done | bytes 294944 | tf_op jit(solution)/shard_map/ppermute | solution.py:141
  112.0 0.1 collective-permute-start.13
  112.1 5.1 %collective-permute-done.13 = f32[288,128]{1,0:T(8,128)S(1)} collective-permute-done((f32[288,128]{1,0:T(8,128)S(1)}, f32[288,128]{1,0:T(8,128)S(1)}, u32[]{:S(2)}, u32[]{:S(2)}) %collective-permute-start.13) | collective-permute-done | bytes 147488 | tf_op jit(solution)/shard_map/ppermute | solution.py:141
  117.3 0.1 collective-permute-start.14
  117.4 7.0 %collective-permute-done.14 = f32[144,128]{1,0:T(8,128)S(1)} collective-permute-done((f32[144,128]{1,0:T(8,128)S(1)}, f32[144,128]{1,0:T(8,128)S(1)}, u32[]{:S(2)}, u32[]{:S(2)}) %collective-permute-start.14) | collective-permute-done | bytes 73760 | tf_op jit(solution)/shard_map/ppermute | solution.py:141
  124.3 0.1 collective-permute-start.15
  124.4 5.2 %collective-permute-done.15 = f32[144,128]{1,0:T(8,128)S(1)} collective-permute-done((f32[144,128]{1,0:T(8,128)S(1)}, f32[144,128]{1,0:T(8,128)S(1)}, u32[]{:S(2)}, u32[]{:S(2)}) %collective-permute-start.15) | collective-permute-done | bytes 73760 | tf_op jit(solution)/shard_map/ppermute | solution.py:141
  129.7 0.1 collective-permute-start.16
  129.8 5.1 %collective-permute-done.16 = f32[288,128]{1,0:T(8,128)S(1)} collective-permute-done((f32[288,128]{1,0:T(8,128)S(1)}, f32[288,128]{1,0:T(8,128)S(1)}, u32[]{:S(2)}, u32[]{:S(2)}) %collective-permute-start.16) | collective-permute-done | bytes 147488 | tf_op jit(solution)/shard_map/ppermute | solution.py:141
  134.9 0.1 collective-permute-start.17
  135.0 6.7 %collective-permute-done.17 = f32[576,128]{1,0:T(8,128)S(1)} collective-permute-done((f32[576,128]{1,0:T(8,128)S(1)}, f32[576,128]{1,0:T(8,128)S(1)}, u32[]{:S(2)}, u32[]{:S(2)}) %collective-permute-start.17) | collective-permute-done | bytes 294944 | tf_op jit(solution)/shard_map/ppermute | solution.py:141
  141.8 0.4 collective-permute-start.18
  142.2 9.5 %collective-permute-done.18 = f32[1152,128]{1,0:T(8,128)S(1)} collective-permute-done((f32[1152,128]{1,0:T(8,128)S(1)}, f32[1152,128]{1,0:T(8,128)S(1)}, u32[]{:S(2)}, u32[]{:S(2)}) %collective-permute-start.18) | collective-permute-done | bytes 589856 | tf_op jit(solution)/shard_map/ppermute | solution.py:141
  151.8 0.1 broadcast_select_fusion.3
  151.9 0.1 pad_maximum_fusion.1
  151.9 0.1 collective-permute-start.19
  152.0 2.8 %collective-permute-done.19 = f32[2304,128]{1,0:T(8,128)S(1)} collective-permute-done((f32[2304,128]{1,0:T(8,128)S(1)}, f32[2304,128]{1,0:T(8,128)S(1)}, u32[]{:S(2)}, u32[]{:S(2)}) %collective-permute-start.19) | collective-permute-done | bytes 1179680 | tf_op jit(solution)/shard_map/ppermute | solution.py:141
  154.9 0.2 broadcast_select_fusion.1
  155.0 0.2 pad_maximum_fusion.refs_0_
  155.2 53.3 %shard_map.44 = f32[192,1024]{1,0:T(8,128)} custom-call(f32[4608,128]{1,0:T(8,128)S(1)} %pad_maximum_fusion.refs_0_, f32[192,1024]{1,0:T(8,128)S(1)} %bitcast.5), custom_call_target="tpu_custom_call" | custom-call | tf_op jit(solution)/shard_map/pallas_call | solution.py:251
  (25 shorter events, 0.4 us)
Async XLA Ops:
  0.0 10.5 %copy-start = (f32[384,512]{1,0:T(8,128)S(1)}, f32[384,512]{1,0:T(8,128)}, u32[]{:S(2)}) copy-start(f32[384,512]{1,0:T(8,128)} %refs_2_.1) | copy-start | bytes 2359300
  1.0 9.4 %collective-permute-start = (f32[128,512]{1,0:T(8,128)S(1)}, f32[128,512]{1,0:T(8,128)S(1)}, u32[]{:S(2)}, u32[]{:S(2)}) collective-permute-start(f32[128,512]{1,0:T(8,128)S(1)} %slice.59), channel_id=1, source_target_pairs={{2,0},{4,2},{6,4},{8,6},{10,8},{12,10},{14,12},{16,14},{18,16},{20... | collective-permute-start | bytes 786440 | tf_op jit(solution)/shard_map/ppermute | solution.py:101
  6.6 1.2 copy-start.4
  7.8 0.7 copy-start.5
  11.5 1.0 copy-start.3
  12.5 8.7 %collective-permute-start.1 = (f32[128,512]{1,0:T(8,128)S(1)}, f32[128,512]{1,0:T(8,128)S(1)}, u32[]{:S(2)}, u32[]{:S(2)}) collective-permute-start(f32[128,512]{1,0:T(8,128)S(1)} %get-tuple-element.28), channel_id=1, source_target_pairs={{30,0},{0,2},{2,4},{4,6},{6,8},{8,10},{10,12},{12,14},{14,16},{16,... | collective-permute-start | bytes 786440 | tf_op jit(solution)/shard_map/ppermute | solution.py:101
  12.5 8.7 %collective-permute-start.2 = (f32[128,512]{1,0:T(8,128)S(1)}, f32[128,512]{1,0:T(8,128)S(1)}, u32[]{:S(2)}, u32[]{:S(2)}) collective-permute-start(f32[128,512]{1,0:T(8,128)S(1)} %get-tuple-element.29), channel_id=1, source_target_pairs={{2,0},{4,2},{6,4},{8,6},{10,8},{12,10},{14,12},{16,14},{18,16},{20... | collective-permute-start | bytes 786440 | tf_op jit(solution)/shard_map/ppermute | solution.py:101
  23.4 1.0 copy-start.1
  24.4 8.5 %collective-permute-start.3 = (f32[128,512]{1,0:T(8,128)S(1)}, f32[128,512]{1,0:T(8,128)S(1)}, u32[]{:S(2)}, u32[]{:S(2)}) collective-permute-start(f32[128,512]{1,0:T(8,128)S(1)} %get-tuple-element.32), channel_id=1, source_target_pairs={{30,0},{0,2},{2,4},{4,6},{6,8},{8,10},{10,12},{12,14},{14,16},{16,... | collective-permute-start | bytes 786440 | tf_op jit(solution)/shard_map/ppermute | solution.py:101
  24.4 8.5 %collective-permute-start.4 = (f32[128,512]{1,0:T(8,128)S(1)}, f32[128,512]{1,0:T(8,128)S(1)}, u32[]{:S(2)}, u32[]{:S(2)}) collective-permute-start(f32[128,512]{1,0:T(8,128)S(1)} %get-tuple-element.33), channel_id=1, source_target_pairs={{2,0},{4,2},{6,4},{8,6},{10,8},{12,10},{14,12},{16,14},{18,16},{20... | collective-permute-start | bytes 786440 | tf_op jit(solution)/shard_map/ppermute | solution.py:101
  35.2 1.0 copy-start.2
  36.2 8.6 %collective-permute-start.5 = (f32[128,512]{1,0:T(8,128)S(1)}, f32[128,512]{1,0:T(8,128)S(1)}, u32[]{:S(2)}, u32[]{:S(2)}) collective-permute-start(f32[128,512]{1,0:T(8,128)S(1)} %get-tuple-element.36), channel_id=1, source_target_pairs={{30,0},{0,2},{2,4},{4,6},{6,8},{8,10},{10,12},{12,14},{14,16},{16,... | collective-permute-start | bytes 786440 | tf_op jit(solution)/shard_map/ppermute | solution.py:101
  36.2 8.6 %collective-permute-start.6 = (f32[128,512]{1,0:T(8,128)S(1)}, f32[128,512]{1,0:T(8,128)S(1)}, u32[]{:S(2)}, u32[]{:S(2)}) collective-permute-start(f32[128,512]{1,0:T(8,128)S(1)} %get-tuple-element.37), channel_id=1, source_target_pairs={{2,0},{4,2},{6,4},{8,6},{10,8},{12,10},{14,12},{16,14},{18,16},{20... | collective-permute-start | bytes 786440 | tf_op jit(solution)/shard_map/ppermute | solution.py:101
  47.1 8.5 %collective-permute-start.7 = (f32[128,512]{1,0:T(8,128)S(1)}, f32[128,512]{1,0:T(8,128)S(1)}, u32[]{:S(2)}, u32[]{:S(2)}) collective-permute-start(f32[128,512]{1,0:T(8,128)S(1)} %get-tuple-element.40), channel_id=1, source_target_pairs={{30,0},{0,2},{2,4},{4,6},{6,8},{8,10},{10,12},{12,14},{14,16},{16,... | collective-permute-start | bytes 786440 | tf_op jit(solution)/shard_map/ppermute | solution.py:101
  47.2 8.5 %collective-permute-start.8 = (f32[128,512]{1,0:T(8,128)S(1)}, f32[128,512]{1,0:T(8,128)S(1)}, u32[]{:S(2)}, u32[]{:S(2)}) collective-permute-start(f32[128,512]{1,0:T(8,128)S(1)} %get-tuple-element.41), channel_id=1, source_target_pairs={{2,0},{4,2},{6,4},{8,6},{10,8},{12,10},{14,12},{16,14},{18,16},{20... | collective-permute-start | bytes 786440 | tf_op jit(solution)/shard_map/ppermute | solution.py:101
  56.7 8.6 %collective-permute-start.9 = (f32[128,512]{1,0:T(8,128)S(1)}, f32[128,512]{1,0:T(8,128)S(1)}, u32[]{:S(2)}, u32[]{:S(2)}) collective-permute-start(f32[128,512]{1,0:T(8,128)S(1)} %get-tuple-element.44), channel_id=1, source_target_pairs={{30,0},{0,2},{2,4},{4,6},{6,8},{8,10},{10,12},{12,14},{14,16},{16,... | collective-permute-start | bytes 786440 | tf_op jit(solution)/shard_map/ppermute | solution.py:101
  66.3 11.5 %all-to-all-start = ((f32[2,192,512]{2,1,0:T(8,128)}), f32[2,192,512]{2,1,0:T(8,128)S(1)}, u32[]{:S(2)}, u32[]{:S(2)}) async-start(f32[2,192,512]{2,1,0:T(8,128)} %bitcast), calls=%async_computation | async-start | bytes 1572864 | tf_op jit(solution)/shard_map/all_to_all | solution.py:237
  81.1 3.2 %collective-permute-start.10 = (f32[2304,128]{1,0:T(8,128)}, f32[2304,128]{1,0:T(8,128)}, u32[]{:S(2)}, u32[]{:S(2)}) collective-permute-start(f32[2304,128]{1,0:T(8,128)} %slice_select_fusion), channel_id=1, source_target_pairs={{0,2},{2,0},{4,6},{6,4},{8,10},{10,8},{12,14},{14,12},{16,18},{18,... | collective-permute-start | bytes 3538952 | tf_op jit(solution)/shard_map/ppermute | solution.py:141
  85.8 1.0 copy-start.6
  86.9 15.4 %collective-permute-start.11 = (f32[1152,128]{1,0:T(8,128)S(1)}, f32[1152,128]{1,0:T(8,128)S(1)}, u32[]{:S(2)}, u32[]{:S(2)}) collective-permute-start(f32[1152,128]{1,0:T(8,128)S(1)} %slice_select_fusion.1), channel_id=1, source_target_pairs={{0,1},{1,0},{2,3},{3,2},{4,5},{5,4},{6,7},{7,6},{8,9},{9,8},{10,11... | collective-permute-start | bytes 1769480 | tf_op jit(solution)/shard_map/ppermute | solution.py:141
  103.7 8.3 %collective-permute-start.12 = (f32[576,128]{1,0:T(8,128)S(1)}, f32[576,128]{1,0:T(8,128)S(1)}, u32[]{:S(2)}, u32[]{:S(2)}) collective-permute-start(f32[576,128]{1,0:T(8,128)S(1)} %slice_select_fusion.2), channel_id=1, source_target_pairs={{0,4},{2,6},{4,0},{6,2},{8,12},{10,14},{12,8},{14,10},{16,20},{18,... | collective-permute-start | bytes 884744 | tf_op jit(solution)/shard_map/ppermute | solution.py:141
  112.0 5.2 %collective-permute-start.13 = (f32[288,128]{1,0:T(8,128)S(1)}, f32[288,128]{1,0:T(8,128)S(1)}, u32[]{:S(2)}, u32[]{:S(2)}) collective-permute-start(f32[288,128]{1,0:T(8,128)S(1)} %slice_select_fusion.3), channel_id=1, source_target_pairs={{0,8},{2,10},{4,12},{6,14},{8,0},{10,2},{12,4},{14,6},{16,24},{18,... | collective-permute-start | bytes 442376 | tf_op jit(solution)/shard_map/ppermute | solution.py:141
  117.3 7.0 %collective-permute-start.14 = (f32[144,128]{1,0:T(8,128)S(1)}, f32[144,128]{1,0:T(8,128)S(1)}, u32[]{:S(2)}, u32[]{:S(2)}) collective-permute-start(f32[144,128]{1,0:T(8,128)S(1)} %slice_select_fusion.4), channel_id=1, source_target_pairs={{0,16},{2,18},{4,20},{6,22},{8,24},{10,26},{12,28},{14,30},{16,0},... | collective-permute-start | bytes 221192 | tf_op jit(solution)/shard_map/ppermute | solution.py:141
  124.3 5.3 %collective-permute-start.15 = (f32[144,128]{1,0:T(8,128)S(1)}, f32[144,128]{1,0:T(8,128)S(1)}, u32[]{:S(2)}, u32[]{:S(2)}) collective-permute-start(f32[144,128]{1,0:T(8,128)S(1)} %select_add_fusion.4), channel_id=1, source_target_pairs={{0,16},{2,18},{4,20},{6,22},{8,24},{10,26},{12,28},{14,30},{16,0},... | collective-permute-start | bytes 221192 | tf_op jit(solution)/shard_map/ppermute | solution.py:141
  129.7 5.2 %collective-permute-start.16 = (f32[288,128]{1,0:T(8,128)S(1)}, f32[288,128]{1,0:T(8,128)S(1)}, u32[]{:S(2)}, u32[]{:S(2)}) collective-permute-start(f32[288,128]{1,0:T(8,128)S(1)} %pad_maximum_fusion.5), channel_id=1, source_target_pairs={{0,8},{2,10},{4,12},{6,14},{8,0},{10,2},{12,4},{14,6},{16,24},{18,... | collective-permute-start | bytes 442376 | tf_op jit(solution)/shard_map/ppermute | solution.py:141
  134.9 6.8 %collective-permute-start.17 = (f32[576,128]{1,0:T(8,128)S(1)}, f32[576,128]{1,0:T(8,128)S(1)}, u32[]{:S(2)}, u32[]{:S(2)}) collective-permute-start(f32[576,128]{1,0:T(8,128)S(1)} %pad_maximum_fusion.4), channel_id=1, source_target_pairs={{0,4},{2,6},{4,0},{6,2},{8,12},{10,14},{12,8},{14,10},{16,20},{18,... | collective-permute-start | bytes 884744 | tf_op jit(solution)/shard_map/ppermute | solution.py:141
  141.8 9.9 %collective-permute-start.18 = (f32[1152,128]{1,0:T(8,128)S(1)}, f32[1152,128]{1,0:T(8,128)S(1)}, u32[]{:S(2)}, u32[]{:S(2)}) collective-permute-start(f32[1152,128]{1,0:T(8,128)S(1)} %pad_maximum_fusion.3), channel_id=1, source_target_pairs={{0,1},{1,0},{2,3},{3,2},{4,5},{5,4},{6,7},{7,6},{8,9},{9,8},{10,11... | collective-permute-start | bytes 1769480 | tf_op jit(solution)/shard_map/ppermute | solution.py:141
  151.9 2.9 %collective-permute-start.19 = (f32[2304,128]{1,0:T(8,128)S(1)}, f32[2304,128]{1,0:T(8,128)S(1)}, u32[]{:S(2)}, u32[]{:S(2)}) collective-permute-start(f32[2304,128]{1,0:T(8,128)S(1)} %pad_maximum_fusion.1), channel_id=1, source_target_pairs={{0,2},{2,0},{4,6},{6,4},{8,10},{10,8},{12,14},{14,12},{16,18},{18,... | collective-permute-start | bytes 3538952 | tf_op jit(solution)/shard_map/ppermute | solution.py:141

commit v2 on v1

--- a/solution.py
+++ b/solution.py
@@ -118,7 +118,7 @@
         if last:
             part, down = got
             top = shifted(down, "dom", 1)
-            return jnp.concatenate([part[:halo] + top, part[halo:]], axis=0)
+            return part, top
         now, part, up, down = got
         top = shifted(down, "dom", 1)
         bottom = shifted(up, "dom", -1)
@@ -136,29 +136,88 @@
         at += below
 
 
-def exchanged(block, axis, bit):
-    route = [(i, i ^ bit) for i in range(lax.axis_size(axis))]
+def half_gram(mine, other, second, out_ref, base_ref):
+    own, own_lo = split(mine.T)
+    other, other_lo = split(other.T)
+    cols = own.shape[0]
+    half = cols // 2
+
+    def put(at, value):
+        span = slice(at, at + value.shape[0])
+        out_ref[span, :] = value if base_ref is None else base_ref[span, :] + value
+
+    at = 0
+    for p in range(0, cols, LANES):
+        put(at, product((own[p:], own_lo[p:]), (own[p : p + LANES], own_lo[p : p + LANES]), NT))
+        at += cols - p
+
+    def cross(left, right):
+        for i, p in enumerate(range(0, cols, LANES)):
+            cut = slice(p, p + LANES)
+            put(at + i * half, product(left, (right[0][cut], right[1][cut]), NT))
+
+    @pl.when(second == 0)
+    def _():
+        cross((other[:half], other_lo[:half]), (own, own_lo))
+
+    @pl.when(second == 1)
+    def _():
+        cross((own[half:], own_lo[half:]), (other, other_lo))
+
+
+def low_gram_kernel(halo, second_ref, mine_ref, other_ref, out_ref):
+    half_gram(mine_ref[halo:, :], other_ref[...], second_ref[0], out_ref, None)
+
+
+def high_gram_kernel(second_ref, part_ref, top_ref, other_ref, base_ref, out_ref):
+    halo = top_ref.shape[0]
+    half_gram(part_ref[:halo, :] + top_ref[...], other_ref[...], second_ref[0], out_ref, base_ref)
+
+
+def exchanged(block, axis, mask):
+    route = [(i, i ^ mask) for i in range(lax.axis_size(axis))]
     return lax.ppermute(block, axis, route)
-
-
-def summed(block, stages):
-    for axis, bit in stages:
-        half = block.shape[0] // 2
-        upper = (lax.axis_index(axis) & bit) != 0
-        pair = block.reshape(2, half, block.shape[1])
-        keep = jnp.where(upper, pair[1], pair[0])
-        send = jnp.where(upper, pair[0], pair[1])
-        block = keep + exchanged(send, axis, bit)
-    for axis, bit in reversed(stages):
-        upper = (lax.axis_index(axis) & bit) != 0
-        other = exchanged(block, axis, bit)
-        block = jnp.concatenate([jnp.where(upper, other, block), jnp.where(upper, block, other)], axis=0)
-    return block
 
 
 def bits(axis):
     count = lax.axis_size(axis)
-    return [(axis, 1 << i) for i in range(count.bit_length() - 1)]
+    return [(axis, 1 << i, 2) for i in range(count.bit_length() - 1)]
+
+
+def rank(axis, unit, count):
+    return (lax.axis_index(axis) // unit) % count
+
+
+def scattered(block, stages):
+    for axis, unit, count in stages:
+        mine = rank(axis, unit, count)
+        pieces = block.reshape(count, -1, block.shape[-1])
+        total = lax.dynamic_index_in_dim(pieces, mine, keepdims=False)
+        for d in range(1, count):
+            piece = lax.dynamic_index_in_dim(pieces, mine ^ d, keepdims=False)
+            total = total + exchanged(piece, axis, d * unit)
+        block = total
+    return block
+
+
+def gathered(block, stage):
+    axis, unit, count = stage
+    mine = rank(axis, unit, count)
+    pieces = jnp.stack([block] + [exchanged(block, axis, d * unit) for d in range(1, count)])
+    bit = 1
+    while bit < count:
+        pair = pieces.reshape((count // (2 * bit), 2, bit) + block.shape)
+        pieces = jnp.where((mine & bit) != 0, pair[:, ::-1], pair).reshape(pieces.shape)
+        bit *= 2
+    return pieces
+
+
+def summed(block, stages):
+    width = block.shape[-1]
+    block = scattered(block, stages)
+    for stage in reversed(stages):
+        block = gathered(block, stage).reshape(-1, width)
+    return block
 
 
 def inverse_factor(block, out_ref):
@@ -195,17 +254,33 @@
             rows[t] = kept
 
 
-def factor_kernel(scale, gram_ref, rows_ref, out_ref, work_ref, hi_ref, lo_ref, inverse_ref):
+def packed_block(gram_ref, row, col, panels):
+    at = sum(panels - p for p in range(col)) + row - col
+    return gram_ref[at * LANES : (at + 1) * LANES, :]
+
+
+def halved_block(gram_ref, row, col, panels):
+    mid = panels // 2
+    triangle = mid * (mid + 1) // 2
+    if (row < mid) == (col < mid):
+        second, row, col = int(row >= mid), row % mid, col % mid
+        at = sum(mid - p for p in range(col)) + row - col
+    else:
+        second, at = divmod(row - mid, mid // 2)
+        at += triangle + col * (mid // 2)
+    chunk = gram_ref.shape[2] // LANES
+    part, at = divmod(at, chunk)
+    return gram_ref[part, second, at * LANES : (at + 1) * LANES, :]
+
+
+def factor_kernel(scale, block_of, gram_ref, rows_ref, out_ref, work_ref, hi_ref, lo_ref, inverse_ref):
     panels, total = work_ref.shape[:2]
     size = panels * LANES
-    at = 0
     for p in range(panels):
-        below = size - p * LANES
-        work_ref[p, size - below : size, :] = gram_ref[at : at + below, :] * scale
+        for r in range(panels):
+            block = block_of(gram_ref, r, p, panels) * scale if r >= p else jnp.zeros((LANES, LANES), F32)
+            work_ref[p, r * LANES : (r + 1) * LANES, :] = block
         work_ref[p, size:, :] = rows_ref[:, p * LANES : (p + 1) * LANES]
-        if p > 0:
-            work_ref[p, : size - below, :] = jnp.zeros((size - below, LANES), F32)
-        at += below
 
     def panel(p, carry):
         offset = pl.multiple_of(p * LANES, LANES)
@@ -228,27 +303,81 @@
         out_ref[:, p * LANES : (p + 1) * LANES] = work_ref[p, size:, :]
 
 
+def any_orb_gram(part, top):
+    halo = top.shape[0]
+    current = jnp.concatenate([part[:halo] + top, part[halo:]], axis=0)
+    rows = lax.all_to_all(current, "orb", split_axis=0, concat_axis=1, tiled=True)
+    panels = rows.shape[1] // LANES
+    packed = LANES * panels * (panels + 1) // 2
+    gram = kernel_call(gram_kernel, f32(packed, LANES))(rows)
+    dom = bits("dom")
+    return rows, summed(gram, dom[:1] + bits("orb") + dom[1:]), packed_block
+
+
+def two_orb_gram(part, top):
+    own, cols = part.shape
+    halo = top.shape[0]
+    second = lax.axis_index("orb")
+    panels = cols // LANES
+    packed = LANES * (panels * (panels + 1) // 2 + panels * (panels // 2))
+    flag = second.reshape(1)
+    low = exchanged(part[halo:], "orb", 1)
+    gram = low_gram(flag, part, low, halo, packed)
+    high = exchanged(part[:halo] + top, "orb", 1)
+    gram = high_gram(flag, part, top, high, gram)
+    dom = bits("dom")
+    stages = dom if len(dom) < 4 else dom[:-2] + [("dom", dom[-2][1], 4)]
+    gram = scattered(gram, stages)
+    for stage in reversed(stages[1:]):
+        gram = gathered(gram, stage).reshape(-1, LANES)
+    gram = gathered(gathered(gram, ("orb", 1, 2)), stages[0])
+    mine = jnp.concatenate([part[:halo] + top, part[halo:]], axis=0).reshape(2, own // 2, cols)
+    other = jnp.concatenate([high, low], axis=0).reshape(2, own // 2, cols)
+    mine = jnp.where(second == 0, mine[0], mine[1])
+    other = jnp.where(second == 0, other[0], other[1])
+    rows = jnp.where(
+        second == 0, jnp.concatenate([mine, other], axis=1), jnp.concatenate([other, mine], axis=1)
+    )
+    return rows, gram, halved_block
+
+
+def with_flag(body, out_shape, count):
+    specs = [pl.BlockSpec(memory_space=pltpu.SMEM)] + [pl.BlockSpec(memory_space=pltpu.VMEM)] * count
+    return pl.pallas_call(
+        body,
+        out_shape=out_shape,
+        in_specs=specs,
+        compiler_params=pltpu.CompilerParams(vmem_limit_bytes=VMEM_BYTES),
+    )
+
+
+def low_gram(flag, part, low, halo, packed):
+    kernel = lambda *refs: low_gram_kernel(halo, *refs)
+    return with_flag(kernel, f32(packed, LANES), 2)(flag, part, low)
+
+
+def high_gram(flag, part, top, high, gram):
+    return with_flag(high_gram_kernel, f32(*gram.shape), 4)(flag, part, top, high, gram)
+
+
 def body(orbitals, cell_mats, cell_map):
     own, cols = orbitals.shape
     size = cell_mats.shape[1]
     node_total = own * lax.axis_size("dom")
     matrix = kernel_call(order_kernel, [bf16(size, size)] * 2)(cell_map, cell_mats)
-    current = filtered_columns(orbitals, matrix)
-    regrouped = lax.all_to_all(current, "orb", split_axis=0, concat_axis=1, tiled=True)
-    count, width = regrouped.shape
+    part, top = filtered_columns(orbitals, matrix)
+    two = lax.axis_size("orb") == 2 and cols % (2 * LANES) == 0 and lax.axis_size("dom") > 1
+    rows, gram, block_of = (two_orb_gram if two else any_orb_gram)(part, top)
+    count, width = rows.shape
     panels = width // LANES
-    packed = LANES * panels * (panels + 1) // 2
-    gram = kernel_call(gram_kernel, f32(packed, LANES))(regrouped)
-    dom = bits("dom")
-    gram = summed(gram, dom[:1] + bits("orb") + dom[1:])
     scratch = [
         pltpu.VMEM((panels, width + count, LANES), F32),
         pltpu.VMEM((panels, width + count, LANES), BF16),
         pltpu.VMEM((panels, width + count, LANES), BF16),
         pltpu.VMEM((LANES, LANES), F32),
     ]
-    factor = lambda *refs: factor_kernel(1.0 / node_total, *refs)
-    return kernel_call(factor, f32(count, width), scratch)(gram, regrouped)
+    factor = lambda *refs: factor_kernel(1.0 / node_total, block_of, *refs)
+    return kernel_call(factor, f32(count, width), scratch)(gram, rows)
 
 
 def solution(mesh):

time: 209 us -> 191 us (0.914)
  waiting for transfers between devices: 101 us -> 67 us
  starting transfers between devices: 28.4 us -> 43.2 us
    ppermute x10 -> x13, waiting for transfers between devices: 68.1 us -> 43 us  [exchanged(): return lax.ppermute(block, axis, route)]
    ppermute x10 -> x13, starting transfers between devices: 1.17 us -> 19.7 us  [exchanged(): return lax.ppermute(block, axis, route)]
    all_to_all x1 -> x0, waiting for transfers between devices: 7.78 us -> none  [body(): lax.all_to_all(current, 'orb', split_axis=0, concat_axis=1, tiled=True)]
    all_to_all x1 -> x0, starting transfers between devices: 3.72 us -> none  [body(): lax.all_to_all(current, 'orb', split_axis=0, concat_axis=1, tiled=True)]
    another operation x0 -> x6, other arithmetic: none -> 2.85 us  [the longest x5 2.82 us: gathered(): jnp.stack([block] + [exchanged(block, axis, d * unit) for d in range(1, c...]
    pallas_call x2 -> x3, Pallas kernels: 55.4 us -> 55.7 us  [the longest x1 53.3 us: body(): return kernel_call(factor, f32(count, width), scratch)(gram, rows)]
    unnamed x14 -> x22, local copies, waits for them, and re-layouts: 5.87 us -> 5.88 us
  transfers between devices with their start and end apart: 21 -> 23, of which waited for: 17 -> 17; matrix products, arithmetic and copies ran while one was open for 0% -> 0% of each run, Pallas kernels for 1% -> 1%
where the time goes in v2:
time: 191 us
  waiting for transfers between devices  67 us (35%)
  Pallas kernels  65.9 us (35%)
  starting transfers between devices  43.2 us (23%)
  local copies, waits for them, and re-layouts  7.86 us (4%)
  other arithmetic  6.56 us (3%)
    pallas_call x1, Pallas kernels, body(): return kernel_call(factor, f32(count, width), scratch)(gram, rows)  53.3 us
    ppermute x13, waiting for transfers between devices, exchanged(): return lax.ppermute(block, axis, route)  43 us
    ppermute x10, waiting for transfers between devices, shifted(): return lax.ppermute(block, axis, route)  24 us
    ppermute x10, starting transfers between devices, shifted(): return lax.ppermute(block, axis, route)  23.6 us
    ppermute x13, starting transfers between devices, exchanged(): return lax.ppermute(block, axis, route)  19.7 us
    pallas_call x5, Pallas kernels, filtered_columns(): got = kernel_call(body, outs)(*matrix, *state)  8.93 us
    unnamed x22, local copies, waits for them, and re-layouts  5.88 us
  transfers between devices with their start and end apart: 23, of which 17 were waited for; matrix products, arithmetic and copies ran while one was open for 0% of the time, Pallas kernels for 1%

profile of v2, /device:TPU:0, one launch (start us, length us, event | category | flops | bytes accessed | tf_op | source)
XLA Modules:
  0.0 190.8 jit_solution(11143866991816188050)
XLA Ops:
  0.0 1.0 slice.30
  1.0 5.5 %collective-permute-start = (f32[128,512]{1,0:T(8,128)S(1)}, f32[128,512]{1,0:T(8,128)S(1)}, u32[]{:S(2)}, u32[]{:S(2)}) collective-permute-start(f32[128,512]{1,0:T(8,128)S(1)} %slice.30), channel_id=1, source_target_pairs={{2,0},{4,2},{6,4},{8,6},{10,8},{12,10},{14,12},{16,14},{18,16},{20... | collective-permute-start | bytes 786440 | tf_op jit(solution)/shard_map/ppermute | solution.py:101
  6.6 1.2 copy-done.4
  7.8 0.7 copy-done.5
  8.5 1.3 shard_map.37
  9.7 0.7 collective-permute-done.refs_3_
  10.5 1.0 shard_map.38
  11.5 1.0 copy-done.3
  12.5 0.0 collective-permute-start.1
  12.5 4.6 %collective-permute-start.2 = (f32[128,512]{1,0:T(8,128)S(1)}, f32[128,512]{1,0:T(8,128)S(1)}, u32[]{:S(2)}, u32[]{:S(2)}) collective-permute-start(f32[128,512]{1,0:T(8,128)S(1)} %get-tuple-element.29), channel_id=1, source_target_pairs={{2,0},{4,2},{6,4},{8,6},{10,8},{12,10},{14,12},{16,14},{18,16},{20... | collective-permute-start | bytes 786440 | tf_op jit(solution)/shard_map/ppermute | solution.py:101
  17.1 4.1 %collective-permute-done.1.refs_3_ = f32[128,512]{1,0:T(8,128)S(1)} collective-permute-done((f32[128,512]{1,0:T(8,128)S(1)}, f32[128,512]{1,0:T(8,128)S(1)}, u32[]{:S(2)}, u32[]{:S(2)}) %collective-permute-start.1) | collective-permute-done | bytes 262176 | tf_op jit(solution)/shard_map/ppermute | solution.py:101
  21.1 2.3 %shard_map.39 = (f32[512,512]{1,0:T(8,128)S(1)}, f32[512,512]{1,0:T(8,128)S(1)}, f32[128,512]{1,0:T(8,128)S(1)}, f32[128,512]{1,0:T(8,128)S(1)}) custom-call(bf16[512,512]{1,0:T(8,128)(2,1)S(1)} %get-tuple-element.25.refs_0_, bf16[512,512]{1,0:T(8,128)(2,1)S(1)} %get-tuple-element.26.refs_1_, f32[512,512]{1,0:T(8,128)S(1)} %get-tuple-element.27.refs_2_, ...), custom_call_target="tpu_custom_call" | custom-call | tf_op jit(solution)/shard_map/pallas_call | solution.py:117
  23.4 1.0 copy-done.1
  24.4 4.4 %collective-permute-start.4 = (f32[128,512]{1,0:T(8,128)S(1)}, f32[128,512]{1,0:T(8,128)S(1)}, u32[]{:S(2)}, u32[]{:S(2)}) collective-permute-start(f32[128,512]{1,0:T(8,128)S(1)} %get-tuple-element.33), channel_id=1, source_target_pairs={{2,0},{4,2},{6,4},{8,6},{10,8},{12,10},{14,12},{16,14},{18,16},{20... | collective-permute-start | bytes 786440 | tf_op jit(solution)/shard_map/ppermute | solution.py:101
  28.9 4.1 %collective-permute-done.3.refs_3_ = f32[128,512]{1,0:T(8,128)S(1)} collective-permute-done((f32[128,512]{1,0:T(8,128)S(1)}, f32[128,512]{1,0:T(8,128)S(1)}, u32[]{:S(2)}, u32[]{:S(2)}) %collective-permute-start.3) | collective-permute-done | bytes 262176 | tf_op jit(solution)/shard_map/ppermute | solution.py:101
  32.9 2.3 %shard_map.40 = (f32[512,512]{1,0:T(8,128)S(1)}, f32[512,512]{1,0:T(8,128)S(1)}, f32[128,512]{1,0:T(8,128)S(1)}, f32[128,512]{1,0:T(8,128)S(1)}) custom-call(bf16[512,512]{1,0:T(8,128)(2,1)S(1)} %get-tuple-element.25.refs_0_, bf16[512,512]{1,0:T(8,128)(2,1)S(1)} %get-tuple-element.26.refs_1_, f32[512,512]{1,0:T(8,128)S(1)} %get-tuple-element.31.refs_2_, ...), custom_call_target="tpu_custom_call" | custom-call | tf_op jit(solution)/shard_map/pallas_call | solution.py:117
  35.2 1.0 copy-done.2
  36.2 4.4 %collective-permute-start.6 = (f32[128,512]{1,0:T(8,128)S(1)}, f32[128,512]{1,0:T(8,128)S(1)}, u32[]{:S(2)}, u32[]{:S(2)}) collective-permute-start(f32[128,512]{1,0:T(8,128)S(1)} %get-tuple-element.37), channel_id=1, source_target_pairs={{2,0},{4,2},{6,4},{8,6},{10,8},{12,10},{14,12},{16,14},{18,16},{20... | collective-permute-start | bytes 786440 | tf_op jit(solution)/shard_map/ppermute | solution.py:101
  40.6 4.1 %collective-permute-done.5.refs_3_ = f32[128,512]{1,0:T(8,128)S(1)} collective-permute-done((f32[128,512]{1,0:T(8,128)S(1)}, f32[128,512]{1,0:T(8,128)S(1)}, u32[]{:S(2)}, u32[]{:S(2)}) %collective-permute-start.5) | collective-permute-done | bytes 262176 | tf_op jit(solution)/shard_map/ppermute | solution.py:101
  44.8 2.3 %shard_map.41 = (f32[512,512]{1,0:T(8,128)S(1)}, f32[512,512]{1,0:T(8,128)S(1)}, f32[128,512]{1,0:T(8,128)S(1)}, f32[128,512]{1,0:T(8,128)S(1)}) custom-call(bf16[512,512]{1,0:T(8,128)(2,1)S(1)} %get-tuple-element.25.refs_0_, bf16[512,512]{1,0:T(8,128)(2,1)S(1)} %get-tuple-element.26.refs_1_, f32[512,512]{1,0:T(8,128)S(1)} %get-tuple-element.35.refs_2_, ...), custom_call_target="tpu_custom_call" | custom-call | tf_op jit(solution)/shard_map/pallas_call | solution.py:117
  47.1 0.1 collective-permute-start.7
  47.2 4.4 %collective-permute-start.8 = (f32[128,512]{1,0:T(8,128)S(1)}, f32[128,512]{1,0:T(8,128)S(1)}, u32[]{:S(2)}, u32[]{:S(2)}) collective-permute-start(f32[128,512]{1,0:T(8,128)S(1)} %get-tuple-element.41), channel_id=1, source_target_pairs={{2,0},{4,2},{6,4},{8,6},{10,8},{12,10},{14,12},{16,14},{18,16},{20... | collective-permute-start | bytes 786440 | tf_op jit(solution)/shard_map/ppermute | solution.py:101
  51.6 4.1 %collective-permute-done.7.refs_3_ = f32[128,512]{1,0:T(8,128)S(1)} collective-permute-done((f32[128,512]{1,0:T(8,128)S(1)}, f32[128,512]{1,0:T(8,128)S(1)}, u32[]{:S(2)}, u32[]{:S(2)}) %collective-permute-start.7) | collective-permute-done | bytes 262176 | tf_op jit(solution)/shard_map/ppermute | solution.py:101
  55.6 1.0 shard_map.42
  56.7 0.1 collective-permute-start.9
  56.8 1.6 collective-permute-start.11
  58.3 6.9 %collective-permute-done.9.top_ref = f32[128,512]{1,0:T(8,128)S(1)} collective-permute-done((f32[128,512]{1,0:T(8,128)S(1)}, f32[128,512]{1,0:T(8,128)S(1)}, u32[]{:S(2)}, u32[]{:S(2)}) %collective-permute-start.9) | collective-permute-done | bytes 262176 | tf_op jit(solution)/shard_map/ppermute | solution.py:101
  65.3 1.6 collective-permute-start.10
  66.9 1.9 %collective-permute-done.11.refs_2_ = f32[256,512]{1,0:T(8,128)S(1)} collective-permute-done((f32[256,512]{1,0:T(8,128)S(1)}, f32[256,512]{1,0:T(8,128)S(1)}, u32[]{:S(2)}, u32[]{:S(2)}) %collective-permute-start.11) | collective-permute-done | bytes 524320 | tf_op jit(solution)/shard_map/ppermute | solution.py:179
  68.8 1.3 shard_map.43.base_ref
  70.2 1.6 collective-permute-done.10.other_ref
  71.8 1.0 shard_map.44
  72.8 0.9 dynamic-slice_bitcast_fusion
  73.7 2.3 %collective-permute-done.12 = f32[1152,128]{1,0:T(8,128)} collective-permute-done((f32[1152,128]{1,0:T(8,128)}, f32[1152,128]{1,0:T(8,128)}, u32[]{:S(2)}, u32[]{:S(2)}) %collective-permute-start.12) | collective-permute-done | bytes 589856 | tf_op jit(solution)/shard_map/ppermute | solution.py:179
  76.0 1.1 bitcast_add_fusion
  77.1 0.0 copy-start.6
  77.2 0.8 copy-done.6
  78.0 0.1 collective-permute-start.13
  78.1 9.0 %collective-permute-done.13 = f32[576,128]{1,0:T(8,128)S(1)} collective-permute-done((f32[576,128]{1,0:T(8,128)S(1)}, f32[576,128]{1,0:T(8,128)S(1)}, u32[]{:S(2)}, u32[]{:S(2)}) %collective-permute-start.13) | collective-permute-done | bytes 294944 | tf_op jit(solution)/shard_map/ppermute | solution.py:179
  87.1 1.0 bitcast_add_fusion.1
  88.1 1.9 %collective-permute-start.14 = (f32[144,128]{1,0:T(8,128)S(1)}, f32[144,128]{1,0:T(8,128)S(1)}, u32[]{:S(2)}, u32[]{:S(2)}) collective-permute-start(f32[144,128]{1,0:T(8,128)S(1)} %get-tuple-element.45), channel_id=1, source_target_pairs={{0,8},{2,10},{4,12},{6,14},{8,0},{10,2},{12,4},{14,6},{16,24},{18,... | collective-permute-start | bytes 221192 | tf_op jit(solution)/shard_map/ppermute | solution.py:179
  90.0 7.0 %collective-permute-start.15 = (f32[144,128]{1,0:T(8,128)S(1)}, f32[144,128]{1,0:T(8,128)S(1)}, u32[]{:S(2)}, u32[]{:S(2)}) collective-permute-start(f32[144,128]{1,0:T(8,128)S(1)} %get-tuple-element.47), channel_id=1, source_target_pairs={{0,16},{2,18},{4,20},{6,22},{8,24},{10,26},{12,28},{14,30},{16,0},... | collective-permute-start | bytes 221192 | tf_op jit(solution)/shard_map/ppermute | solution.py:179
  97.0 4.9 %collective-permute-done.15 = f32[144,128]{1,0:T(8,128)S(1)} collective-permute-done((f32[144,128]{1,0:T(8,128)S(1)}, f32[144,128]{1,0:T(8,128)S(1)}, u32[]{:S(2)}, u32[]{:S(2)}) %collective-permute-start.15) | collective-permute-done | bytes 73760 | tf_op jit(solution)/shard_map/ppermute | solution.py:179
  101.9 1.4 collective-permute-done.16
  103.3 0.8 collective-permute-start.17
  104.1 1.7 collective-permute-start.18
  105.8 2.0 %collective-permute-start.19 = (f32[144,128]{1,0:T(8,128)S(1)}, f32[144,128]{1,0:T(8,128)S(1)}, u32[]{:S(2)}, u32[]{:S(2)}) collective-permute-start(f32[144,128]{1,0:T(8,128)S(1)} %fusion.3), channel_id=1, source_target_pairs={{0,24},{2,26},{4,28},{6,30},{8,16},{10,18},{12,20},{14,22},{16,8},... | collective-permute-start | bytes 221192 | tf_op jit(solution)/shard_map/ppermute | solution.py:179
  107.7 2.8 %collective-permute-done.18 = f32[144,128]{1,0:T(8,128)S(1)} collective-permute-done((f32[144,128]{1,0:T(8,128)S(1)}, f32[144,128]{1,0:T(8,128)S(1)}, u32[]{:S(2)}, u32[]{:S(2)}) %collective-permute-start.18) | collective-permute-done | bytes 73760 | tf_op jit(solution)/shard_map/ppermute | solution.py:179
  110.5 1.5 collective-permute-done.19
  112.1 1.5 collective-permute-start.20
  113.6 5.3 %collective-permute-done.20 = f32[576,128]{1,0:T(8,128)S(1)} collective-permute-done((f32[576,128]{1,0:T(8,128)S(1)}, f32[576,128]{1,0:T(8,128)S(1)}, u32[]{:S(2)}, u32[]{:S(2)}) %collective-permute-start.20) | collective-permute-done | bytes 294944 | tf_op jit(solution)/shard_map/ppermute | solution.py:179
  119.0 1.6 collective-permute-start.21
  120.6 9.7 %collective-permute-done.21 = f32[1152,128]{1,0:T(8,128)} collective-permute-done((f32[1152,128]{1,0:T(8,128)S(1)}, f32[1152,128]{1,0:T(8,128)}, u32[]{:S(2)}, u32[]{:S(2)}) %collective-permute-start.21) | collective-permute-done | bytes 589856 | tf_op jit(solution)/shard_map/ppermute | solution.py:179
  130.3 1.1 pad_maximum_fusion.1
  131.5 1.1 reverse_select_fusion.1
  132.6 0.2 copy-done.10
  132.9 0.1 fusion
  132.9 0.1 slice_select_fusion
  133.0 0.1 maximum_select_fusion.refs_1_
  133.1 0.1 fusion.4
  133.2 2.6 %collective-permute-done.22 = f32[2,1152,128]{2,1,0:T(8,128)} collective-permute-done((f32[2,1152,128]{2,1,0:T(8,128)}, f32[2,1152,128]{2,1,0:T(8,128)}, u32[]{:S(2)}, u32[]{:S(2)}) %collective-permute-start.22) | collective-permute-done | bytes 1179680 | tf_op jit(solution)/shard_map/ppermute | solution.py:179
  135.8 1.5 pad_maximum_fusion
  137.3 0.2 reverse_select_fusion.refs_0_
  137.5 53.3 %shard_map.45 = f32[192,1024]{1,0:T(8,128)} custom-call(f32[2,2,1152,128]{3,2,1,0:T(8,128)S(1)} %reverse_select_fusion.refs_0_, f32[192,1024]{1,0:T(8,128)S(1)} %maximum_select_fusion.refs_1_), custom_call_target="tpu_custom_call" | custom-call | tf_op jit(solution)/shard_map/pallas_call | solution.py:380
  (35 shorter events, 0.4 us)
Async XLA Ops:
  0.0 10.5 %copy-start = (f32[384,512]{1,0:T(8,128)S(1)}, f32[384,512]{1,0:T(8,128)}, u32[]{:S(2)}) copy-start(f32[384,512]{1,0:T(8,128)} %refs_2_.1) | copy-start | bytes 2359300
  1.0 9.4 %collective-permute-start = (f32[128,512]{1,0:T(8,128)S(1)}, f32[128,512]{1,0:T(8,128)S(1)}, u32[]{:S(2)}, u32[]{:S(2)}) collective-permute-start(f32[128,512]{1,0:T(8,128)S(1)} %slice.30), channel_id=1, source_target_pairs={{2,0},{4,2},{6,4},{8,6},{10,8},{12,10},{14,12},{16,14},{18,16},{20... | collective-permute-start | bytes 786440 | tf_op jit(solution)/shard_map/ppermute | solution.py:101
  6.6 1.2 copy-start.4
  7.8 0.7 copy-start.5
  11.5 1.0 copy-start.3
  12.5 8.7 %collective-permute-start.1 = (f32[128,512]{1,0:T(8,128)S(1)}, f32[128,512]{1,0:T(8,128)S(1)}, u32[]{:S(2)}, u32[]{:S(2)}) collective-permute-start(f32[128,512]{1,0:T(8,128)S(1)} %get-tuple-element.28), channel_id=1, source_target_pairs={{30,0},{0,2},{2,4},{4,6},{6,8},{8,10},{10,12},{12,14},{14,16},{16,... | collective-permute-start | bytes 786440 | tf_op jit(solution)/shard_map/ppermute | solution.py:101
  12.5 8.7 %collective-permute-start.2 = (f32[128,512]{1,0:T(8,128)S(1)}, f32[128,512]{1,0:T(8,128)S(1)}, u32[]{:S(2)}, u32[]{:S(2)}) collective-permute-start(f32[128,512]{1,0:T(8,128)S(1)} %get-tuple-element.29), channel_id=1, source_target_pairs={{2,0},{4,2},{6,4},{8,6},{10,8},{12,10},{14,12},{16,14},{18,16},{20... | collective-permute-start | bytes 786440 | tf_op jit(solution)/shard_map/ppermute | solution.py:101
  23.4 1.0 copy-start.1
  24.4 8.5 %collective-permute-start.3 = (f32[128,512]{1,0:T(8,128)S(1)}, f32[128,512]{1,0:T(8,128)S(1)}, u32[]{:S(2)}, u32[]{:S(2)}) collective-permute-start(f32[128,512]{1,0:T(8,128)S(1)} %get-tuple-element.32), channel_id=1, source_target_pairs={{30,0},{0,2},{2,4},{4,6},{6,8},{8,10},{10,12},{12,14},{14,16},{16,... | collective-permute-start | bytes 786440 | tf_op jit(solution)/shard_map/ppermute | solution.py:101
  24.4 8.5 %collective-permute-start.4 = (f32[128,512]{1,0:T(8,128)S(1)}, f32[128,512]{1,0:T(8,128)S(1)}, u32[]{:S(2)}, u32[]{:S(2)}) collective-permute-start(f32[128,512]{1,0:T(8,128)S(1)} %get-tuple-element.33), channel_id=1, source_target_pairs={{2,0},{4,2},{6,4},{8,6},{10,8},{12,10},{14,12},{16,14},{18,16},{20... | collective-permute-start | bytes 786440 | tf_op jit(solution)/shard_map/ppermute | solution.py:101
  35.2 1.0 copy-start.2
  36.2 8.6 %collective-permute-start.5 = (f32[128,512]{1,0:T(8,128)S(1)}, f32[128,512]{1,0:T(8,128)S(1)}, u32[]{:S(2)}, u32[]{:S(2)}) collective-permute-start(f32[128,512]{1,0:T(8,128)S(1)} %get-tuple-element.36), channel_id=1, source_target_pairs={{30,0},{0,2},{2,4},{4,6},{6,8},{8,10},{10,12},{12,14},{14,16},{16,... | collective-permute-start | bytes 786440 | tf_op jit(solution)/shard_map/ppermute | solution.py:101
  36.2 8.6 %collective-permute-start.6 = (f32[128,512]{1,0:T(8,128)S(1)}, f32[128,512]{1,0:T(8,128)S(1)}, u32[]{:S(2)}, u32[]{:S(2)}) collective-permute-start(f32[128,512]{1,0:T(8,128)S(1)} %get-tuple-element.37), channel_id=1, source_target_pairs={{2,0},{4,2},{6,4},{8,6},{10,8},{12,10},{14,12},{16,14},{18,16},{20... | collective-permute-start | bytes 786440 | tf_op jit(solution)/shard_map/ppermute | solution.py:101
  47.1 8.5 %collective-permute-start.7 = (f32[128,512]{1,0:T(8,128)S(1)}, f32[128,512]{1,0:T(8,128)S(1)}, u32[]{:S(2)}, u32[]{:S(2)}) collective-permute-start(f32[128,512]{1,0:T(8,128)S(1)} %get-tuple-element.40), channel_id=1, source_target_pairs={{30,0},{0,2},{2,4},{4,6},{6,8},{8,10},{10,12},{12,14},{14,16},{16,... | collective-permute-start | bytes 786440 | tf_op jit(solution)/shard_map/ppermute | solution.py:101
  47.2 8.5 %collective-permute-start.8 = (f32[128,512]{1,0:T(8,128)S(1)}, f32[128,512]{1,0:T(8,128)S(1)}, u32[]{:S(2)}, u32[]{:S(2)}) collective-permute-start(f32[128,512]{1,0:T(8,128)S(1)} %get-tuple-element.41), channel_id=1, source_target_pairs={{2,0},{4,2},{6,4},{8,6},{10,8},{12,10},{14,12},{16,14},{18,16},{20... | collective-permute-start | bytes 786440 | tf_op jit(solution)/shard_map/ppermute | solution.py:101
  56.7 8.6 %collective-permute-start.9 = (f32[128,512]{1,0:T(8,128)S(1)}, f32[128,512]{1,0:T(8,128)S(1)}, u32[]{:S(2)}, u32[]{:S(2)}) collective-permute-start(f32[128,512]{1,0:T(8,128)S(1)} %get-tuple-element.44), channel_id=1, source_target_pairs={{30,0},{0,2},{2,4},{4,6},{6,8},{8,10},{10,12},{12,14},{14,16},{16,... | collective-permute-start | bytes 786440 | tf_op jit(solution)/shard_map/ppermute | solution.py:101
  56.8 13.4 %copy-start.7 = (f32[256,512]{1,0:T(8,128)}, f32[256,512]{1,0:T(8,128)S(1)}, u32[]{:S(2)}) copy-start(f32[256,512]{1,0:T(8,128)S(1)} %slice.32) | copy-start | bytes 1572868
  56.8 12.1 %collective-permute-start.11 = (f32[256,512]{1,0:T(8,128)S(1)}, f32[256,512]{1,0:T(8,128)S(1)}, u32[]{:S(2)}, u32[]{:S(2)}) collective-permute-start(f32[256,512]{1,0:T(8,128)S(1)} %slice.32), channel_id=1, source_target_pairs={{0,1},{1,0},{2,3},{3,2},{4,5},{5,4},{6,7},{7,6},{8,9},{9,8},{10,11... | collective-permute-start | bytes 1572872 | tf_op jit(solution)/shard_map/ppermute | solution.py:179
  65.3 4.9 %copy-start.9 = (f32[128,512]{1,0:T(8,128)}, f32[128,512]{1,0:T(8,128)S(1)}, u32[]{:S(2)}) copy-start(f32[128,512]{1,0:T(8,128)S(1)} %slice_add_fusion) | copy-start | bytes 786436
  65.3 6.4 %collective-permute-start.10 = (f32[128,512]{1,0:T(8,128)S(1)}, f32[128,512]{1,0:T(8,128)S(1)}, u32[]{:S(2)}, u32[]{:S(2)}) collective-permute-start(f32[128,512]{1,0:T(8,128)S(1)} %slice_add_fusion), channel_id=1, source_target_pairs={{0,1},{1,0},{2,3},{3,2},{4,5},{5,4},{6,7},{7,6},{8,9},{9,8},{10,11... | collective-permute-start | bytes 786440 | tf_op jit(solution)/shard_map/ppermute | solution.py:179
  73.7 2.3 %collective-permute-start.12 = (f32[1152,128]{1,0:T(8,128)}, f32[1152,128]{1,0:T(8,128)}, u32[]{:S(2)}, u32[]{:S(2)}) collective-permute-start(f32[1152,128]{1,0:T(8,128)} %dynamic-slice_bitcast_fusion), channel_id=1, source_target_pairs={{0,2},{2,0},{4,6},{6,4},{8,10},{10,8},{12,14},{14,12},{16,18},{18,... | collective-permute-start | bytes 1769480 | tf_op jit(solution)/shard_map/ppermute | solution.py:179
  77.1 0.8 copy-start.6
  78.0 9.1 %collective-permute-start.13 = (f32[576,128]{1,0:T(8,128)S(1)}, f32[576,128]{1,0:T(8,128)S(1)}, u32[]{:S(2)}, u32[]{:S(2)}) collective-permute-start(f32[576,128]{1,0:T(8,128)S(1)} %dynamic-slice_bitcast_fusion.1), channel_id=1, source_target_pairs={{0,4},{2,6},{4,0},{6,2},{8,12},{10,14},{12,8},{14,10},{16,20},{18,... | collective-permute-start | bytes 884744 | tf_op jit(solution)/shard_map/ppermute | solution.py:179
  88.1 8.9 %collective-permute-start.14 = (f32[144,128]{1,0:T(8,128)S(1)}, f32[144,128]{1,0:T(8,128)S(1)}, u32[]{:S(2)}, u32[]{:S(2)}) collective-permute-start(f32[144,128]{1,0:T(8,128)S(1)} %get-tuple-element.45), channel_id=1, source_target_pairs={{0,8},{2,10},{4,12},{6,14},{8,0},{10,2},{12,4},{14,6},{16,24},{18,... | collective-permute-start | bytes 221192 | tf_op jit(solution)/shard_map/ppermute | solution.py:179
  90.0 11.8 %collective-permute-start.15 = (f32[144,128]{1,0:T(8,128)S(1)}, f32[144,128]{1,0:T(8,128)S(1)}, u32[]{:S(2)}, u32[]{:S(2)}) collective-permute-start(f32[144,128]{1,0:T(8,128)S(1)} %get-tuple-element.47), channel_id=1, source_target_pairs={{0,16},{2,18},{4,20},{6,22},{8,24},{10,26},{12,28},{14,30},{16,0},... | collective-permute-start | bytes 221192 | tf_op jit(solution)/shard_map/ppermute | solution.py:179
  97.0 6.3 %collective-permute-start.16 = (f32[144,128]{1,0:T(8,128)S(1)}, f32[144,128]{1,0:T(8,128)S(1)}, u32[]{:S(2)}, u32[]{:S(2)}) collective-permute-start(f32[144,128]{1,0:T(8,128)S(1)} %get-tuple-element.46), channel_id=1, source_target_pairs={{0,24},{2,26},{4,28},{6,30},{8,16},{10,18},{12,20},{14,22},{16,8},... | collective-permute-start | bytes 221192 | tf_op jit(solution)/shard_map/ppermute | solution.py:179
  103.3 4.5 %collective-permute-start.17 = (f32[144,128]{1,0:T(8,128)S(1)}, f32[144,128]{1,0:T(8,128)S(1)}, u32[]{:S(2)}, u32[]{:S(2)}) collective-permute-start(f32[144,128]{1,0:T(8,128)S(1)} %fusion.3), channel_id=1, source_target_pairs={{0,8},{2,10},{4,12},{6,14},{8,0},{10,2},{12,4},{14,6},{16,24},{18,... | collective-permute-start | bytes 221192 | tf_op jit(solution)/shard_map/ppermute | solution.py:179
  104.1 6.4 %collective-permute-start.18 = (f32[144,128]{1,0:T(8,128)S(1)}, f32[144,128]{1,0:T(8,128)S(1)}, u32[]{:S(2)}, u32[]{:S(2)}) collective-permute-start(f32[144,128]{1,0:T(8,128)S(1)} %fusion.3), channel_id=1, source_target_pairs={{0,16},{2,18},{4,20},{6,22},{8,24},{10,26},{12,28},{14,30},{16,0},... | collective-permute-start | bytes 221192 | tf_op jit(solution)/shard_map/ppermute | solution.py:179
  105.8 6.3 %collective-permute-start.19 = (f32[144,128]{1,0:T(8,128)S(1)}, f32[144,128]{1,0:T(8,128)S(1)}, u32[]{:S(2)}, u32[]{:S(2)}) collective-permute-start(f32[144,128]{1,0:T(8,128)S(1)} %fusion.3), channel_id=1, source_target_pairs={{0,24},{2,26},{4,28},{6,30},{8,16},{10,18},{12,20},{14,22},{16,8},... | collective-permute-start | bytes 221192 | tf_op jit(solution)/shard_map/ppermute | solution.py:179
  112.1 6.8 %collective-permute-start.20 = (f32[576,128]{1,0:T(8,128)S(1)}, f32[576,128]{1,0:T(8,128)S(1)}, u32[]{:S(2)}, u32[]{:S(2)}) collective-permute-start(f32[576,128]{1,0:T(8,128)S(1)} %bitcast.49), channel_id=1, source_target_pairs={{0,4},{2,6},{4,0},{6,2},{8,12},{10,14},{12,8},{14,10},{16,20},{18,... | collective-permute-start | bytes 884744 | tf_op jit(solution)/shard_map/ppermute | solution.py:179
  119.0 11.3 %collective-permute-start.21 = (f32[1152,128]{1,0:T(8,128)S(1)}, f32[1152,128]{1,0:T(8,128)}, u32[]{:S(2)}, u32[]{:S(2)}) collective-permute-start(f32[1152,128]{1,0:T(8,128)S(1)} %bitcast.44), channel_id=1, source_target_pairs={{0,1},{1,0},{2,3},{3,2},{4,5},{5,4},{6,7},{7,6},{8,9},{9,8},{10,11... | collective-permute-start | bytes 1769480 | tf_op jit(solution)/shard_map/ppermute | solution.py:179
  131.5 1.2 copy-start.8
  131.5 1.4 copy-start.10
  132.6 3.2 %collective-permute-start.22 = (f32[2,1152,128]{2,1,0:T(8,128)}, f32[2,1152,128]{2,1,0:T(8,128)}, u32[]{:S(2)}, u32[]{:S(2)}) collective-permute-start(f32[2,1152,128]{2,1,0:T(8,128)} %reverse_select_fusion.1), channel_id=1, source_target_pairs={{0,2},{2,0},{4,6},{6,4},{8,10},{10,8},{12,14},{14,12},{16,18},{18,... | collective-permute-start | bytes 3538952 | tf_op jit(solution)/shard_map/ppermute | solution.py:179

commit v3 on v2

--- a/solution.py
+++ b/solution.py
@@ -169,9 +169,16 @@
     half_gram(mine_ref[halo:, :], other_ref[...], second_ref[0], out_ref, None)
 
 
-def high_gram_kernel(second_ref, part_ref, top_ref, other_ref, base_ref, out_ref):
+def high_gram_kernel(pieces, second_ref, part_ref, top_ref, other_ref, base_ref, out_ref, all_ref):
     halo = top_ref.shape[0]
-    half_gram(part_ref[:halo, :] + top_ref[...], other_ref[...], second_ref[0], out_ref, base_ref)
+    half_gram(part_ref[:halo, :] + top_ref[...], other_ref[...], second_ref[0], all_ref, base_ref)
+    panels = top_ref.shape[1] // LANES
+    total = all_ref.shape[0]
+    cut = LANES * panels * (panels + 1) // 2
+    a, b, piece = cut // pieces, (total - cut) // pieces, total // pieces
+    for i in range(pieces):
+        out_ref[i * piece : i * piece + a, :] = all_ref[i * a : (i + 1) * a, :]
+        out_ref[i * piece + a : (i + 1) * piece, :] = all_ref[cut + i * b : cut + (i + 1) * b, :]
 
 
 def exchanged(block, axis, mask):
@@ -222,36 +229,94 @@
 
 def inverse_factor(block, out_ref):
     size = block.shape[0]
+    count = size // SUB
+    shape = (SUB, size)
     rows = [block[t : t + SUB] for t in range(0, size, SUB)]
-    sub = lax.broadcasted_iota(jnp.int32, (SUB, size), 0)
-    lane = lax.broadcasted_iota(jnp.int32, (SUB, size), 1)
-    for b in range(size // SUB):
+    sub = lax.broadcasted_iota(jnp.int32, shape, 0)
+    lane = lax.broadcasted_iota(jnp.int32, shape, 1)
+
+    def across(v, at):
+        return [jnp.broadcast_to(v[:, at + k : at + k + 1], shape) for k in range(SUB)]
+
+    def down(v, k):
+        return jnp.broadcast_to(v[k : k + 1], shape)
+
+    cols, below, ahead = across(rows[0], 0), across(rows[1], 0), across(rows[1], SUB)
+    for b in range(count):
         at = b * SUB
+        more = b + 1 < count
+        raw = list(below)
         here = (lane >= at) & (lane < at + SUB)
-        top = rows[b]
-        cols = [jnp.broadcast_to(top[:, at + k : at + k + 1], (SUB, size)) for k in range(SUB)]
-        top = jnp.where(here, jnp.where(lane - at == sub, 1.0, 0.0), top)
-        scale = jnp.zeros((SUB, size), F32)
-        done = jnp.zeros((SUB, size), F32)
+        top = jnp.where(here, jnp.where(lane - at == sub, 1.0, 0.0), rows[b])
+        scale = jnp.zeros(shape, F32)
+        done = jnp.zeros(shape, F32)
+        pivot = down(cols[0], 0)
         for k in range(SUB):
-            pivot = jnp.broadcast_to(cols[k][k : k + 1], (SUB, size))
             inverse = 1.0 / pivot
-            row = jnp.broadcast_to(top[k : k + 1], (SUB, size))
+            row = down(top, k)
             done = jnp.where(sub == k, row * lax.rsqrt(pivot), done)
             scale = jnp.where(sub == k, inverse, scale)
+            heads = [down(cols[m], k) for m in range(k + 1, SUB)]
+            if heads:
+                pivot = down(cols[k + 1], k + 1) - (heads[0] * inverse) * heads[0]
             ratio = jnp.where(sub == k, 0.0, cols[k] * inverse)
             top = top - ratio * row
-            for m in range(k + 1, SUB):
-                cols[m] = cols[m] - ratio * jnp.broadcast_to(cols[m][k : k + 1], (SUB, size))
+            part = below[k] * inverse
+            for m, head in enumerate(heads, k + 1):
+                cols[m] = cols[m] - ratio * head
+                if more:
+                    below[m] = below[m] - part * head
+            if more:
+                for j in range(SUB):
+                    ahead[j] = ahead[j] - part * down(below[k], j)
         out_ref[at : at + SUB, :] = jnp.where(lane < at + SUB, done, 0.0)
         top = top * scale
-        for t in range(b + 1, size // SUB):
-            left = rows[t]
-            kept = jnp.where(here, 0.0, left)
-            for k in range(SUB):
-                column = jnp.broadcast_to(left[:, at + k : at + k + 1], (SUB, size))
-                kept = kept - column * jnp.broadcast_to(top[k : k + 1], (SUB, size))
+        spread = [down(top, k) for k in range(SUB)]
+        for t in range(b + 1, count):
+            kept = jnp.where(here, 0.0, rows[t])
+            for k, column in enumerate(raw if t == b + 1 else across(rows[t], at)):
+                kept = kept - column * spread[k]
             rows[t] = kept
+        cols = ahead
+        if b + 2 < count:
+            below, ahead = across(rows[b + 2], at + SUB), across(rows[b + 2], at + 2 * SUB)
+
+
+def pair_of(v):
+    return jnp.concatenate(split(v), axis=1)
+
+
+def weights(pair):
+    hi, lo = pair[:, :LANES], pair[:, LANES:]
+    return jnp.concatenate(
+        [jnp.concatenate([hi, hi], axis=1), jnp.concatenate([lo, jnp.zeros_like(lo)], axis=1)], axis=0
+    )
+
+
+def folded(pair, weight):
+    both = contract(pair, weight, NT)
+    half = both.shape[1] // 2
+    return both[:, :half] + both[:, half:]
+
+
+def factor_panels(work_ref, pair_ref, weight_ref, inverse_ref):
+    def panel(p, carry):
+        mine = pl.ds(pl.multiple_of(p * LANES, LANES), LANES)
+
+        def update(k, inner):
+            work_ref[p] = work_ref[p] - folded(pair_ref[k], weights(pair_ref[k, mine, :]))
+            return inner
+
+        lax.fori_loop(0, p, update, 0)
+        inverse_factor(work_ref[p, mine, :], inverse_ref)
+        weight = weights(pair_of(inverse_ref[...]))
+        solved = folded(pair_of(work_ref[p]), weight)
+        weight_ref[p] = weight
+        pair_ref[p] = pair_of(solved)
+        work_ref[p] = solved
+        return carry
+
+    lax.fori_loop(0, work_ref.shape[0], panel, 0)
 
 
 def packed_block(gram_ref, row, col, panels):
@@ -259,51 +324,112 @@
     return gram_ref[at * LANES : (at + 1) * LANES, :]
 
 
-def halved_block(gram_ref, row, col, panels):
-    mid = panels // 2
-    triangle = mid * (mid + 1) // 2
-    if (row < mid) == (col < mid):
-        second, row, col = int(row >= mid), row % mid, col % mid
-        at = sum(mid - p for p in range(col)) + row - col
-    else:
-        second, at = divmod(row - mid, mid // 2)
-        at += triangle + col * (mid // 2)
-    chunk = gram_ref.shape[2] // LANES
-    part, at = divmod(at, chunk)
-    return gram_ref[part, second, at * LANES : (at + 1) * LANES, :]
-
-
-def factor_kernel(scale, block_of, gram_ref, rows_ref, out_ref, work_ref, hi_ref, lo_ref, inverse_ref):
-    panels, total = work_ref.shape[:2]
+def factor_kernel(scale, gram_ref, rows_ref, out_ref, work_ref, pair_ref, weight_ref, inverse_ref):
+    panels = work_ref.shape[0]
     size = panels * LANES
     for p in range(panels):
         for r in range(panels):
-            block = block_of(gram_ref, r, p, panels) * scale if r >= p else jnp.zeros((LANES, LANES), F32)
+            block = packed_block(gram_ref, r, p, panels) * scale if r >= p else jnp.zeros((LANES, LANES), F32)
             work_ref[p, r * LANES : (r + 1) * LANES, :] = block
         work_ref[p, size:, :] = rows_ref[:, p * LANES : (p + 1) * LANES]
-
-    def panel(p, carry):
-        offset = pl.multiple_of(p * LANES, LANES)
-
-        def update(k, inner):
-            mine = pl.ds(offset, LANES)
-            pair = (hi_ref[k, mine, :], lo_ref[k, mine, :])
-            work_ref[p] = work_ref[p] - product((hi_ref[k], lo_ref[k]), pair, NT)
-            return inner
-
-        lax.fori_loop(0, p, update, 0)
-        inverse_factor(work_ref[p, pl.ds(offset, LANES), :], inverse_ref)
-        solved = product(split(work_ref[p]), split(inverse_ref[...]), NT)
-        hi_ref[p], lo_ref[p] = split(solved)
-        work_ref[p] = solved
-        return carry
-
-    lax.fori_loop(0, panels, panel, 0)
+    factor_panels(work_ref, pair_ref, weight_ref, inverse_ref)
     for p in range(panels):
         out_ref[:, p * LANES : (p + 1) * LANES] = work_ref[p, size:, :]
 
 
-def any_orb_gram(part, top):
+def factor_all(gram, rows, scale):
+    count, width = rows.shape
+    panels = width // LANES
+    scratch = [
+        pltpu.VMEM((panels, width + count, LANES), F32),
+        pltpu.VMEM((panels, width + count, 2 * LANES), BF16),
+        pltpu.VMEM((panels, 2 * LANES, 2 * LANES), BF16),
+        pltpu.VMEM((LANES, LANES), F32),
+    ]
+    return kernel_call(lambda *refs: factor_kernel(scale, *refs), f32(count, width), scratch)(gram, rows)
+
+
+def quarter_block(ref, second, at):
+    part, at = divmod(at, ref.shape[2] // LANES)
+    return ref[part, second, at * LANES : (at + 1) * LANES, :]
+
+
+def triangle_block(ref, second, row, col, panels):
+    return quarter_block(ref, second, sum(panels - p for p in range(col)) + row - col)
+
+
+def first_kernel(scale, tri_ref, rows_ref, out_ref, pair_ref, weight_ref, work_ref, inverse_ref):
+    panels = work_ref.shape[0]
+    size = panels * LANES
+    for p in range(panels):
+        for r in range(panels):
+            block = jnp.zeros((LANES, LANES), F32)
+            if r >= p:
+                block = triangle_block(tri_ref, 0, r, p, panels) * scale
+            work_ref[p, r * LANES : (r + 1) * LANES, :] = block
+        work_ref[p, size:, :] = rows_ref[:, p * LANES : (p + 1) * LANES]
+    factor_panels(work_ref, pair_ref, weight_ref, inverse_ref)
+    for p in range(panels):
+        out_ref[:, p * LANES : (p + 1) * LANES] = work_ref[p, size:, :]
+
+
+def second_kernel(
+    scale, tri_ref, cross_ref, rows_ref, done_ref, pair_ref, weight_ref,
+    out_ref, work_ref, left_ref, new_pair_ref, new_weight_ref, inverse_ref,
+):
+    panels = work_ref.shape[0]
+    size = panels * LANES
+    half = panels // 2
+    for p in range(panels):
+        blocks = []
+        for r in range(panels):
+            second, inner = divmod(r, half)
+            blocks.append(quarter_block(cross_ref, second, p * half + inner))
+        solve = jnp.concatenate(blocks, axis=0) * scale
+        for k in range(p):
+            pair = left_ref[:size, 2 * k * LANES : 2 * (k + 1) * LANES]
+            solve = solve - folded(pair, weights(pair_ref[k, p * LANES : (p + 1) * LANES, :]))
+        span = slice(2 * p * LANES, 2 * (p + 1) * LANES)
+        left_ref[:size, span] = pair_of(folded(pair_of(solve), weight_ref[p]))
+        left_ref[size:, span] = pair_ref[p, size:, :]
+    for p in range(panels):
+        mine = left_ref[p * LANES : (p + 1) * LANES, :]
+        weight = jnp.concatenate(
+            [weights(mine[:, 2 * k * LANES : 2 * (k + 1) * LANES]) for k in range(panels)], axis=1
+        )
+        drop = folded(left_ref[...], weight)
+        for r in range(panels):
+            block = jnp.zeros((LANES, LANES), F32)
+            if r >= p:
+                block = triangle_block(tri_ref, 1, r, p, panels) * scale - drop[r * LANES : (r + 1) * LANES]
+            work_ref[p, r * LANES : (r + 1) * LANES, :] = block
+        work_ref[p, size:, :] = rows_ref[:, size + p * LANES : size + (p + 1) * LANES] - drop[size:]
+    factor_panels(work_ref, new_pair_ref, new_weight_ref, inverse_ref)
+    out_ref[:, :size] = done_ref[...]
+    for p in range(panels):
+        out_ref[:, size + p * LANES : size + (p + 1) * LANES] = work_ref[p, size:, :]
+
+
+def factor_halves(tri, cross, rows, scale):
+    count, width = rows.shape
+    size = width // 2
+    panels = size // LANES
+    total = size + count
+    pairs, weight = (panels, total, 2 * LANES), (panels, 2 * LANES, 2 * LANES)
+    work = [pltpu.VMEM((panels, total, LANES), F32)]
+    inverse = [pltpu.VMEM((LANES, LANES), F32)]
+    done, pair, mult = kernel_call(
+        lambda *refs: first_kernel(scale, *refs),
+        [f32(count, size), bf16(*pairs), bf16(*weight)],
+        work + inverse,
+    )(tri, rows)
+    more = [pltpu.VMEM((total, panels * 2 * LANES), BF16), pltpu.VMEM(pairs, BF16), pltpu.VMEM(weight, BF16)]
+    return kernel_call(
+        lambda *refs: second_kernel(scale, *refs), f32(count, width), work + more + inverse
+    )(tri, cross, rows, done, pair, mult)
+
+
+def any_orb(part, top, scale):
     halo = top.shape[0]
     current = jnp.concatenate([part[:halo] + top, part[halo:]], axis=0)
     rows = lax.all_to_all(current, "orb", split_axis=0, concat_axis=1, tiled=True)
@@ -311,10 +437,10 @@
     packed = LANES * panels * (panels + 1) // 2
     gram = kernel_call(gram_kernel, f32(packed, LANES))(rows)
     dom = bits("dom")
-    return rows, summed(gram, dom[:1] + bits("orb") + dom[1:]), packed_block
-
-
-def two_orb_gram(part, top):
+    return factor_all(summed(gram, dom[:1] + bits("orb") + dom[1:]), rows, scale)
+
+
+def two_orb(part, top, scale):
     own, cols = part.shape
     halo = top.shape[0]
     second = lax.axis_index("orb")
@@ -328,9 +454,8 @@
     dom = bits("dom")
     stages = dom if len(dom) < 4 else dom[:-2] + [("dom", dom[-2][1], 4)]
     gram = scattered(gram, stages)
-    for stage in reversed(stages[1:]):
-        gram = gathered(gram, stage).reshape(-1, LANES)
-    gram = gathered(gathered(gram, ("orb", 1, 2)), stages[0])
+    cut = LANES * panels * (panels + 1) // 2 // lax.axis_size("dom")
+    tri, cross = [everywhere(piece, stages) for piece in (gram[:cut], gram[cut:])]
     mine = jnp.concatenate([part[:halo] + top, part[halo:]], axis=0).reshape(2, own // 2, cols)
     other = jnp.concatenate([high, low], axis=0).reshape(2, own // 2, cols)
     mine = jnp.where(second == 0, mine[0], mine[1])
@@ -338,15 +463,22 @@
     rows = jnp.where(
         second == 0, jnp.concatenate([mine, other], axis=1), jnp.concatenate([other, mine], axis=1)
     )
-    return rows, gram, halved_block
-
-
-def with_flag(body, out_shape, count):
+    return factor_halves(tri, cross, rows, scale)
+
+
+def everywhere(block, stages):
+    for stage in reversed(stages[1:]):
+        block = gathered(block, stage).reshape(-1, LANES)
+    return gathered(gathered(block, ("orb", 1, 2)), stages[0])
+
+
+def with_flag(body, out_shape, count, scratch=()):
     specs = [pl.BlockSpec(memory_space=pltpu.SMEM)] + [pl.BlockSpec(memory_space=pltpu.VMEM)] * count
     return pl.pallas_call(
         body,
         out_shape=out_shape,
         in_specs=specs,
+        scratch_shapes=list(scratch),
         compiler_params=pltpu.CompilerParams(vmem_limit_bytes=VMEM_BYTES),
     )
 
@@ -357,7 +489,8 @@
 
 
 def high_gram(flag, part, top, high, gram):
-    return with_flag(high_gram_kernel, f32(*gram.shape), 4)(flag, part, top, high, gram)
+    kernel = lambda *refs: high_gram_kernel(lax.axis_size("dom"), *refs)
+    return with_flag(kernel, f32(*gram.shape), 4, [pltpu.VMEM(gram.shape, F32)])(flag, part, top, high, gram)
 
 
 def body(orbitals, cell_mats, cell_map):
@@ -366,18 +499,15 @@
     node_total = own * lax.axis_size("dom")
     matrix = kernel_call(order_kernel, [bf16(size, size)] * 2)(cell_map, cell_mats)
     part, top = filtered_columns(orbitals, matrix)
-    two = lax.axis_size("orb") == 2 and cols % (2 * LANES) == 0 and lax.axis_size("dom") > 1
-    rows, gram, block_of = (two_orb_gram if two else any_orb_gram)(part, top)
-    count, width = rows.shape
-    panels = width // LANES
-    scratch = [
-        pltpu.VMEM((panels, width + count, LANES), F32),
-        pltpu.VMEM((panels, width + count, LANES), BF16),
-        pltpu.VMEM((panels, width + count, LANES), BF16),
-        pltpu.VMEM((LANES, LANES), F32),
-    ]
-    factor = lambda *refs: factor_kernel(1.0 / node_total, block_of, *refs)
-    return kernel_call(factor, f32(count, width), scratch)(gram, rows)
+    panels = cols // LANES
+    two = (
+        lax.axis_size("orb") == 2
+        and lax.axis_size("dom") > 1
+        and cols % (2 * LANES) == 0
+        and (LANES * panels * (panels + 1) // 2) % lax.axis_size("dom") == 0
+        and (LANES * panels * panels // 2) % lax.axis_size("dom") == 0
+    )
+    return (two_orb if two else any_orb)(part, top, 1.0 / node_total)
 
 
 def solution(mesh):

time: 191 us -> 164 us (0.86)
  Pallas kernels: 65.9 us -> 47.6 us
  waiting for transfers between devices: 67 us -> 55.2 us
  starting transfers between devices: 43.2 us -> 51 us
  other arithmetic: 6.56 us -> 2.15 us
    pallas_call x2 -> x3, Pallas kernels: 54.3 us -> 36.1 us  [the longest x1 19.2 us: factor_halves(): kernel_call(lambda *refs: second_kernel(scale, *refs), f32(count, width),...]
    ppermute x13 -> x19, waiting for transfers between devices: 43 us -> 31.2 us  [exchanged(): return lax.ppermute(block, axis, route)]
    ppermute x13 -> x19, starting transfers between devices: 19.7 us -> 27.5 us  [exchanged(): return lax.ppermute(block, axis, route)]
    another operation x5 -> x10, other arithmetic: 2.82 us -> 0.38 us  [gathered(): jnp.stack([block] + [exchanged(block, axis, d * unit) for d in range(1, c...]
    unnamed x22 -> x16, local copies, waits for them, and re-layouts: 5.88 us -> 4.93 us
  transfers between devices with their start and end apart: 23 -> 29, of which waited for: 17 -> 19; matrix products, arithmetic and copies ran while one was open for 0% -> 1% of each run, Pallas kernels for 1% -> 2%
where the time goes in v3:
time: 164 us; the launch traced here: 163 us
  waiting for transfers between devices  55.2 us (34%)
  starting transfers between devices  51 us (31%)
  Pallas kernels  47.6 us (29%)
  local copies, waits for them, and re-layouts  6.94 us (4%)
  other arithmetic  2.15 us (1%)
    ppermute x19, waiting for transfers between devices, exchanged(): return lax.ppermute(block, axis, route)  31.2 us
    ppermute x19, starting transfers between devices, exchanged(): return lax.ppermute(block, axis, route)  27.5 us
    ppermute x10, waiting for transfers between devices, shifted(): return lax.ppermute(block, axis, route)  24 us
    ppermute x10, starting transfers between devices, shifted(): return lax.ppermute(block, axis, route)  23.6 us
    pallas_call x1, Pallas kernels, factor_halves(): kernel_call(lambda *refs: second_kernel(scale, *refs), f32(count, width),...  19.2 us
    pallas_call x1, Pallas kernels, factor_halves(): kernel_call(lambda *refs: first_kernel(scale, *refs), [f32(count, size),...  15.8 us
    pallas_call x5, Pallas kernels, filtered_columns(): got = kernel_call(body, outs)(*matrix, *state)  8.93 us
    unnamed x16, local copies, waits for them, and re-layouts  4.93 us
  transfers between devices with their start and end apart: 29, of which 19 were waited for; matrix products, arithmetic and copies ran while one was open for 1% of the time, Pallas kernels for 2%

profile of v3, /device:TPU:0, one launch (start us, length us, event | category | flops | bytes accessed | tf_op | source)
XLA Modules:
  0.0 163.3 jit_solution(1369080909304849551)
XLA Ops:
  0.0 1.0 slice.36
  1.0 5.5 %collective-permute-start = (f32[128,512]{1,0:T(8,128)S(1)}, f32[128,512]{1,0:T(8,128)S(1)}, u32[]{:S(2)}, u32[]{:S(2)}) collective-permute-start(f32[128,512]{1,0:T(8,128)S(1)} %slice.36), channel_id=1, source_target_pairs={{2,0},{4,2},{6,4},{8,6},{10,8},{12,10},{14,12},{16,14},{18,16},{20... | collective-permute-start | bytes 786440 | tf_op jit(solution)/shard_map/ppermute | solution.py:101
  6.6 1.2 copy-done.4
  7.8 0.7 copy-done.5
  8.5 1.3 shard_map.37
  9.8 0.7 collective-permute-done.refs_3_
  10.5 1.0 shard_map.38
  11.5 1.0 copy-done.3
  12.5 4.6 %collective-permute-start.2 = (f32[128,512]{1,0:T(8,128)S(1)}, f32[128,512]{1,0:T(8,128)S(1)}, u32[]{:S(2)}, u32[]{:S(2)}) collective-permute-start(f32[128,512]{1,0:T(8,128)S(1)} %get-tuple-element.32), channel_id=1, source_target_pairs={{2,0},{4,2},{6,4},{8,6},{10,8},{12,10},{14,12},{16,14},{18,16},{20... | collective-permute-start | bytes 786440 | tf_op jit(solution)/shard_map/ppermute | solution.py:101
  17.1 4.1 %collective-permute-done.1.refs_3_ = f32[128,512]{1,0:T(8,128)S(1)} collective-permute-done((f32[128,512]{1,0:T(8,128)S(1)}, f32[128,512]{1,0:T(8,128)S(1)}, u32[]{:S(2)}, u32[]{:S(2)}) %collective-permute-start.1) | collective-permute-done | bytes 262176 | tf_op jit(solution)/shard_map/ppermute | solution.py:101
  21.2 2.3 %shard_map.39 = (f32[512,512]{1,0:T(8,128)S(1)}, f32[512,512]{1,0:T(8,128)S(1)}, f32[128,512]{1,0:T(8,128)S(1)}, f32[128,512]{1,0:T(8,128)S(1)}) custom-call(bf16[512,512]{1,0:T(8,128)(2,1)S(1)} %get-tuple-element.28.refs_0_, bf16[512,512]{1,0:T(8,128)(2,1)S(1)} %get-tuple-element.29.refs_1_, f32[512,512]{1,0:T(8,128)S(1)} %get-tuple-element.30.refs_2_, ...), custom_call_target="tpu_custom_call" | custom-call | tf_op jit(solution)/shard_map/pallas_call | solution.py:117
  23.5 1.0 copy-done.1
  24.5 4.4 %collective-permute-start.4 = (f32[128,512]{1,0:T(8,128)S(1)}, f32[128,512]{1,0:T(8,128)S(1)}, u32[]{:S(2)}, u32[]{:S(2)}) collective-permute-start(f32[128,512]{1,0:T(8,128)S(1)} %get-tuple-element.36), channel_id=1, source_target_pairs={{2,0},{4,2},{6,4},{8,6},{10,8},{12,10},{14,12},{16,14},{18,16},{20... | collective-permute-start | bytes 786440 | tf_op jit(solution)/shard_map/ppermute | solution.py:101
  28.9 4.1 %collective-permute-done.3.refs_3_ = f32[128,512]{1,0:T(8,128)S(1)} collective-permute-done((f32[128,512]{1,0:T(8,128)S(1)}, f32[128,512]{1,0:T(8,128)S(1)}, u32[]{:S(2)}, u32[]{:S(2)}) %collective-permute-start.3) | collective-permute-done | bytes 262176 | tf_op jit(solution)/shard_map/ppermute | solution.py:101
  33.0 2.3 %shard_map.40 = (f32[512,512]{1,0:T(8,128)S(1)}, f32[512,512]{1,0:T(8,128)S(1)}, f32[128,512]{1,0:T(8,128)S(1)}, f32[128,512]{1,0:T(8,128)S(1)}) custom-call(bf16[512,512]{1,0:T(8,128)(2,1)S(1)} %get-tuple-element.28.refs_0_, bf16[512,512]{1,0:T(8,128)(2,1)S(1)} %get-tuple-element.29.refs_1_, f32[512,512]{1,0:T(8,128)S(1)} %get-tuple-element.34.refs_2_, ...), custom_call_target="tpu_custom_call" | custom-call | tf_op jit(solution)/shard_map/pallas_call | solution.py:117
  35.3 1.0 copy-done.2
  36.3 4.4 %collective-permute-start.6 = (f32[128,512]{1,0:T(8,128)S(1)}, f32[128,512]{1,0:T(8,128)S(1)}, u32[]{:S(2)}, u32[]{:S(2)}) collective-permute-start(f32[128,512]{1,0:T(8,128)S(1)} %get-tuple-element.40), channel_id=1, source_target_pairs={{2,0},{4,2},{6,4},{8,6},{10,8},{12,10},{14,12},{16,14},{18,16},{20... | collective-permute-start | bytes 786440 | tf_op jit(solution)/shard_map/ppermute | solution.py:101
  40.7 4.1 %collective-permute-done.5.refs_3_ = f32[128,512]{1,0:T(8,128)S(1)} collective-permute-done((f32[128,512]{1,0:T(8,128)S(1)}, f32[128,512]{1,0:T(8,128)S(1)}, u32[]{:S(2)}, u32[]{:S(2)}) %collective-permute-start.5) | collective-permute-done | bytes 262176 | tf_op jit(solution)/shard_map/ppermute | solution.py:101
  44.9 2.3 %shard_map.41 = (f32[512,512]{1,0:T(8,128)S(1)}, f32[512,512]{1,0:T(8,128)S(1)}, f32[128,512]{1,0:T(8,128)S(1)}, f32[128,512]{1,0:T(8,128)S(1)}) custom-call(bf16[512,512]{1,0:T(8,128)(2,1)S(1)} %get-tuple-element.28.refs_0_, bf16[512,512]{1,0:T(8,128)(2,1)S(1)} %get-tuple-element.29.refs_1_, f32[512,512]{1,0:T(8,128)S(1)} %get-tuple-element.38.refs_2_, ...), custom_call_target="tpu_custom_call" | custom-call | tf_op jit(solution)/shard_map/pallas_call | solution.py:117
  47.2 0.1 collective-permute-start.7
  47.3 4.4 %collective-permute-start.8 = (f32[128,512]{1,0:T(8,128)S(1)}, f32[128,512]{1,0:T(8,128)S(1)}, u32[]{:S(2)}, u32[]{:S(2)}) collective-permute-start(f32[128,512]{1,0:T(8,128)S(1)} %get-tuple-element.44), channel_id=1, source_target_pairs={{2,0},{4,2},{6,4},{8,6},{10,8},{12,10},{14,12},{16,14},{18,16},{20... | collective-permute-start | bytes 786440 | tf_op jit(solution)/shard_map/ppermute | solution.py:101
  51.7 4.1 %collective-permute-done.7.refs_3_ = f32[128,512]{1,0:T(8,128)S(1)} collective-permute-done((f32[128,512]{1,0:T(8,128)S(1)}, f32[128,512]{1,0:T(8,128)S(1)}, u32[]{:S(2)}, u32[]{:S(2)}) %collective-permute-start.7) | collective-permute-done | bytes 262176 | tf_op jit(solution)/shard_map/ppermute | solution.py:101
  55.8 1.0 shard_map.42
  56.9 1.6 collective-permute-start.11
  58.4 6.9 %collective-permute-done.9.refs_2_ = f32[128,512]{1,0:T(8,128)S(1)} collective-permute-done((f32[128,512]{1,0:T(8,128)S(1)}, f32[128,512]{1,0:T(8,128)S(1)}, u32[]{:S(2)}, u32[]{:S(2)}) %collective-permute-start.9) | collective-permute-done | bytes 262176 | tf_op jit(solution)/shard_map/ppermute | solution.py:101
  65.4 1.6 collective-permute-start.10
  67.0 1.9 %collective-permute-done.11.refs_2_ = f32[256,512]{1,0:T(8,128)S(1)} collective-permute-done((f32[256,512]{1,0:T(8,128)S(1)}, f32[256,512]{1,0:T(8,128)S(1)}, u32[]{:S(2)}, u32[]{:S(2)}) %collective-permute-start.11) | collective-permute-done | bytes 524320 | tf_op jit(solution)/shard_map/ppermute | solution.py:186
  68.9 1.3 shard_map.43.refs_4_
  70.3 1.6 collective-permute-done.10.refs_3_
  71.9 1.1 shard_map.44
  73.0 0.9 dynamic-slice_bitcast_fusion
  73.9 2.3 %collective-permute-done.12 = f32[1152,128]{1,0:T(8,128)} collective-permute-done((f32[1152,128]{1,0:T(8,128)}, f32[1152,128]{1,0:T(8,128)}, u32[]{:S(2)}, u32[]{:S(2)}) %collective-permute-start.12) | collective-permute-done | bytes 589856 | tf_op jit(solution)/shard_map/ppermute | solution.py:186
  76.2 1.1 bitcast_add_fusion
  77.4 0.1 collective-permute-start.13
  77.6 8.9 %collective-permute-done.13 = f32[576,128]{1,0:T(8,128)S(1)} collective-permute-done((f32[576,128]{1,0:T(8,128)S(1)}, f32[576,128]{1,0:T(8,128)S(1)}, u32[]{:S(2)}, u32[]{:S(2)}) %collective-permute-start.13) | collective-permute-done | bytes 294944 | tf_op jit(solution)/shard_map/ppermute | solution.py:186
  86.6 8.3 %collective-permute-start.16 = (f32[144,128]{1,0:T(8,128)S(1)}, f32[144,128]{1,0:T(8,128)S(1)}, u32[]{:S(2)}, u32[]{:S(2)}) collective-permute-start(f32[144,128]{1,0:T(8,128)S(1)} %get-tuple-element.52), channel_id=1, source_target_pairs={{0,24},{2,26},{4,28},{6,30},{8,16},{10,18},{12,20},{14,22},{16,8},... | collective-permute-start | bytes 221192 | tf_op jit(solution)/shard_map/ppermute | solution.py:186
  94.9 0.6 collective-permute-start.14
  95.5 0.1 maximum_select_fusion.refs_1_.refs_2_
  95.6 2.2 %collective-permute-done.16 = f32[144,128]{1,0:T(8,128)S(1)} collective-permute-done((f32[144,128]{1,0:T(8,128)S(1)}, f32[144,128]{1,0:T(8,128)S(1)}, u32[]{:S(2)}, u32[]{:S(2)}) %collective-permute-start.16) | collective-permute-done | bytes 73760 | tf_op jit(solution)/shard_map/ppermute | solution.py:186
  97.8 2.4 %collective-permute-done.15 = f32[144,128]{1,0:T(8,128)S(1)} collective-permute-done((f32[144,128]{1,0:T(8,128)S(1)}, f32[144,128]{1,0:T(8,128)S(1)}, u32[]{:S(2)}, u32[]{:S(2)}) %collective-permute-start.15) | collective-permute-done | bytes 73760 | tf_op jit(solution)/shard_map/ppermute | solution.py:186
  100.1 0.6 collective-permute-done.14
  100.8 2.1 %collective-permute-start.25 = (f32[64,128]{1,0:T(8,128)S(1)}, f32[64,128]{1,0:T(8,128)S(1)}, u32[]{:S(2)}, u32[]{:S(2)}) collective-permute-start(f32[64,128]{1,0:T(8,128)S(1)} %get-tuple-element.55), channel_id=1, source_target_pairs={{0,24},{2,26},{4,28},{6,30},{8,16},{10,18},{12,20},{14,22},{16,8},... | collective-permute-start | bytes 98312 | tf_op jit(solution)/shard_map/ppermute | solution.py:186
  102.9 0.5 collective-permute-start.24
  103.3 1.9 %collective-permute-start.23 = (f32[64,128]{1,0:T(8,128)S(1)}, f32[64,128]{1,0:T(8,128)S(1)}, u32[]{:S(2)}, u32[]{:S(2)}) collective-permute-start(f32[64,128]{1,0:T(8,128)S(1)} %get-tuple-element.55), channel_id=1, source_target_pairs={{0,8},{2,10},{4,12},{6,14},{8,0},{10,2},{12,4},{14,6},{16,24},{18,... | collective-permute-start | bytes 98312 | tf_op jit(solution)/shard_map/ppermute | solution.py:186
  105.2 2.0 %collective-permute-start.19 = (f32[80,128]{1,0:T(8,128)S(1)}, f32[80,128]{1,0:T(8,128)S(1)}, u32[]{:S(2)}, u32[]{:S(2)}) collective-permute-start(f32[80,128]{1,0:T(8,128)S(1)} %get-tuple-element.57), channel_id=1, source_target_pairs={{0,24},{2,26},{4,28},{6,30},{8,16},{10,18},{12,20},{14,22},{16,8},... | collective-permute-start | bytes 122888 | tf_op jit(solution)/shard_map/ppermute | solution.py:186
  107.3 2.3 %collective-permute-start.17 = (f32[80,128]{1,0:T(8,128)S(1)}, f32[80,128]{1,0:T(8,128)S(1)}, u32[]{:S(2)}, u32[]{:S(2)}) collective-permute-start(f32[80,128]{1,0:T(8,128)S(1)} %get-tuple-element.57), channel_id=1, source_target_pairs={{0,8},{2,10},{4,12},{6,14},{8,0},{10,2},{12,4},{14,6},{16,24},{18,... | collective-permute-start | bytes 122888 | tf_op jit(solution)/shard_map/ppermute | solution.py:186
  109.7 1.6 collective-permute-start.26
  111.3 0.9 collective-permute-done.18
  112.2 1.5 collective-permute-start.20
  113.8 1.0 collective-permute-done.26
  114.8 1.6 collective-permute-start.27
  116.4 1.3 collective-permute-done.20
  117.7 1.6 collective-permute-start.21
  119.3 3.1 %collective-permute-done.27 = f32[512,128]{1,0:T(8,128)S(1)} collective-permute-done((f32[512,128]{1,0:T(8,128)S(1)}, f32[512,128]{1,0:T(8,128)S(1)}, u32[]{:S(2)}, u32[]{:S(2)}) %collective-permute-start.27) | collective-permute-done | bytes 262176 | tf_op jit(solution)/shard_map/ppermute | solution.py:186
  122.4 0.1 collective-permute-start.28
  122.6 3.3 %collective-permute-done.21 = f32[640,128]{1,0:T(8,128)S(1)} collective-permute-done((f32[640,128]{1,0:T(8,128)S(1)}, f32[640,128]{1,0:T(8,128)S(1)}, u32[]{:S(2)}, u32[]{:S(2)}) %collective-permute-start.21) | collective-permute-done | bytes 327712 | tf_op jit(solution)/shard_map/ppermute | solution.py:186
  126.0 0.1 collective-permute-start.22
  126.1 0.1 pad_maximum_fusion.1
  126.2 0.1 reverse_select_fusion.1.refs_1_
  126.3 1.9 %collective-permute-done.22 = f32[2,640,128]{2,1,0:T(8,128)S(1)} collective-permute-done((f32[2,640,128]{2,1,0:T(8,128)S(1)}, f32[2,640,128]{2,1,0:T(8,128)S(1)}, u32[]{:S(2)}, u32[]{:S(2)}) %collective-permute-start.22) | collective-permute-done | bytes 655392 | tf_op jit(solution)/shard_map/ppermute | solution.py:186
  128.1 0.1 pad_maximum_fusion
  128.2 0.1 reverse_select_fusion.refs_0_
  128.3 15.8 %shard_map.45 = (f32[192,512]{1,0:T(8,128)S(1)}, bf16[4,704,256]{2,1,0:T(8,128)(2,1)S(1)}, bf16[4,256,256]{2,1,0:T(8,128)(2,1)S(1)}) custom-call(f32[2,2,640,128]{3,2,1,0:T(8,128)S(1)} %reverse_select_fusion.refs_0_, f32[192,1024]{1,0:T(8,128)S(1)} %maximum_select_fusion.refs_1_.refs_2_), custom_call_target="tpu_custom_call" | custom-call | tf_op jit(solution)/shard_map/pallas_call | solution.py:421
  144.1 19.2 %shard_map.46 = f32[192,1024]{1,0:T(8,128)} custom-call(f32[2,2,640,128]{3,2,1,0:T(8,128)S(1)} %reverse_select_fusion.refs_0_, f32[2,2,512,128]{3,2,1,0:T(8,128)S(1)} %reverse_select_fusion.1.refs_1_, f32[192,1024]{1,0:T(8,128)S(1)} %maximum_select_fusion.refs_1_.refs_2_, f32[192,512]{1,0:T(8,128)S(1)} %get-tuple-element.48.refs_3_, ...), custom_call_target="tpu_custom_call" | custom-call | tf_op jit(solution)/shard_map/pallas_call | solution.py:427
  (54 shorter events, 0.8 us)
Async XLA Ops:
  0.0 10.5 %copy-start = (f32[384,512]{1,0:T(8,128)S(1)}, f32[384,512]{1,0:T(8,128)}, u32[]{:S(2)}) copy-start(f32[384,512]{1,0:T(8,128)} %refs_2_.1) | copy-start | bytes 2359300
  1.0 9.4 %collective-permute-start = (f32[128,512]{1,0:T(8,128)S(1)}, f32[128,512]{1,0:T(8,128)S(1)}, u32[]{:S(2)}, u32[]{:S(2)}) collective-permute-start(f32[128,512]{1,0:T(8,128)S(1)} %slice.36), channel_id=1, source_target_pairs={{2,0},{4,2},{6,4},{8,6},{10,8},{12,10},{14,12},{16,14},{18,16},{20... | collective-permute-start | bytes 786440 | tf_op jit(solution)/shard_map/ppermute | solution.py:101
  6.6 1.2 copy-start.4
  7.8 0.7 copy-start.5
  11.5 1.0 copy-start.3
  12.5 8.7 %collective-permute-start.1 = (f32[128,512]{1,0:T(8,128)S(1)}, f32[128,512]{1,0:T(8,128)S(1)}, u32[]{:S(2)}, u32[]{:S(2)}) collective-permute-start(f32[128,512]{1,0:T(8,128)S(1)} %get-tuple-element.31), channel_id=1, source_target_pairs={{30,0},{0,2},{2,4},{4,6},{6,8},{8,10},{10,12},{12,14},{14,16},{16,... | collective-permute-start | bytes 786440 | tf_op jit(solution)/shard_map/ppermute | solution.py:101
  12.5 8.7 %collective-permute-start.2 = (f32[128,512]{1,0:T(8,128)S(1)}, f32[128,512]{1,0:T(8,128)S(1)}, u32[]{:S(2)}, u32[]{:S(2)}) collective-permute-start(f32[128,512]{1,0:T(8,128)S(1)} %get-tuple-element.32), channel_id=1, source_target_pairs={{2,0},{4,2},{6,4},{8,6},{10,8},{12,10},{14,12},{16,14},{18,16},{20... | collective-permute-start | bytes 786440 | tf_op jit(solution)/shard_map/ppermute | solution.py:101
  23.5 1.0 copy-start.1
  24.5 8.5 %collective-permute-start.3 = (f32[128,512]{1,0:T(8,128)S(1)}, f32[128,512]{1,0:T(8,128)S(1)}, u32[]{:S(2)}, u32[]{:S(2)}) collective-permute-start(f32[128,512]{1,0:T(8,128)S(1)} %get-tuple-element.35), channel_id=1, source_target_pairs={{30,0},{0,2},{2,4},{4,6},{6,8},{8,10},{10,12},{12,14},{14,16},{16,... | collective-permute-start | bytes 786440 | tf_op jit(solution)/shard_map/ppermute | solution.py:101
  24.5 8.5 %collective-permute-start.4 = (f32[128,512]{1,0:T(8,128)S(1)}, f32[128,512]{1,0:T(8,128)S(1)}, u32[]{:S(2)}, u32[]{:S(2)}) collective-permute-start(f32[128,512]{1,0:T(8,128)S(1)} %get-tuple-element.36), channel_id=1, source_target_pairs={{2,0},{4,2},{6,4},{8,6},{10,8},{12,10},{14,12},{16,14},{18,16},{20... | collective-permute-start | bytes 786440 | tf_op jit(solution)/shard_map/ppermute | solution.py:101
  35.3 1.0 copy-start.2
  36.3 8.6 %collective-permute-start.5 = (f32[128,512]{1,0:T(8,128)S(1)}, f32[128,512]{1,0:T(8,128)S(1)}, u32[]{:S(2)}, u32[]{:S(2)}) collective-permute-start(f32[128,512]{1,0:T(8,128)S(1)} %get-tuple-element.39), channel_id=1, source_target_pairs={{30,0},{0,2},{2,4},{4,6},{6,8},{8,10},{10,12},{12,14},{14,16},{16,... | collective-permute-start | bytes 786440 | tf_op jit(solution)/shard_map/ppermute | solution.py:101
  36.3 8.6 %collective-permute-start.6 = (f32[128,512]{1,0:T(8,128)S(1)}, f32[128,512]{1,0:T(8,128)S(1)}, u32[]{:S(2)}, u32[]{:S(2)}) collective-permute-start(f32[128,512]{1,0:T(8,128)S(1)} %get-tuple-element.40), channel_id=1, source_target_pairs={{2,0},{4,2},{6,4},{8,6},{10,8},{12,10},{14,12},{16,14},{18,16},{20... | collective-permute-start | bytes 786440 | tf_op jit(solution)/shard_map/ppermute | solution.py:101
  47.2 8.5 %collective-permute-start.7 = (f32[128,512]{1,0:T(8,128)S(1)}, f32[128,512]{1,0:T(8,128)S(1)}, u32[]{:S(2)}, u32[]{:S(2)}) collective-permute-start(f32[128,512]{1,0:T(8,128)S(1)} %get-tuple-element.43), channel_id=1, source_target_pairs={{30,0},{0,2},{2,4},{4,6},{6,8},{8,10},{10,12},{12,14},{14,16},{16,... | collective-permute-start | bytes 786440 | tf_op jit(solution)/shard_map/ppermute | solution.py:101
  47.3 8.5 %collective-permute-start.8 = (f32[128,512]{1,0:T(8,128)S(1)}, f32[128,512]{1,0:T(8,128)S(1)}, u32[]{:S(2)}, u32[]{:S(2)}) collective-permute-start(f32[128,512]{1,0:T(8,128)S(1)} %get-tuple-element.44), channel_id=1, source_target_pairs={{2,0},{4,2},{6,4},{8,6},{10,8},{12,10},{14,12},{16,14},{18,16},{20... | collective-permute-start | bytes 786440 | tf_op jit(solution)/shard_map/ppermute | solution.py:101
  56.8 8.6 %collective-permute-start.9 = (f32[128,512]{1,0:T(8,128)S(1)}, f32[128,512]{1,0:T(8,128)S(1)}, u32[]{:S(2)}, u32[]{:S(2)}) collective-permute-start(f32[128,512]{1,0:T(8,128)S(1)} %get-tuple-element.47), channel_id=1, source_target_pairs={{30,0},{0,2},{2,4},{4,6},{6,8},{8,10},{10,12},{12,14},{14,16},{16,... | collective-permute-start | bytes 786440 | tf_op jit(solution)/shard_map/ppermute | solution.py:101
  56.9 12.1 %collective-permute-start.11 = (f32[256,512]{1,0:T(8,128)S(1)}, f32[256,512]{1,0:T(8,128)S(1)}, u32[]{:S(2)}, u32[]{:S(2)}) collective-permute-start(f32[256,512]{1,0:T(8,128)S(1)} %slice.38), channel_id=1, source_target_pairs={{0,1},{1,0},{2,3},{3,2},{4,5},{5,4},{6,7},{7,6},{8,9},{9,8},{10,11... | collective-permute-start | bytes 1572872 | tf_op jit(solution)/shard_map/ppermute | solution.py:186
  65.4 4.9 %copy-start.6 = (f32[128,512]{1,0:T(8,128)}, f32[128,512]{1,0:T(8,128)S(1)}, u32[]{:S(2)}) copy-start(f32[128,512]{1,0:T(8,128)S(1)} %slice_add_fusion) | copy-start | bytes 786436
  65.4 6.4 %collective-permute-start.10 = (f32[128,512]{1,0:T(8,128)S(1)}, f32[128,512]{1,0:T(8,128)S(1)}, u32[]{:S(2)}, u32[]{:S(2)}) collective-permute-start(f32[128,512]{1,0:T(8,128)S(1)} %slice_add_fusion), channel_id=1, source_target_pairs={{0,1},{1,0},{2,3},{3,2},{4,5},{5,4},{6,7},{7,6},{8,9},{9,8},{10,11... | collective-permute-start | bytes 786440 | tf_op jit(solution)/shard_map/ppermute | solution.py:186
  73.9 3.6 %copy-start.7 = (f32[128,512]{1,0:T(8,128)S(1)}, f32[128,512]{1,0:T(8,128)}, u32[]{:S(2)}) copy-start(f32[128,512]{1,0:T(8,128)} %copy-done.6) | copy-start | bytes 786436
  73.9 2.3 %collective-permute-start.12 = (f32[1152,128]{1,0:T(8,128)}, f32[1152,128]{1,0:T(8,128)}, u32[]{:S(2)}, u32[]{:S(2)}) collective-permute-start(f32[1152,128]{1,0:T(8,128)} %dynamic-slice_bitcast_fusion), channel_id=1, source_target_pairs={{0,2},{2,0},{4,6},{6,4},{8,10},{10,8},{12,14},{14,12},{16,18},{18,... | collective-permute-start | bytes 1769480 | tf_op jit(solution)/shard_map/ppermute | solution.py:186
  77.4 9.1 %collective-permute-start.13 = (f32[576,128]{1,0:T(8,128)S(1)}, f32[576,128]{1,0:T(8,128)S(1)}, u32[]{:S(2)}, u32[]{:S(2)}) collective-permute-start(f32[576,128]{1,0:T(8,128)S(1)} %dynamic-slice_bitcast_fusion.1), channel_id=1, source_target_pairs={{0,4},{2,6},{4,0},{6,2},{8,12},{10,14},{12,8},{14,10},{16,20},{18,... | collective-permute-start | bytes 884744 | tf_op jit(solution)/shard_map/ppermute | solution.py:186
  86.6 11.2 %collective-permute-start.16 = (f32[144,128]{1,0:T(8,128)S(1)}, f32[144,128]{1,0:T(8,128)S(1)}, u32[]{:S(2)}, u32[]{:S(2)}) collective-permute-start(f32[144,128]{1,0:T(8,128)S(1)} %get-tuple-element.52), channel_id=1, source_target_pairs={{0,24},{2,26},{4,28},{6,30},{8,16},{10,18},{12,20},{14,22},{16,8},... | collective-permute-start | bytes 221192 | tf_op jit(solution)/shard_map/ppermute | solution.py:186
  94.9 5.3 %collective-permute-start.15 = (f32[144,128]{1,0:T(8,128)S(1)}, f32[144,128]{1,0:T(8,128)S(1)}, u32[]{:S(2)}, u32[]{:S(2)}) collective-permute-start(f32[144,128]{1,0:T(8,128)S(1)} %get-tuple-element.53), channel_id=1, source_target_pairs={{0,16},{2,18},{4,20},{6,22},{8,24},{10,26},{12,28},{14,30},{16,0},... | collective-permute-start | bytes 221192 | tf_op jit(solution)/shard_map/ppermute | solution.py:186
  94.9 5.9 %collective-permute-start.14 = (f32[144,128]{1,0:T(8,128)S(1)}, f32[144,128]{1,0:T(8,128)S(1)}, u32[]{:S(2)}, u32[]{:S(2)}) collective-permute-start(f32[144,128]{1,0:T(8,128)S(1)} %get-tuple-element.51), channel_id=1, source_target_pairs={{0,8},{2,10},{4,12},{6,14},{8,0},{10,2},{12,4},{14,6},{16,24},{18,... | collective-permute-start | bytes 221192 | tf_op jit(solution)/shard_map/ppermute | solution.py:186
  100.8 6.5 %collective-permute-start.25 = (f32[64,128]{1,0:T(8,128)S(1)}, f32[64,128]{1,0:T(8,128)S(1)}, u32[]{:S(2)}, u32[]{:S(2)}) collective-permute-start(f32[64,128]{1,0:T(8,128)S(1)} %get-tuple-element.55), channel_id=1, source_target_pairs={{0,24},{2,26},{4,28},{6,30},{8,16},{10,18},{12,20},{14,22},{16,8},... | collective-permute-start | bytes 98312 | tf_op jit(solution)/shard_map/ppermute | solution.py:186
  102.9 6.7 %collective-permute-start.24 = (f32[64,128]{1,0:T(8,128)S(1)}, f32[64,128]{1,0:T(8,128)S(1)}, u32[]{:S(2)}, u32[]{:S(2)}) collective-permute-start(f32[64,128]{1,0:T(8,128)S(1)} %get-tuple-element.55), channel_id=1, source_target_pairs={{0,16},{2,18},{4,20},{6,22},{8,24},{10,26},{12,28},{14,30},{16,0},... | collective-permute-start | bytes 98312 | tf_op jit(solution)/shard_map/ppermute | solution.py:186
  103.3 6.3 %collective-permute-start.23 = (f32[64,128]{1,0:T(8,128)S(1)}, f32[64,128]{1,0:T(8,128)S(1)}, u32[]{:S(2)}, u32[]{:S(2)}) collective-permute-start(f32[64,128]{1,0:T(8,128)S(1)} %get-tuple-element.55), channel_id=1, source_target_pairs={{0,8},{2,10},{4,12},{6,14},{8,0},{10,2},{12,4},{14,6},{16,24},{18,... | collective-permute-start | bytes 98312 | tf_op jit(solution)/shard_map/ppermute | solution.py:186
  105.2 6.1 %collective-permute-start.19 = (f32[80,128]{1,0:T(8,128)S(1)}, f32[80,128]{1,0:T(8,128)S(1)}, u32[]{:S(2)}, u32[]{:S(2)}) collective-permute-start(f32[80,128]{1,0:T(8,128)S(1)} %get-tuple-element.57), channel_id=1, source_target_pairs={{0,24},{2,26},{4,28},{6,30},{8,16},{10,18},{12,20},{14,22},{16,8},... | collective-permute-start | bytes 122888 | tf_op jit(solution)/shard_map/ppermute | solution.py:186
  107.3 4.9 %collective-permute-start.18 = (f32[80,128]{1,0:T(8,128)S(1)}, f32[80,128]{1,0:T(8,128)S(1)}, u32[]{:S(2)}, u32[]{:S(2)}) collective-permute-start(f32[80,128]{1,0:T(8,128)S(1)} %get-tuple-element.57), channel_id=1, source_target_pairs={{0,16},{2,18},{4,20},{6,22},{8,24},{10,26},{12,28},{14,30},{16,0},... | collective-permute-start | bytes 122888 | tf_op jit(solution)/shard_map/ppermute | solution.py:186
  107.3 4.9 %collective-permute-start.17 = (f32[80,128]{1,0:T(8,128)S(1)}, f32[80,128]{1,0:T(8,128)S(1)}, u32[]{:S(2)}, u32[]{:S(2)}) collective-permute-start(f32[80,128]{1,0:T(8,128)S(1)} %get-tuple-element.57), channel_id=1, source_target_pairs={{0,8},{2,10},{4,12},{6,14},{8,0},{10,2},{12,4},{14,6},{16,24},{18,... | collective-permute-start | bytes 122888 | tf_op jit(solution)/shard_map/ppermute | solution.py:186
  109.7 5.0 %collective-permute-start.26 = (f32[256,128]{1,0:T(8,128)S(1)}, f32[256,128]{1,0:T(8,128)S(1)}, u32[]{:S(2)}, u32[]{:S(2)}) collective-permute-start(f32[256,128]{1,0:T(8,128)S(1)} %bitcast.73), channel_id=1, source_target_pairs={{0,4},{2,6},{4,0},{6,2},{8,12},{10,14},{12,8},{14,10},{16,20},{18,... | collective-permute-start | bytes 393224 | tf_op jit(solution)/shard_map/ppermute | solution.py:186
  112.2 5.4 %collective-permute-start.20 = (f32[320,128]{1,0:T(8,128)S(1)}, f32[320,128]{1,0:T(8,128)S(1)}, u32[]{:S(2)}, u32[]{:S(2)}) collective-permute-start(f32[320,128]{1,0:T(8,128)S(1)} %bitcast.69), channel_id=1, source_target_pairs={{0,4},{2,6},{4,0},{6,2},{8,12},{10,14},{12,8},{14,10},{16,20},{18,... | collective-permute-start | bytes 491528 | tf_op jit(solution)/shard_map/ppermute | solution.py:186
  114.8 7.6 %collective-permute-start.27 = (f32[512,128]{1,0:T(8,128)S(1)}, f32[512,128]{1,0:T(8,128)S(1)}, u32[]{:S(2)}, u32[]{:S(2)}) collective-permute-start(f32[512,128]{1,0:T(8,128)S(1)} %bitcast.66), channel_id=1, source_target_pairs={{0,1},{1,0},{2,3},{3,2},{4,5},{5,4},{6,7},{7,6},{8,9},{9,8},{10,11... | collective-permute-start | bytes 786440 | tf_op jit(solution)/shard_map/ppermute | solution.py:186
  117.7 8.2 %collective-permute-start.21 = (f32[640,128]{1,0:T(8,128)S(1)}, f32[640,128]{1,0:T(8,128)S(1)}, u32[]{:S(2)}, u32[]{:S(2)}) collective-permute-start(f32[640,128]{1,0:T(8,128)S(1)} %bitcast.62), channel_id=1, source_target_pairs={{0,1},{1,0},{2,3},{3,2},{4,5},{5,4},{6,7},{7,6},{8,9},{9,8},{10,11... | collective-permute-start | bytes 983048 | tf_op jit(solution)/shard_map/ppermute | solution.py:186
  122.4 3.7 %collective-permute-start.28 = (f32[2,512,128]{2,1,0:T(8,128)S(1)}, f32[2,512,128]{2,1,0:T(8,128)S(1)}, u32[]{:S(2)}, u32[]{:S(2)}) collective-permute-start(f32[2,512,128]{2,1,0:T(8,128)S(1)} %reverse_select_fusion.3), channel_id=1, source_target_pairs={{0,2},{2,0},{4,6},{6,4},{8,10},{10,8},{12,14},{14,12},{16,18},{18,... | collective-permute-start | bytes 1572872 | tf_op jit(solution)/shard_map/ppermute | solution.py:186
  126.0 2.2 %collective-permute-start.22 = (f32[2,640,128]{2,1,0:T(8,128)S(1)}, f32[2,640,128]{2,1,0:T(8,128)S(1)}, u32[]{:S(2)}, u32[]{:S(2)}) collective-permute-start(f32[2,640,128]{2,1,0:T(8,128)S(1)} %reverse_select_fusion.2), channel_id=1, source_target_pairs={{0,2},{2,0},{4,6},{6,4},{8,10},{10,8},{12,14},{14,12},{16,18},{18,... | collective-permute-start | bytes 1966088 | tf_op jit(solution)/shard_map/ppermute | solution.py:186

commit v4 on v3

--- a/solution.py
+++ b/solution.py
@@ -12,7 +12,7 @@
 
 F32, BF16 = jnp.float32, jnp.bfloat16
 LANES, SUB = 128, 8
-VMEM_BYTES = 48 << 20
+VMEM_BYTES = 24 << 20
 
 
 def kernel_call(body, out_shape, scratch=()):
@@ -59,40 +59,55 @@
         out_ref[...] = contract(rows, pick, NT).astype(BF16)
 
 
-def step_kernel(order, own, hi_ref, lo_ref, *refs):
-    size = hi_ref.shape[0]
-    halo = size - own
+def first_kernel_of_filter(hi_ref, lo_ref, own_ref, applied_ref):
+    own = own_ref.shape[0]
+    scale = 1.0 / filter_half
+    applied_ref[...] = product((hi_ref[:, :own], lo_ref[:, :own]), split(own_ref[...]), NN) * scale
+
+
+def edge_columns(ref, own, first, rows=slice(None)):
+    right = ref[rows, own:]
+    if first:
+        return right
+    return jnp.concatenate([ref[rows, : ref.shape[1] - own], right], axis=1)
+
+
+def edge_kernel(order, own, hi_ref, lo_ref, applied_ref, *refs):
+    halo = hi_ref.shape[0] - own
+    scale = (1.0 if order == 0 else 2.0) / filter_half
+    count = 1 if order == 0 else 2
+    delta = split(jnp.concatenate([ref[...] for ref in refs[:count]], axis=0))
+    outs = refs[count:]
+    spans = [slice(own, own + halo)] if order == DEGREE - 1 else [slice(0, halo), slice(own, own + halo)]
+    for span, out_ref in zip(spans, outs):
+        block = [edge_columns(ref, own, order == 0, span) for ref in (hi_ref, lo_ref)]
+        out_ref[...] = applied_ref[span, :] + product(block, delta, NN) * scale
+
+
+def rest_kernel(order, own, hi_ref, lo_ref, applied_ref, vec_ref, *refs):
+    halo = hi_ref.shape[0] - own
+    scale = (1.0 if order == 0 else 2.0) / filter_half
+    last = order == DEGREE - 1
     if order == 0:
-        own_ref, bottom_ref = refs[:2]
-        vec = jnp.concatenate([own_ref[...], bottom_ref[...]], axis=0)
-        outs = refs[2:]
+        bottom = refs[0][...]
+        delta, outs = bottom, refs[1:]
+        vec = jnp.concatenate([vec_ref[...], bottom], axis=0)
     else:
-        part_ref, top_ref, bottom_ref = refs[:3]
+        top, bottom, before_ref = refs[0][...], refs[1][...], refs[2]
+        delta, outs = jnp.concatenate([top, bottom], axis=0), refs[3:]
         vec = jnp.concatenate(
-            [
-                part_ref[:halo, :] + top_ref[...],
-                part_ref[halo:own, :],
-                part_ref[own:, :] + bottom_ref[...],
-            ],
-            axis=0,
+            [vec_ref[:halo, :] + top, vec_ref[halo:own, :], vec_ref[own:, :] + bottom], axis=0
         )
-        outs = refs[3:]
+    rows = slice(0, own) if last else slice(0, own + halo)
+    columns = [edge_columns(ref, own, order == 0, rows) for ref in (hi_ref, lo_ref)]
+    part = applied_ref[rows, :] + product(columns, split(delta), NN) * scale
+    part = part - (filter_center * scale) * vec[rows]
     if order > 0:
-        before_ref, outs = outs[0], outs[1:]
-    scale = (1.0 if order == 0 else 2.0) / filter_half
-    applied = product((hi_ref[...], lo_ref[...]), split(vec), NN) * scale
-    part = applied - (filter_center * scale) * vec
-    if order > 0:
-        part = part - before_ref[...]
-    if order == DEGREE - 1:
-        next_ref, down_ref = outs
-        next_ref[...] = part[:own]
-    else:
-        now_ref, next_ref, up_ref, down_ref = outs
-        now_ref[...] = vec
-        next_ref[...] = part
-        up_ref[...] = applied[:halo]
-    down_ref[...] = applied[own:]
+        part = part - before_ref[rows, :]
+    outs[0][...] = part
+    if not last:
+        outs[1][...] = vec
+        outs[2][...] = product((hi_ref[...], lo_ref[...]), split(part), NN) * (2.0 / filter_half)
 
 
 def shifted(block, axis, distance):
@@ -105,24 +120,23 @@
     own, cols = orbitals.shape
     size = matrix[0].shape[0]
     halo = size - own
-    bottom = shifted(orbitals[:halo], "dom", -1)
-    state = (orbitals, bottom)
+    arrived = (shifted(orbitals[:halo], "dom", -1),)
+    applied = kernel_call(first_kernel_of_filter, f32(size, cols))(*matrix, orbitals)
+    vec, before = orbitals, ()
     for order in range(DEGREE):
         last = order == DEGREE - 1
-        outs = [f32(own if last else size, cols)]
+        edge = lambda *refs, order=order: edge_kernel(order, own, *refs)
+        rest = lambda *refs, order=order: rest_kernel(order, own, *refs)
+        sent = kernel_call(edge, [f32(halo, cols)] * (1 if last else 2))(*matrix, applied, *arrived)
+        moved = [shifted(sent[-1], "dom", 1)]
         if not last:
-            outs = [f32(size, cols)] + outs + [f32(halo, cols)]
-        outs.append(f32(halo, cols))
-        body = lambda *refs, order=order: step_kernel(order, own, *refs)
-        got = kernel_call(body, outs)(*matrix, *state)
+            moved.append(shifted(sent[0], "dom", -1))
+        outs = [f32(own, cols)] if last else [f32(size, cols)] * 3
+        got = kernel_call(rest, outs)(*matrix, applied, vec, *arrived, *before)
         if last:
-            part, down = got
-            top = shifted(down, "dom", 1)
-            return part, top
-        now, part, up, down = got
-        top = shifted(down, "dom", 1)
-        bottom = shifted(up, "dom", -1)
-        state = (part, top, bottom, now)
+            return got[0], moved[0]
+        vec, before, applied = got[0], (got[1],), got[2]
+        arrived = tuple(moved)
 
 
 def gram_kernel(rows_ref, out_ref):

time: 164 us -> 155 us (0.945)
  waiting for transfers between devices: 55.2 us -> 48.5 us
  local copies, waits for them, and re-layouts: 6.94 us -> 3.92 us
    ppermute x10, waiting for transfers between devices: 24 us -> 16.4 us  [shifted(): return lax.ppermute(block, axis, route)]
    unnamed x16 -> x10, local copies, waits for them, and re-layouts: 4.93 us -> 1.92 us
    pallas_call x5 -> x11, Pallas kernels: 8.93 us -> 9.44 us  [the longest x5 6.67 us: filtered_columns(): got = kernel_call(rest, outs)(*matrix, applied, vec, *arrived, *before)]
  transfers between devices with their start and end apart: 29 -> 29, of which waited for: 19 -> 18; matrix products, arithmetic and copies ran while one was open for 1% -> 1% of each run, Pallas kernels for 2% -> 7%
where the time goes in v4:
time: 155 us
  starting transfers between devices  51.7 us (33%)
  waiting for transfers between devices  48.5 us (31%)
  Pallas kernels  48.1 us (31%)
  local copies, waits for them, and re-layouts  3.92 us (3%)
  other arithmetic  2.15 us (1%)
    ppermute x19, waiting for transfers between devices, exchanged(): return lax.ppermute(block, axis, route)  32 us
    ppermute x19, starting transfers between devices, exchanged(): return lax.ppermute(block, axis, route)  27.7 us
    ppermute x10, starting transfers between devices, shifted(): return lax.ppermute(block, axis, route)  24 us
    pallas_call x1, Pallas kernels, factor_halves(): kernel_call(lambda *refs: second_kernel(scale, *refs), f32(count, width),...  19.2 us
    ppermute x10, waiting for transfers between devices, shifted(): return lax.ppermute(block, axis, route)  16.4 us
    pallas_call x1, Pallas kernels, factor_halves(): kernel_call(lambda *refs: first_kernel(scale, *refs), [f32(count, size),...  15.7 us
    pallas_call x5, Pallas kernels, filtered_columns(): got = kernel_call(rest, outs)(*matrix, applied, vec, *arrived, *before)  6.67 us
  transfers between devices with their start and end apart: 29, of which 18 were waited for; matrix products, arithmetic and copies ran while one was open for 1% of the time, Pallas kernels for 7%

profile of v4, /device:TPU:0, one launch (start us, length us, event | category | flops | bytes accessed | tf_op | source)
XLA Modules:
  0.0 154.8 jit_solution(12290925125683939738)
XLA Ops:
  0.0 1.0 slice.36
  1.0 5.5 %collective-permute-start = (f32[128,512]{1,0:T(8,128)S(1)}, f32[128,512]{1,0:T(8,128)S(1)}, u32[]{:S(2)}, u32[]{:S(2)}) collective-permute-start(f32[128,512]{1,0:T(8,128)S(1)} %slice.36), channel_id=1, source_target_pairs={{2,0},{4,2},{6,4},{8,6},{10,8},{12,10},{14,12},{16,14},{18,16},{20... | collective-permute-start | bytes 786440 | tf_op jit(solution)/shard_map/ppermute | solution.py:116
  6.6 1.2 copy-done.1
  7.8 0.7 copy-done.2
  8.5 1.3 shard_map.37
  9.8 1.0 shard_map.38.refs_2_
  10.8 0.4 shard_map.40
  11.2 4.5 %collective-permute-start.2 = (f32[128,512]{1,0:T(8,128)S(1)}, f32[128,512]{1,0:T(8,128)S(1)}, u32[]{:S(2)}, u32[]{:S(2)}) collective-permute-start(f32[128,512]{1,0:T(8,128)S(1)} %get-tuple-element.35), channel_id=1, source_target_pairs={{2,0},{4,2},{6,4},{8,6},{10,8},{12,10},{14,12},{16,14},{18,16},{20... | collective-permute-start | bytes 786440 | tf_op jit(solution)/shard_map/ppermute | solution.py:116
  15.6 1.5 shard_map.39
  17.2 2.5 %collective-permute-done.1.refs_4_.refs_3_ = f32[128,512]{1,0:T(8,128)S(1)} collective-permute-done((f32[128,512]{1,0:T(8,128)S(1)}, f32[128,512]{1,0:T(8,128)S(1)}, u32[]{:S(2)}, u32[]{:S(2)}) %collective-permute-start.1) | collective-permute-done | bytes 262176 | tf_op jit(solution)/shard_map/ppermute | solution.py:116
  19.7 0.4 shard_map.42
  20.1 4.6 %collective-permute-start.4 = (f32[128,512]{1,0:T(8,128)S(1)}, f32[128,512]{1,0:T(8,128)S(1)}, u32[]{:S(2)}, u32[]{:S(2)}) collective-permute-start(f32[128,512]{1,0:T(8,128)S(1)} %get-tuple-element.40), channel_id=1, source_target_pairs={{2,0},{4,2},{6,4},{8,6},{10,8},{12,10},{14,12},{16,14},{18,16},{20... | collective-permute-start | bytes 786440 | tf_op jit(solution)/shard_map/ppermute | solution.py:116
  24.7 1.5 shard_map.41
  26.3 2.5 %collective-permute-done.3.refs_4_.refs_3_ = f32[128,512]{1,0:T(8,128)S(1)} collective-permute-done((f32[128,512]{1,0:T(8,128)S(1)}, f32[128,512]{1,0:T(8,128)S(1)}, u32[]{:S(2)}, u32[]{:S(2)}) %collective-permute-start.3) | collective-permute-done | bytes 262176 | tf_op jit(solution)/shard_map/ppermute | solution.py:116
  28.8 0.4 shard_map.44
  29.3 4.6 %collective-permute-start.6 = (f32[128,512]{1,0:T(8,128)S(1)}, f32[128,512]{1,0:T(8,128)S(1)}, u32[]{:S(2)}, u32[]{:S(2)}) collective-permute-start(f32[128,512]{1,0:T(8,128)S(1)} %get-tuple-element.45), channel_id=1, source_target_pairs={{2,0},{4,2},{6,4},{8,6},{10,8},{12,10},{14,12},{16,14},{18,16},{20... | collective-permute-start | bytes 786440 | tf_op jit(solution)/shard_map/ppermute | solution.py:116
  33.9 1.5 shard_map.43
  35.4 2.5 %collective-permute-done.5.refs_4_.refs_3_ = f32[128,512]{1,0:T(8,128)S(1)} collective-permute-done((f32[128,512]{1,0:T(8,128)S(1)}, f32[128,512]{1,0:T(8,128)S(1)}, u32[]{:S(2)}, u32[]{:S(2)}) %collective-permute-start.5) | collective-permute-done | bytes 262176 | tf_op jit(solution)/shard_map/ppermute | solution.py:116
  37.9 0.4 shard_map.46
  38.4 4.6 %collective-permute-start.8 = (f32[128,512]{1,0:T(8,128)S(1)}, f32[128,512]{1,0:T(8,128)S(1)}, u32[]{:S(2)}, u32[]{:S(2)}) collective-permute-start(f32[128,512]{1,0:T(8,128)S(1)} %get-tuple-element.50), channel_id=1, source_target_pairs={{2,0},{4,2},{6,4},{8,6},{10,8},{12,10},{14,12},{16,14},{18,16},{20... | collective-permute-start | bytes 786440 | tf_op jit(solution)/shard_map/ppermute | solution.py:116
  43.0 1.5 shard_map.45
  44.5 2.4 %collective-permute-done.7.refs_4_.refs_3_ = f32[128,512]{1,0:T(8,128)S(1)} collective-permute-done((f32[128,512]{1,0:T(8,128)S(1)}, f32[128,512]{1,0:T(8,128)S(1)}, u32[]{:S(2)}, u32[]{:S(2)}) %collective-permute-start.7) | collective-permute-done | bytes 262176 | tf_op jit(solution)/shard_map/ppermute | solution.py:116
  46.9 0.3 shard_map.48
  47.3 0.5 shard_map.47.refs_1_
  47.9 1.6 %collective-permute-start.11 = (f32[256,512]{1,0:T(8,128)S(1)}, f32[256,512]{1,0:T(8,128)S(1)}, u32[]{:S(2)}, u32[]{:S(2)}) collective-permute-start(f32[256,512]{1,0:T(8,128)S(1)} %slice.46), channel_id=1, source_target_pairs={{0,1},{1,0},{2,3},{3,2},{4,5},{5,4},{6,7},{7,6},{8,9},{9,8},{10,11... | collective-permute-start | bytes 1572872 | tf_op jit(solution)/shard_map/ppermute | solution.py:200
  49.5 6.4 %collective-permute-done.9.refs_2_ = f32[128,512]{1,0:T(8,128)S(1)} collective-permute-done((f32[128,512]{1,0:T(8,128)S(1)}, f32[128,512]{1,0:T(8,128)S(1)}, u32[]{:S(2)}, u32[]{:S(2)}) %collective-permute-start.9) | collective-permute-done | bytes 262176 | tf_op jit(solution)/shard_map/ppermute | solution.py:116
  55.9 1.6 %collective-permute-start.10 = (f32[128,512]{1,0:T(8,128)S(1)}, f32[128,512]{1,0:T(8,128)S(1)}, u32[]{:S(2)}, u32[]{:S(2)}) collective-permute-start(f32[128,512]{1,0:T(8,128)S(1)} %slice_add_fusion), channel_id=1, source_target_pairs={{0,1},{1,0},{2,3},{3,2},{4,5},{5,4},{6,7},{7,6},{8,9},{9,8},{10,11... | collective-permute-start | bytes 786440 | tf_op jit(solution)/shard_map/ppermute | solution.py:200
  57.5 2.5 %collective-permute-done.11.refs_2_ = f32[256,512]{1,0:T(8,128)S(1)} collective-permute-done((f32[256,512]{1,0:T(8,128)S(1)}, f32[256,512]{1,0:T(8,128)S(1)}, u32[]{:S(2)}, u32[]{:S(2)}) %collective-permute-start.11) | collective-permute-done | bytes 524320 | tf_op jit(solution)/shard_map/ppermute | solution.py:200
  60.0 1.3 shard_map.49.refs_4_
  61.3 1.4 collective-permute-done.10.refs_3_
  62.8 1.1 shard_map.50
  63.9 0.9 dynamic-slice_bitcast_fusion
  64.8 2.3 %collective-permute-done.12 = f32[1152,128]{1,0:T(8,128)} collective-permute-done((f32[1152,128]{1,0:T(8,128)}, f32[1152,128]{1,0:T(8,128)}, u32[]{:S(2)}, u32[]{:S(2)}) %collective-permute-start.12) | collective-permute-done | bytes 589856 | tf_op jit(solution)/shard_map/ppermute | solution.py:200
  67.1 1.1 bitcast_add_fusion
  68.3 0.1 collective-permute-start.13
  68.5 8.9 %collective-permute-done.13 = f32[576,128]{1,0:T(8,128)S(1)} collective-permute-done((f32[576,128]{1,0:T(8,128)S(1)}, f32[576,128]{1,0:T(8,128)S(1)}, u32[]{:S(2)}, u32[]{:S(2)}) %collective-permute-start.13) | collective-permute-done | bytes 294944 | tf_op jit(solution)/shard_map/ppermute | solution.py:200
  77.4 8.8 %collective-permute-start.16 = (f32[144,128]{1,0:T(8,128)S(1)}, f32[144,128]{1,0:T(8,128)S(1)}, u32[]{:S(2)}, u32[]{:S(2)}) collective-permute-start(f32[144,128]{1,0:T(8,128)S(1)} %get-tuple-element.56), channel_id=1, source_target_pairs={{0,24},{2,26},{4,28},{6,30},{8,16},{10,18},{12,20},{14,22},{16,8},... | collective-permute-start | bytes 221192 | tf_op jit(solution)/shard_map/ppermute | solution.py:200
  86.2 0.6 collective-permute-start.14
  86.9 0.1 maximum_select_fusion.refs_1_.refs_2_
  87.0 1.9 %collective-permute-done.16 = f32[144,128]{1,0:T(8,128)S(1)} collective-permute-done((f32[144,128]{1,0:T(8,128)S(1)}, f32[144,128]{1,0:T(8,128)S(1)}, u32[]{:S(2)}, u32[]{:S(2)}) %collective-permute-start.16) | collective-permute-done | bytes 73760 | tf_op jit(solution)/shard_map/ppermute | solution.py:200
  88.8 2.6 %collective-permute-done.15 = f32[144,128]{1,0:T(8,128)S(1)} collective-permute-done((f32[144,128]{1,0:T(8,128)S(1)}, f32[144,128]{1,0:T(8,128)S(1)}, u32[]{:S(2)}, u32[]{:S(2)}) %collective-permute-start.15) | collective-permute-done | bytes 73760 | tf_op jit(solution)/shard_map/ppermute | solution.py:200
  91.5 0.4 collective-permute-done.14
  91.9 2.0 %collective-permute-start.25 = (f32[64,128]{1,0:T(8,128)S(1)}, f32[64,128]{1,0:T(8,128)S(1)}, u32[]{:S(2)}, u32[]{:S(2)}) collective-permute-start(f32[64,128]{1,0:T(8,128)S(1)} %get-tuple-element.59), channel_id=1, source_target_pairs={{0,24},{2,26},{4,28},{6,30},{8,16},{10,18},{12,20},{14,22},{16,8},... | collective-permute-start | bytes 98312 | tf_op jit(solution)/shard_map/ppermute | solution.py:200
  94.0 0.5 collective-permute-start.24
  94.4 2.0 %collective-permute-start.23 = (f32[64,128]{1,0:T(8,128)S(1)}, f32[64,128]{1,0:T(8,128)S(1)}, u32[]{:S(2)}, u32[]{:S(2)}) collective-permute-start(f32[64,128]{1,0:T(8,128)S(1)} %get-tuple-element.59), channel_id=1, source_target_pairs={{0,8},{2,10},{4,12},{6,14},{8,0},{10,2},{12,4},{14,6},{16,24},{18,... | collective-permute-start | bytes 98312 | tf_op jit(solution)/shard_map/ppermute | solution.py:200
  96.4 2.0 %collective-permute-start.19 = (f32[80,128]{1,0:T(8,128)S(1)}, f32[80,128]{1,0:T(8,128)S(1)}, u32[]{:S(2)}, u32[]{:S(2)}) collective-permute-start(f32[80,128]{1,0:T(8,128)S(1)} %get-tuple-element.61), channel_id=1, source_target_pairs={{0,24},{2,26},{4,28},{6,30},{8,16},{10,18},{12,20},{14,22},{16,8},... | collective-permute-start | bytes 122888 | tf_op jit(solution)/shard_map/ppermute | solution.py:200
  98.4 2.4 %collective-permute-start.17 = (f32[80,128]{1,0:T(8,128)S(1)}, f32[80,128]{1,0:T(8,128)S(1)}, u32[]{:S(2)}, u32[]{:S(2)}) collective-permute-start(f32[80,128]{1,0:T(8,128)S(1)} %get-tuple-element.61), channel_id=1, source_target_pairs={{0,8},{2,10},{4,12},{6,14},{8,0},{10,2},{12,4},{14,6},{16,24},{18,... | collective-permute-start | bytes 122888 | tf_op jit(solution)/shard_map/ppermute | solution.py:200
  100.9 1.4 collective-permute-start.26
  102.3 1.0 collective-permute-done.18
  103.3 1.4 collective-permute-start.20
  104.8 1.2 collective-permute-done.26
  106.1 1.6 %collective-permute-start.27 = (f32[512,128]{1,0:T(8,128)S(1)}, f32[512,128]{1,0:T(8,128)S(1)}, u32[]{:S(2)}, u32[]{:S(2)}) collective-permute-start(f32[512,128]{1,0:T(8,128)S(1)} %bitcast.66), channel_id=1, source_target_pairs={{0,1},{1,0},{2,3},{3,2},{4,5},{5,4},{6,7},{7,6},{8,9},{9,8},{10,11... | collective-permute-start | bytes 786440 | tf_op jit(solution)/shard_map/ppermute | solution.py:200
  107.7 1.1 collective-permute-done.20
  108.8 1.6 %collective-permute-start.21 = (f32[640,128]{1,0:T(8,128)S(1)}, f32[640,128]{1,0:T(8,128)S(1)}, u32[]{:S(2)}, u32[]{:S(2)}) collective-permute-start(f32[640,128]{1,0:T(8,128)S(1)} %bitcast.62), channel_id=1, source_target_pairs={{0,1},{1,0},{2,3},{3,2},{4,5},{5,4},{6,7},{7,6},{8,9},{9,8},{10,11... | collective-permute-start | bytes 983048 | tf_op jit(solution)/shard_map/ppermute | solution.py:200
  110.4 3.5 %collective-permute-done.27 = f32[512,128]{1,0:T(8,128)S(1)} collective-permute-done((f32[512,128]{1,0:T(8,128)S(1)}, f32[512,128]{1,0:T(8,128)S(1)}, u32[]{:S(2)}, u32[]{:S(2)}) %collective-permute-start.27) | collective-permute-done | bytes 262176 | tf_op jit(solution)/shard_map/ppermute | solution.py:200
  113.9 0.1 collective-permute-start.28
  114.1 3.3 %collective-permute-done.21 = f32[640,128]{1,0:T(8,128)S(1)} collective-permute-done((f32[640,128]{1,0:T(8,128)S(1)}, f32[640,128]{1,0:T(8,128)S(1)}, u32[]{:S(2)}, u32[]{:S(2)}) %collective-permute-start.21) | collective-permute-done | bytes 327712 | tf_op jit(solution)/shard_map/ppermute | solution.py:200
  117.5 0.1 collective-permute-start.22
  117.7 0.1 reverse_select_fusion.1.refs_1_
  117.8 1.9 %collective-permute-done.22 = f32[2,640,128]{2,1,0:T(8,128)S(1)} collective-permute-done((f32[2,640,128]{2,1,0:T(8,128)S(1)}, f32[2,640,128]{2,1,0:T(8,128)S(1)}, u32[]{:S(2)}, u32[]{:S(2)}) %collective-permute-start.22) | collective-permute-done | bytes 655392 | tf_op jit(solution)/shard_map/ppermute | solution.py:200
  119.6 0.1 pad_maximum_fusion
  119.7 0.1 reverse_select_fusion.refs_0_
  119.8 15.7 %shard_map.51 = (f32[192,512]{1,0:T(8,128)S(1)}, bf16[4,704,256]{2,1,0:T(8,128)(2,1)S(1)}, bf16[4,256,256]{2,1,0:T(8,128)(2,1)S(1)}) custom-call(f32[2,2,640,128]{3,2,1,0:T(8,128)S(1)} %reverse_select_fusion.refs_0_, f32[192,1024]{1,0:T(8,128)S(1)} %maximum_select_fusion.refs_1_.refs_2_), custom_call_target="tpu_custom_call" | custom-call | tf_op jit(solution)/shard_map/pallas_call | solution.py:435
  135.6 19.2 %shard_map.52 = f32[192,1024]{1,0:T(8,128)} custom-call(f32[2,2,640,128]{3,2,1,0:T(8,128)S(1)} %reverse_select_fusion.refs_0_, f32[2,2,512,128]{3,2,1,0:T(8,128)S(1)} %reverse_select_fusion.1.refs_1_, f32[192,1024]{1,0:T(8,128)S(1)} %maximum_select_fusion.refs_1_.refs_2_, f32[192,512]{1,0:T(8,128)S(1)} %get-tuple-element.52.refs_3_, ...), custom_call_target="tpu_custom_call" | custom-call | tf_op jit(solution)/shard_map/pallas_call | solution.py:441
  (54 shorter events, 1.1 us)
Async XLA Ops:
  0.0 9.8 %copy-start = (f32[384,512]{1,0:T(8,128)S(1)}, f32[384,512]{1,0:T(8,128)}, u32[]{:S(2)}) copy-start(f32[384,512]{1,0:T(8,128)} %refs_3_.1) | copy-start | bytes 2359300
  1.0 9.7 %collective-permute-start = (f32[128,512]{1,0:T(8,128)S(1)}, f32[128,512]{1,0:T(8,128)S(1)}, u32[]{:S(2)}, u32[]{:S(2)}) collective-permute-start(f32[128,512]{1,0:T(8,128)S(1)} %slice.36), channel_id=1, source_target_pairs={{2,0},{4,2},{6,4},{8,6},{10,8},{12,10},{14,12},{16,14},{18,16},{20... | collective-permute-start | bytes 786440 | tf_op jit(solution)/shard_map/ppermute | solution.py:116
  6.6 1.2 copy-start.1
  7.8 0.7 copy-start.2
  11.1 8.5 %collective-permute-start.1 = (f32[128,512]{1,0:T(8,128)S(1)}, f32[128,512]{1,0:T(8,128)S(1)}, u32[]{:S(2)}, u32[]{:S(2)}) collective-permute-start(f32[128,512]{1,0:T(8,128)S(1)} %get-tuple-element.34), channel_id=1, source_target_pairs={{30,0},{0,2},{2,4},{4,6},{6,8},{8,10},{10,12},{12,14},{14,16},{16,... | collective-permute-start | bytes 786440 | tf_op jit(solution)/shard_map/ppermute | solution.py:116
  11.2 8.5 %collective-permute-start.2 = (f32[128,512]{1,0:T(8,128)S(1)}, f32[128,512]{1,0:T(8,128)S(1)}, u32[]{:S(2)}, u32[]{:S(2)}) collective-permute-start(f32[128,512]{1,0:T(8,128)S(1)} %get-tuple-element.35), channel_id=1, source_target_pairs={{2,0},{4,2},{6,4},{8,6},{10,8},{12,10},{14,12},{16,14},{18,16},{20... | collective-permute-start | bytes 786440 | tf_op jit(solution)/shard_map/ppermute | solution.py:116
  20.1 8.8 %collective-permute-start.3 = (f32[128,512]{1,0:T(8,128)S(1)}, f32[128,512]{1,0:T(8,128)S(1)}, u32[]{:S(2)}, u32[]{:S(2)}) collective-permute-start(f32[128,512]{1,0:T(8,128)S(1)} %get-tuple-element.39), channel_id=1, source_target_pairs={{30,0},{0,2},{2,4},{4,6},{6,8},{8,10},{10,12},{12,14},{14,16},{16,... | collective-permute-start | bytes 786440 | tf_op jit(solution)/shard_map/ppermute | solution.py:116
  20.1 8.7 %collective-permute-start.4 = (f32[128,512]{1,0:T(8,128)S(1)}, f32[128,512]{1,0:T(8,128)S(1)}, u32[]{:S(2)}, u32[]{:S(2)}) collective-permute-start(f32[128,512]{1,0:T(8,128)S(1)} %get-tuple-element.40), channel_id=1, source_target_pairs={{2,0},{4,2},{6,4},{8,6},{10,8},{12,10},{14,12},{16,14},{18,16},{20... | collective-permute-start | bytes 786440 | tf_op jit(solution)/shard_map/ppermute | solution.py:116
  29.2 8.7 %collective-permute-start.5 = (f32[128,512]{1,0:T(8,128)S(1)}, f32[128,512]{1,0:T(8,128)S(1)}, u32[]{:S(2)}, u32[]{:S(2)}) collective-permute-start(f32[128,512]{1,0:T(8,128)S(1)} %get-tuple-element.44), channel_id=1, source_target_pairs={{30,0},{0,2},{2,4},{4,6},{6,8},{8,10},{10,12},{12,14},{14,16},{16,... | collective-permute-start | bytes 786440 | tf_op jit(solution)/shard_map/ppermute | solution.py:116
  29.3 8.6 %collective-permute-start.6 = (f32[128,512]{1,0:T(8,128)S(1)}, f32[128,512]{1,0:T(8,128)S(1)}, u32[]{:S(2)}, u32[]{:S(2)}) collective-permute-start(f32[128,512]{1,0:T(8,128)S(1)} %get-tuple-element.45), channel_id=1, source_target_pairs={{2,0},{4,2},{6,4},{8,6},{10,8},{12,10},{14,12},{16,14},{18,16},{20... | collective-permute-start | bytes 786440 | tf_op jit(solution)/shard_map/ppermute | solution.py:116
  38.3 8.6 %collective-permute-start.7 = (f32[128,512]{1,0:T(8,128)S(1)}, f32[128,512]{1,0:T(8,128)S(1)}, u32[]{:S(2)}, u32[]{:S(2)}) collective-permute-start(f32[128,512]{1,0:T(8,128)S(1)} %get-tuple-element.49), channel_id=1, source_target_pairs={{30,0},{0,2},{2,4},{4,6},{6,8},{8,10},{10,12},{12,14},{14,16},{16,... | collective-permute-start | bytes 786440 | tf_op jit(solution)/shard_map/ppermute | solution.py:116
  38.4 8.5 %collective-permute-start.8 = (f32[128,512]{1,0:T(8,128)S(1)}, f32[128,512]{1,0:T(8,128)S(1)}, u32[]{:S(2)}, u32[]{:S(2)}) collective-permute-start(f32[128,512]{1,0:T(8,128)S(1)} %get-tuple-element.50), channel_id=1, source_target_pairs={{2,0},{4,2},{6,4},{8,6},{10,8},{12,10},{14,12},{16,14},{18,16},{20... | collective-permute-start | bytes 786440 | tf_op jit(solution)/shard_map/ppermute | solution.py:116
  47.2 8.6 %collective-permute-start.9 = (f32[128,512]{1,0:T(8,128)S(1)}, f32[128,512]{1,0:T(8,128)S(1)}, u32[]{:S(2)}, u32[]{:S(2)}) collective-permute-start(f32[128,512]{1,0:T(8,128)S(1)} %shard_map.48), channel_id=1, source_target_pairs={{30,0},{0,2},{2,4},{4,6},{6,8},{8,10},{10,12},{12,14},{14,16},{16,... | collective-permute-start | bytes 786440 | tf_op jit(solution)/shard_map/ppermute | solution.py:116
  47.9 12.1 %collective-permute-start.11 = (f32[256,512]{1,0:T(8,128)S(1)}, f32[256,512]{1,0:T(8,128)S(1)}, u32[]{:S(2)}, u32[]{:S(2)}) collective-permute-start(f32[256,512]{1,0:T(8,128)S(1)} %slice.46), channel_id=1, source_target_pairs={{0,1},{1,0},{2,3},{3,2},{4,5},{5,4},{6,7},{7,6},{8,9},{9,8},{10,11... | collective-permute-start | bytes 1572872 | tf_op jit(solution)/shard_map/ppermute | solution.py:200
  55.9 5.4 %copy-start.3 = (f32[128,512]{1,0:T(8,128)}, f32[128,512]{1,0:T(8,128)S(1)}, u32[]{:S(2)}) copy-start(f32[128,512]{1,0:T(8,128)S(1)} %slice_add_fusion) | copy-start | bytes 786436
  55.9 6.9 %collective-permute-start.10 = (f32[128,512]{1,0:T(8,128)S(1)}, f32[128,512]{1,0:T(8,128)S(1)}, u32[]{:S(2)}, u32[]{:S(2)}) collective-permute-start(f32[128,512]{1,0:T(8,128)S(1)} %slice_add_fusion), channel_id=1, source_target_pairs={{0,1},{1,0},{2,3},{3,2},{4,5},{5,4},{6,7},{7,6},{8,9},{9,8},{10,11... | collective-permute-start | bytes 786440 | tf_op jit(solution)/shard_map/ppermute | solution.py:200
  64.7 3.6 %copy-start.4 = (f32[128,512]{1,0:T(8,128)S(1)}, f32[128,512]{1,0:T(8,128)}, u32[]{:S(2)}) copy-start(f32[128,512]{1,0:T(8,128)} %copy-done.3) | copy-start | bytes 786436
  64.7 2.3 %collective-permute-start.12 = (f32[1152,128]{1,0:T(8,128)}, f32[1152,128]{1,0:T(8,128)}, u32[]{:S(2)}, u32[]{:S(2)}) collective-permute-start(f32[1152,128]{1,0:T(8,128)} %dynamic-slice_bitcast_fusion), channel_id=1, source_target_pairs={{0,2},{2,0},{4,6},{6,4},{8,10},{10,8},{12,14},{14,12},{16,18},{18,... | collective-permute-start | bytes 1769480 | tf_op jit(solution)/shard_map/ppermute | solution.py:200
  68.3 9.1 %collective-permute-start.13 = (f32[576,128]{1,0:T(8,128)S(1)}, f32[576,128]{1,0:T(8,128)S(1)}, u32[]{:S(2)}, u32[]{:S(2)}) collective-permute-start(f32[576,128]{1,0:T(8,128)S(1)} %dynamic-slice_bitcast_fusion.1), channel_id=1, source_target_pairs={{0,4},{2,6},{4,0},{6,2},{8,12},{10,14},{12,8},{14,10},{16,20},{18,... | collective-permute-start | bytes 884744 | tf_op jit(solution)/shard_map/ppermute | solution.py:200
  77.4 11.4 %collective-permute-start.16 = (f32[144,128]{1,0:T(8,128)S(1)}, f32[144,128]{1,0:T(8,128)S(1)}, u32[]{:S(2)}, u32[]{:S(2)}) collective-permute-start(f32[144,128]{1,0:T(8,128)S(1)} %get-tuple-element.56), channel_id=1, source_target_pairs={{0,24},{2,26},{4,28},{6,30},{8,16},{10,18},{12,20},{14,22},{16,8},... | collective-permute-start | bytes 221192 | tf_op jit(solution)/shard_map/ppermute | solution.py:200
  86.2 5.3 %collective-permute-start.15 = (f32[144,128]{1,0:T(8,128)S(1)}, f32[144,128]{1,0:T(8,128)S(1)}, u32[]{:S(2)}, u32[]{:S(2)}) collective-permute-start(f32[144,128]{1,0:T(8,128)S(1)} %get-tuple-element.57), channel_id=1, source_target_pairs={{0,16},{2,18},{4,20},{6,22},{8,24},{10,26},{12,28},{14,30},{16,0},... | collective-permute-start | bytes 221192 | tf_op jit(solution)/shard_map/ppermute | solution.py:200
  86.2 5.7 %collective-permute-start.14 = (f32[144,128]{1,0:T(8,128)S(1)}, f32[144,128]{1,0:T(8,128)S(1)}, u32[]{:S(2)}, u32[]{:S(2)}) collective-permute-start(f32[144,128]{1,0:T(8,128)S(1)} %get-tuple-element.55), channel_id=1, source_target_pairs={{0,8},{2,10},{4,12},{6,14},{8,0},{10,2},{12,4},{14,6},{16,24},{18,... | collective-permute-start | bytes 221192 | tf_op jit(solution)/shard_map/ppermute | solution.py:200
  91.9 6.4 %collective-permute-start.25 = (f32[64,128]{1,0:T(8,128)S(1)}, f32[64,128]{1,0:T(8,128)S(1)}, u32[]{:S(2)}, u32[]{:S(2)}) collective-permute-start(f32[64,128]{1,0:T(8,128)S(1)} %get-tuple-element.59), channel_id=1, source_target_pairs={{0,24},{2,26},{4,28},{6,30},{8,16},{10,18},{12,20},{14,22},{16,8},... | collective-permute-start | bytes 98312 | tf_op jit(solution)/shard_map/ppermute | solution.py:200
  94.0 6.8 %collective-permute-start.24 = (f32[64,128]{1,0:T(8,128)S(1)}, f32[64,128]{1,0:T(8,128)S(1)}, u32[]{:S(2)}, u32[]{:S(2)}) collective-permute-start(f32[64,128]{1,0:T(8,128)S(1)} %get-tuple-element.59), channel_id=1, source_target_pairs={{0,16},{2,18},{4,20},{6,22},{8,24},{10,26},{12,28},{14,30},{16,0},... | collective-permute-start | bytes 98312 | tf_op jit(solution)/shard_map/ppermute | solution.py:200
  94.4 6.4 %collective-permute-start.23 = (f32[64,128]{1,0:T(8,128)S(1)}, f32[64,128]{1,0:T(8,128)S(1)}, u32[]{:S(2)}, u32[]{:S(2)}) collective-permute-start(f32[64,128]{1,0:T(8,128)S(1)} %get-tuple-element.59), channel_id=1, source_target_pairs={{0,8},{2,10},{4,12},{6,14},{8,0},{10,2},{12,4},{14,6},{16,24},{18,... | collective-permute-start | bytes 98312 | tf_op jit(solution)/shard_map/ppermute | solution.py:200
  96.4 5.9 %collective-permute-start.19 = (f32[80,128]{1,0:T(8,128)S(1)}, f32[80,128]{1,0:T(8,128)S(1)}, u32[]{:S(2)}, u32[]{:S(2)}) collective-permute-start(f32[80,128]{1,0:T(8,128)S(1)} %get-tuple-element.61), channel_id=1, source_target_pairs={{0,24},{2,26},{4,28},{6,30},{8,16},{10,18},{12,20},{14,22},{16,8},... | collective-permute-start | bytes 122888 | tf_op jit(solution)/shard_map/ppermute | solution.py:200
  98.4 4.9 %collective-permute-start.18 = (f32[80,128]{1,0:T(8,128)S(1)}, f32[80,128]{1,0:T(8,128)S(1)}, u32[]{:S(2)}, u32[]{:S(2)}) collective-permute-start(f32[80,128]{1,0:T(8,128)S(1)} %get-tuple-element.61), channel_id=1, source_target_pairs={{0,16},{2,18},{4,20},{6,22},{8,24},{10,26},{12,28},{14,30},{16,0},... | collective-permute-start | bytes 122888 | tf_op jit(solution)/shard_map/ppermute | solution.py:200
  98.4 4.9 %collective-permute-start.17 = (f32[80,128]{1,0:T(8,128)S(1)}, f32[80,128]{1,0:T(8,128)S(1)}, u32[]{:S(2)}, u32[]{:S(2)}) collective-permute-start(f32[80,128]{1,0:T(8,128)S(1)} %get-tuple-element.61), channel_id=1, source_target_pairs={{0,8},{2,10},{4,12},{6,14},{8,0},{10,2},{12,4},{14,6},{16,24},{18,... | collective-permute-start | bytes 122888 | tf_op jit(solution)/shard_map/ppermute | solution.py:200
  100.9 5.1 %collective-permute-start.26 = (f32[256,128]{1,0:T(8,128)S(1)}, f32[256,128]{1,0:T(8,128)S(1)}, u32[]{:S(2)}, u32[]{:S(2)}) collective-permute-start(f32[256,128]{1,0:T(8,128)S(1)} %bitcast.73), channel_id=1, source_target_pairs={{0,4},{2,6},{4,0},{6,2},{8,12},{10,14},{12,8},{14,10},{16,20},{18,... | collective-permute-start | bytes 393224 | tf_op jit(solution)/shard_map/ppermute | solution.py:200
  103.3 5.4 %collective-permute-start.20 = (f32[320,128]{1,0:T(8,128)S(1)}, f32[320,128]{1,0:T(8,128)S(1)}, u32[]{:S(2)}, u32[]{:S(2)}) collective-permute-start(f32[320,128]{1,0:T(8,128)S(1)} %bitcast.69), channel_id=1, source_target_pairs={{0,4},{2,6},{4,0},{6,2},{8,12},{10,14},{12,8},{14,10},{16,20},{18,... | collective-permute-start | bytes 491528 | tf_op jit(solution)/shard_map/ppermute | solution.py:200
  106.1 7.8 %collective-permute-start.27 = (f32[512,128]{1,0:T(8,128)S(1)}, f32[512,128]{1,0:T(8,128)S(1)}, u32[]{:S(2)}, u32[]{:S(2)}) collective-permute-start(f32[512,128]{1,0:T(8,128)S(1)} %bitcast.66), channel_id=1, source_target_pairs={{0,1},{1,0},{2,3},{3,2},{4,5},{5,4},{6,7},{7,6},{8,9},{9,8},{10,11... | collective-permute-start | bytes 786440 | tf_op jit(solution)/shard_map/ppermute | solution.py:200
  108.8 8.6 %collective-permute-start.21 = (f32[640,128]{1,0:T(8,128)S(1)}, f32[640,128]{1,0:T(8,128)S(1)}, u32[]{:S(2)}, u32[]{:S(2)}) collective-permute-start(f32[640,128]{1,0:T(8,128)S(1)} %bitcast.62), channel_id=1, source_target_pairs={{0,1},{1,0},{2,3},{3,2},{4,5},{5,4},{6,7},{7,6},{8,9},{9,8},{10,11... | collective-permute-start | bytes 983048 | tf_op jit(solution)/shard_map/ppermute | solution.py:200
  113.9 3.7 %collective-permute-start.28 = (f32[2,512,128]{2,1,0:T(8,128)S(1)}, f32[2,512,128]{2,1,0:T(8,128)S(1)}, u32[]{:S(2)}, u32[]{:S(2)}) collective-permute-start(f32[2,512,128]{2,1,0:T(8,128)S(1)} %reverse_select_fusion.3), channel_id=1, source_target_pairs={{0,2},{2,0},{4,6},{6,4},{8,10},{10,8},{12,14},{14,12},{16,18},{18,... | collective-permute-start | bytes 1572872 | tf_op jit(solution)/shard_map/ppermute | solution.py:200
  117.5 2.2 %collective-permute-start.22 = (f32[2,640,128]{2,1,0:T(8,128)S(1)}, f32[2,640,128]{2,1,0:T(8,128)S(1)}, u32[]{:S(2)}, u32[]{:S(2)}) collective-permute-start(f32[2,640,128]{2,1,0:T(8,128)S(1)} %reverse_select_fusion.2), channel_id=1, source_target_pairs={{0,2},{2,0},{4,6},{6,4},{8,10},{10,8},{12,14},{14,12},{16,18},{18,... | collective-permute-start | bytes 1966088 | tf_op jit(solution)/shard_map/ppermute | solution.py:200

commit v5 on v4

--- a/solution.py
+++ b/solution.py
@@ -255,45 +255,58 @@
     def down(v, k):
         return jnp.broadcast_to(v[k : k + 1], shape)
 
-    cols, below, ahead = across(rows[0], 0), across(rows[1], 0), across(rows[1], SUB)
-    for b in range(count):
-        at = b * SUB
-        more = b + 1 < count
-        raw = list(below)
-        here = (lane >= at) & (lane < at + SUB)
-        top = jnp.where(here, jnp.where(lane - at == sub, 1.0, 0.0), rows[b])
-        scale = jnp.zeros(shape, F32)
-        done = jnp.zeros(shape, F32)
-        pivot = down(cols[0], 0)
-        for k in range(SUB):
-            inverse = 1.0 / pivot
-            row = down(top, k)
-            done = jnp.where(sub == k, row * lax.rsqrt(pivot), done)
-            scale = jnp.where(sub == k, inverse, scale)
-            heads = [down(cols[m], k) for m in range(k + 1, SUB)]
-            if heads:
-                pivot = down(cols[k + 1], k + 1) - (heads[0] * inverse) * heads[0]
-            ratio = jnp.where(sub == k, 0.0, cols[k] * inverse)
-            top = top - ratio * row
-            part = below[k] * inverse
-            for m, head in enumerate(heads, k + 1):
-                cols[m] = cols[m] - ratio * head
+    for start in range(0, count, count // 2):
+        stop, at = start + count // 2, start * SUB
+        cols, below = across(rows[start], at), across(rows[start + 1], at)
+        ahead = across(rows[start + 1], at + SUB)
+        near = []
+        for b in range(start, stop):
+            at = b * SUB
+            more = b + 1 < stop
+            raw = list(below)
+            here = (lane >= at) & (lane < at + SUB)
+            top = jnp.where(here, jnp.where(lane - at == sub, 1.0, 0.0), rows[b])
+            scale = jnp.zeros(shape, F32)
+            done = jnp.zeros(shape, F32)
+            pivot = down(cols[0], 0)
+            for k in range(SUB):
+                inverse = 1.0 / pivot
+                row = down(top, k)
+                done = jnp.where(sub == k, row * lax.rsqrt(pivot), done)
+                scale = jnp.where(sub == k, inverse, scale)
+                heads = [down(cols[m], k) for m in range(k + 1, SUB)]
+                if heads:
+                    pivot = down(cols[k + 1], k + 1) - (heads[0] * inverse) * heads[0]
+                ratio = jnp.where(sub == k, 0.0, cols[k] * inverse)
+                top = top - ratio * row
+                part = below[k] * inverse
+                for m, head in enumerate(heads, k + 1):
+                    cols[m] = cols[m] - ratio * head
+                    if more:
+                        below[m] = below[m] - part * head
                 if more:
-                    below[m] = below[m] - part * head
-            if more:
-                for j in range(SUB):
-                    ahead[j] = ahead[j] - part * down(below[k], j)
-        out_ref[at : at + SUB, :] = jnp.where(lane < at + SUB, done, 0.0)
-        top = top * scale
-        spread = [down(top, k) for k in range(SUB)]
-        for t in range(b + 1, count):
-            kept = jnp.where(here, 0.0, rows[t])
-            for k, column in enumerate(raw if t == b + 1 else across(rows[t], at)):
-                kept = kept - column * spread[k]
-            rows[t] = kept
-        cols = ahead
-        if b + 2 < count:
-            below, ahead = across(rows[b + 2], at + SUB), across(rows[b + 2], at + 2 * SUB)
+                    for j in range(SUB):
+                        ahead[j] = ahead[j] - part * down(below[k], j)
+            factor = jnp.where(lane < at + SUB, done, 0.0)
+            out_ref[at : at + SUB, :] = factor
+            near.append(jnp.where(lane < stop * SUB, factor, done))
+            if not more:
+                continue
+            top = top * scale
+            spread = [down(top, k) for k in range(SUB)]
+            for t in range(b + 1, stop):
+                kept = jnp.where(here, 0.0, rows[t])
+                for k, column in enumerate(raw if t == b + 1 else across(rows[t], at)):
+                    kept = kept - column * spread[k]
+                rows[t] = kept
+            cols = ahead
+            if b + 2 < stop:
+                below, ahead = across(rows[b + 2], at + SUB), across(rows[b + 2], at + 2 * SUB)
+        if stop < count:
+            pair = split(jnp.concatenate(near, axis=0))
+            drop = product(pair, pair, ((0,), (0,)))
+            for t in range(stop, count):
+                rows[t] = jnp.where(lane < stop * SUB, 0.0, rows[t]) - drop[t * SUB : (t + 1) * SUB]
 
 
 def pair_of(v):

time: 155 us -> 151 us (0.974)
  Pallas kernels: 48.1 us -> 44 us
    pallas_call x1, Pallas kernels: 19.2 us -> 17.1 us  [factor_halves(): kernel_call(lambda *refs: second_kernel(scale, *refs), f32(count, width),...]
    pallas_call x1, Pallas kernels: 15.7 us -> 13.7 us  [factor_halves(): kernel_call(lambda *refs: first_kernel(scale, *refs), [f32(count, size),...]
where the time goes in v5:
time: 151 us
  starting transfers between devices  51.7 us (34%)
  waiting for transfers between devices  48.5 us (32%)
  Pallas kernels  44 us (29%)
  local copies, waits for them, and re-layouts  3.92 us (3%)
  other arithmetic  2.15 us (1%)
    ppermute x19, waiting for transfers between devices, exchanged(): return lax.ppermute(block, axis, route)  32 us
    ppermute x19, starting transfers between devices, exchanged(): return lax.ppermute(block, axis, route)  27.7 us
    ppermute x10, starting transfers between devices, shifted(): return lax.ppermute(block, axis, route)  24 us
    pallas_call x1, Pallas kernels, factor_halves(): kernel_call(lambda *refs: second_kernel(scale, *refs), f32(count, width),...  17.1 us
    ppermute x10, waiting for transfers between devices, shifted(): return lax.ppermute(block, axis, route)  16.4 us
    pallas_call x1, Pallas kernels, factor_halves(): kernel_call(lambda *refs: first_kernel(scale, *refs), [f32(count, size),...  13.7 us
    pallas_call x5, Pallas kernels, filtered_columns(): got = kernel_call(rest, outs)(*matrix, applied, vec, *arrived, *before)  6.67 us
  transfers between devices with their start and end apart: 29, of which 18 were waited for; matrix products, arithmetic and copies ran while one was open for 1% of the time, Pallas kernels for 7%

profile of v5, /device:TPU:0, one launch (start us, length us, event | category | flops | bytes accessed | tf_op | source)
XLA Modules:
  0.0 150.7 jit_solution(6204091394735345512)
XLA Ops:
  0.0 1.0 slice.36
  1.0 5.5 %collective-permute-start = (f32[128,512]{1,0:T(8,128)S(1)}, f32[128,512]{1,0:T(8,128)S(1)}, u32[]{:S(2)}, u32[]{:S(2)}) collective-permute-start(f32[128,512]{1,0:T(8,128)S(1)} %slice.36), channel_id=1, source_target_pairs={{2,0},{4,2},{6,4},{8,6},{10,8},{12,10},{14,12},{16,14},{18,16},{20... | collective-permute-start | bytes 786440 | tf_op jit(solution)/shard_map/ppermute | solution.py:116
  6.6 1.2 copy-done.1
  7.8 0.7 copy-done.2
  8.5 1.3 shard_map.37
  9.8 1.0 shard_map.38.refs_2_
  10.8 0.4 shard_map.40
  11.2 4.5 %collective-permute-start.2 = (f32[128,512]{1,0:T(8,128)S(1)}, f32[128,512]{1,0:T(8,128)S(1)}, u32[]{:S(2)}, u32[]{:S(2)}) collective-permute-start(f32[128,512]{1,0:T(8,128)S(1)} %get-tuple-element.35), channel_id=1, source_target_pairs={{2,0},{4,2},{6,4},{8,6},{10,8},{12,10},{14,12},{16,14},{18,16},{20... | collective-permute-start | bytes 786440 | tf_op jit(solution)/shard_map/ppermute | solution.py:116
  15.6 1.5 %shard_map.39 = (f32[512,512]{1,0:T(8,128)S(1)}, f32[512,512]{1,0:T(8,128)S(1)}, f32[512,512]{1,0:T(8,128)S(1)}) custom-call(bf16[512,512]{1,0:T(8,128)(2,1)S(1)} %get-tuple-element.30.hi_ref.refs_0_, bf16[512,512]{1,0:T(8,128)(2,1)S(1)} %get-tuple-element.31.lo_ref.refs_1_, f32[512,512]{1,0:T(8,128)S(1)} %shard_map.38.refs_2_, f32[384,512]{1,0:T(8,128)S(1)} %copy-done, ...), custom_call_target="tpu_custom_call" | custom-call | tf_op jit(solution)/shard_map/pallas_call | solution.py:135
  17.2 2.5 %collective-permute-done.1.refs_4_.refs_3_ = f32[128,512]{1,0:T(8,128)S(1)} collective-permute-done((f32[128,512]{1,0:T(8,128)S(1)}, f32[128,512]{1,0:T(8,128)S(1)}, u32[]{:S(2)}, u32[]{:S(2)}) %collective-permute-start.1) | collective-permute-done | bytes 262176 | tf_op jit(solution)/shard_map/ppermute | solution.py:116
  19.7 0.4 shard_map.42
  20.1 4.6 %collective-permute-start.4 = (f32[128,512]{1,0:T(8,128)S(1)}, f32[128,512]{1,0:T(8,128)S(1)}, u32[]{:S(2)}, u32[]{:S(2)}) collective-permute-start(f32[128,512]{1,0:T(8,128)S(1)} %get-tuple-element.40), channel_id=1, source_target_pairs={{2,0},{4,2},{6,4},{8,6},{10,8},{12,10},{14,12},{16,14},{18,16},{20... | collective-permute-start | bytes 786440 | tf_op jit(solution)/shard_map/ppermute | solution.py:116
  24.7 1.5 %shard_map.41 = (f32[512,512]{1,0:T(8,128)S(1)}, f32[512,512]{1,0:T(8,128)S(1)}, f32[512,512]{1,0:T(8,128)S(1)}) custom-call(bf16[512,512]{1,0:T(8,128)(2,1)S(1)} %get-tuple-element.30.hi_ref.refs_0_, bf16[512,512]{1,0:T(8,128)(2,1)S(1)} %get-tuple-element.31.lo_ref.refs_1_, f32[512,512]{1,0:T(8,128)S(1)} %get-tuple-element.32.refs_2_, ...), custom_call_target="tpu_custom_call" | custom-call | tf_op jit(solution)/shard_map/pallas_call | solution.py:135
  26.3 2.5 %collective-permute-done.3.refs_4_.refs_3_ = f32[128,512]{1,0:T(8,128)S(1)} collective-permute-done((f32[128,512]{1,0:T(8,128)S(1)}, f32[128,512]{1,0:T(8,128)S(1)}, u32[]{:S(2)}, u32[]{:S(2)}) %collective-permute-start.3) | collective-permute-done | bytes 262176 | tf_op jit(solution)/shard_map/ppermute | solution.py:116
  28.8 0.4 shard_map.44
  29.3 4.6 %collective-permute-start.6 = (f32[128,512]{1,0:T(8,128)S(1)}, f32[128,512]{1,0:T(8,128)S(1)}, u32[]{:S(2)}, u32[]{:S(2)}) collective-permute-start(f32[128,512]{1,0:T(8,128)S(1)} %get-tuple-element.45), channel_id=1, source_target_pairs={{2,0},{4,2},{6,4},{8,6},{10,8},{12,10},{14,12},{16,14},{18,16},{20... | collective-permute-start | bytes 786440 | tf_op jit(solution)/shard_map/ppermute | solution.py:116
  33.9 1.5 %shard_map.43 = (f32[512,512]{1,0:T(8,128)S(1)}, f32[512,512]{1,0:T(8,128)S(1)}, f32[512,512]{1,0:T(8,128)S(1)}) custom-call(bf16[512,512]{1,0:T(8,128)(2,1)S(1)} %get-tuple-element.30.hi_ref.refs_0_, bf16[512,512]{1,0:T(8,128)(2,1)S(1)} %get-tuple-element.31.lo_ref.refs_1_, f32[512,512]{1,0:T(8,128)S(1)} %get-tuple-element.37.refs_2_, ...), custom_call_target="tpu_custom_call" | custom-call | tf_op jit(solution)/shard_map/pallas_call | solution.py:135
  35.4 2.5 %collective-permute-done.5.refs_4_.refs_3_ = f32[128,512]{1,0:T(8,128)S(1)} collective-permute-done((f32[128,512]{1,0:T(8,128)S(1)}, f32[128,512]{1,0:T(8,128)S(1)}, u32[]{:S(2)}, u32[]{:S(2)}) %collective-permute-start.5) | collective-permute-done | bytes 262176 | tf_op jit(solution)/shard_map/ppermute | solution.py:116
  37.9 0.4 shard_map.46
  38.4 4.6 %collective-permute-start.8 = (f32[128,512]{1,0:T(8,128)S(1)}, f32[128,512]{1,0:T(8,128)S(1)}, u32[]{:S(2)}, u32[]{:S(2)}) collective-permute-start(f32[128,512]{1,0:T(8,128)S(1)} %get-tuple-element.50), channel_id=1, source_target_pairs={{2,0},{4,2},{6,4},{8,6},{10,8},{12,10},{14,12},{16,14},{18,16},{20... | collective-permute-start | bytes 786440 | tf_op jit(solution)/shard_map/ppermute | solution.py:116
  43.0 1.5 %shard_map.45 = (f32[512,512]{1,0:T(8,128)S(1)}, f32[512,512]{1,0:T(8,128)S(1)}, f32[512,512]{1,0:T(8,128)S(1)}) custom-call(bf16[512,512]{1,0:T(8,128)(2,1)S(1)} %get-tuple-element.30.hi_ref.refs_0_, bf16[512,512]{1,0:T(8,128)(2,1)S(1)} %get-tuple-element.31.lo_ref.refs_1_, f32[512,512]{1,0:T(8,128)S(1)} %get-tuple-element.42.refs_2_, ...), custom_call_target="tpu_custom_call" | custom-call | tf_op jit(solution)/shard_map/pallas_call | solution.py:135
  44.5 2.4 %collective-permute-done.7.refs_4_.refs_3_ = f32[128,512]{1,0:T(8,128)S(1)} collective-permute-done((f32[128,512]{1,0:T(8,128)S(1)}, f32[128,512]{1,0:T(8,128)S(1)}, u32[]{:S(2)}, u32[]{:S(2)}) %collective-permute-start.7) | collective-permute-done | bytes 262176 | tf_op jit(solution)/shard_map/ppermute | solution.py:116
  46.9 0.3 shard_map.48
  47.3 0.5 shard_map.47.refs_1_
  47.9 1.6 %collective-permute-start.11 = (f32[256,512]{1,0:T(8,128)S(1)}, f32[256,512]{1,0:T(8,128)S(1)}, u32[]{:S(2)}, u32[]{:S(2)}) collective-permute-start(f32[256,512]{1,0:T(8,128)S(1)} %slice.46), channel_id=1, source_target_pairs={{0,1},{1,0},{2,3},{3,2},{4,5},{5,4},{6,7},{7,6},{8,9},{9,8},{10,11... | collective-permute-start | bytes 1572872 | tf_op jit(solution)/shard_map/ppermute | solution.py:200
  49.5 6.4 %collective-permute-done.9.refs_2_ = f32[128,512]{1,0:T(8,128)S(1)} collective-permute-done((f32[128,512]{1,0:T(8,128)S(1)}, f32[128,512]{1,0:T(8,128)S(1)}, u32[]{:S(2)}, u32[]{:S(2)}) %collective-permute-start.9) | collective-permute-done | bytes 262176 | tf_op jit(solution)/shard_map/ppermute | solution.py:116
  55.9 1.6 %collective-permute-start.10 = (f32[128,512]{1,0:T(8,128)S(1)}, f32[128,512]{1,0:T(8,128)S(1)}, u32[]{:S(2)}, u32[]{:S(2)}) collective-permute-start(f32[128,512]{1,0:T(8,128)S(1)} %slice_add_fusion), channel_id=1, source_target_pairs={{0,1},{1,0},{2,3},{3,2},{4,5},{5,4},{6,7},{7,6},{8,9},{9,8},{10,11... | collective-permute-start | bytes 786440 | tf_op jit(solution)/shard_map/ppermute | solution.py:200
  57.5 2.5 %collective-permute-done.11.refs_2_ = f32[256,512]{1,0:T(8,128)S(1)} collective-permute-done((f32[256,512]{1,0:T(8,128)S(1)}, f32[256,512]{1,0:T(8,128)S(1)}, u32[]{:S(2)}, u32[]{:S(2)}) %collective-permute-start.11) | collective-permute-done | bytes 524320 | tf_op jit(solution)/shard_map/ppermute | solution.py:200
  60.0 1.3 shard_map.49.refs_4_
  61.3 1.4 collective-permute-done.10.refs_3_
  62.8 1.1 shard_map.50
  63.9 0.9 dynamic-slice_bitcast_fusion
  64.8 2.3 %collective-permute-done.12 = f32[1152,128]{1,0:T(8,128)} collective-permute-done((f32[1152,128]{1,0:T(8,128)}, f32[1152,128]{1,0:T(8,128)}, u32[]{:S(2)}, u32[]{:S(2)}) %collective-permute-start.12) | collective-permute-done | bytes 589856 | tf_op jit(solution)/shard_map/ppermute | solution.py:200
  67.1 1.1 bitcast_add_fusion
  68.3 0.1 collective-permute-start.13
  68.5 8.9 %collective-permute-done.13 = f32[576,128]{1,0:T(8,128)S(1)} collective-permute-done((f32[576,128]{1,0:T(8,128)S(1)}, f32[576,128]{1,0:T(8,128)S(1)}, u32[]{:S(2)}, u32[]{:S(2)}) %collective-permute-start.13) | collective-permute-done | bytes 294944 | tf_op jit(solution)/shard_map/ppermute | solution.py:200
  77.4 8.8 %collective-permute-start.16 = (f32[144,128]{1,0:T(8,128)S(1)}, f32[144,128]{1,0:T(8,128)S(1)}, u32[]{:S(2)}, u32[]{:S(2)}) collective-permute-start(f32[144,128]{1,0:T(8,128)S(1)} %get-tuple-element.56), channel_id=1, source_target_pairs={{0,24},{2,26},{4,28},{6,30},{8,16},{10,18},{12,20},{14,22},{16,8},... | collective-permute-start | bytes 221192 | tf_op jit(solution)/shard_map/ppermute | solution.py:200
  86.2 0.6 collective-permute-start.14
  86.9 0.1 maximum_select_fusion.refs_1_.refs_2_
  87.0 1.9 %collective-permute-done.16 = f32[144,128]{1,0:T(8,128)S(1)} collective-permute-done((f32[144,128]{1,0:T(8,128)S(1)}, f32[144,128]{1,0:T(8,128)S(1)}, u32[]{:S(2)}, u32[]{:S(2)}) %collective-permute-start.16) | collective-permute-done | bytes 73760 | tf_op jit(solution)/shard_map/ppermute | solution.py:200
  88.8 2.6 %collective-permute-done.15 = f32[144,128]{1,0:T(8,128)S(1)} collective-permute-done((f32[144,128]{1,0:T(8,128)S(1)}, f32[144,128]{1,0:T(8,128)S(1)}, u32[]{:S(2)}, u32[]{:S(2)}) %collective-permute-start.15) | collective-permute-done | bytes 73760 | tf_op jit(solution)/shard_map/ppermute | solution.py:200
  91.5 0.4 collective-permute-done.14
  91.9 2.0 %collective-permute-start.25 = (f32[64,128]{1,0:T(8,128)S(1)}, f32[64,128]{1,0:T(8,128)S(1)}, u32[]{:S(2)}, u32[]{:S(2)}) collective-permute-start(f32[64,128]{1,0:T(8,128)S(1)} %get-tuple-element.59), channel_id=1, source_target_pairs={{0,24},{2,26},{4,28},{6,30},{8,16},{10,18},{12,20},{14,22},{16,8},... | collective-permute-start | bytes 98312 | tf_op jit(solution)/shard_map/ppermute | solution.py:200
  94.0 0.5 collective-permute-start.24
  94.4 2.0 %collective-permute-start.23 = (f32[64,128]{1,0:T(8,128)S(1)}, f32[64,128]{1,0:T(8,128)S(1)}, u32[]{:S(2)}, u32[]{:S(2)}) collective-permute-start(f32[64,128]{1,0:T(8,128)S(1)} %get-tuple-element.59), channel_id=1, source_target_pairs={{0,8},{2,10},{4,12},{6,14},{8,0},{10,2},{12,4},{14,6},{16,24},{18,... | collective-permute-start | bytes 98312 | tf_op jit(solution)/shard_map/ppermute | solution.py:200
  96.4 2.0 %collective-permute-start.19 = (f32[80,128]{1,0:T(8,128)S(1)}, f32[80,128]{1,0:T(8,128)S(1)}, u32[]{:S(2)}, u32[]{:S(2)}) collective-permute-start(f32[80,128]{1,0:T(8,128)S(1)} %get-tuple-element.61), channel_id=1, source_target_pairs={{0,24},{2,26},{4,28},{6,30},{8,16},{10,18},{12,20},{14,22},{16,8},... | collective-permute-start | bytes 122888 | tf_op jit(solution)/shard_map/ppermute | solution.py:200
  98.4 2.4 %collective-permute-start.17 = (f32[80,128]{1,0:T(8,128)S(1)}, f32[80,128]{1,0:T(8,128)S(1)}, u32[]{:S(2)}, u32[]{:S(2)}) collective-permute-start(f32[80,128]{1,0:T(8,128)S(1)} %get-tuple-element.61), channel_id=1, source_target_pairs={{0,8},{2,10},{4,12},{6,14},{8,0},{10,2},{12,4},{14,6},{16,24},{18,... | collective-permute-start | bytes 122888 | tf_op jit(solution)/shard_map/ppermute | solution.py:200
  100.9 1.4 collective-permute-start.26
  102.3 1.0 collective-permute-done.18
  103.3 1.4 collective-permute-start.20
  104.8 1.2 collective-permute-done.26
  106.1 1.6 %collective-permute-start.27 = (f32[512,128]{1,0:T(8,128)S(1)}, f32[512,128]{1,0:T(8,128)S(1)}, u32[]{:S(2)}, u32[]{:S(2)}) collective-permute-start(f32[512,128]{1,0:T(8,128)S(1)} %bitcast.66), channel_id=1, source_target_pairs={{0,1},{1,0},{2,3},{3,2},{4,5},{5,4},{6,7},{7,6},{8,9},{9,8},{10,11... | collective-permute-start | bytes 786440 | tf_op jit(solution)/shard_map/ppermute | solution.py:200
  107.7 1.1 collective-permute-done.20
  108.8 1.6 %collective-permute-start.21 = (f32[640,128]{1,0:T(8,128)S(1)}, f32[640,128]{1,0:T(8,128)S(1)}, u32[]{:S(2)}, u32[]{:S(2)}) collective-permute-start(f32[640,128]{1,0:T(8,128)S(1)} %bitcast.62), channel_id=1, source_target_pairs={{0,1},{1,0},{2,3},{3,2},{4,5},{5,4},{6,7},{7,6},{8,9},{9,8},{10,11... | collective-permute-start | bytes 983048 | tf_op jit(solution)/shard_map/ppermute | solution.py:200
  110.4 3.5 %collective-permute-done.27 = f32[512,128]{1,0:T(8,128)S(1)} collective-permute-done((f32[512,128]{1,0:T(8,128)S(1)}, f32[512,128]{1,0:T(8,128)S(1)}, u32[]{:S(2)}, u32[]{:S(2)}) %collective-permute-start.27) | collective-permute-done | bytes 262176 | tf_op jit(solution)/shard_map/ppermute | solution.py:200
  113.9 0.1 collective-permute-start.28
  114.1 3.3 %collective-permute-done.21 = f32[640,128]{1,0:T(8,128)S(1)} collective-permute-done((f32[640,128]{1,0:T(8,128)S(1)}, f32[640,128]{1,0:T(8,128)S(1)}, u32[]{:S(2)}, u32[]{:S(2)}) %collective-permute-start.21) | collective-permute-done | bytes 327712 | tf_op jit(solution)/shard_map/ppermute | solution.py:200
  117.5 0.1 collective-permute-start.22
  117.7 0.1 reverse_select_fusion.1.refs_1_
  117.8 1.9 %collective-permute-done.22 = f32[2,640,128]{2,1,0:T(8,128)S(1)} collective-permute-done((f32[2,640,128]{2,1,0:T(8,128)S(1)}, f32[2,640,128]{2,1,0:T(8,128)S(1)}, u32[]{:S(2)}, u32[]{:S(2)}) %collective-permute-start.22) | collective-permute-done | bytes 655392 | tf_op jit(solution)/shard_map/ppermute | solution.py:200
  119.6 0.1 pad_maximum_fusion
  119.7 0.1 reverse_select_fusion.refs_0_
  119.8 13.7 %shard_map.51 = (f32[192,512]{1,0:T(8,128)S(1)}, bf16[4,704,256]{2,1,0:T(8,128)(2,1)S(1)}, bf16[4,256,256]{2,1,0:T(8,128)(2,1)S(1)}) custom-call(f32[2,2,640,128]{3,2,1,0:T(8,128)S(1)} %reverse_select_fusion.refs_0_, f32[192,1024]{1,0:T(8,128)S(1)} %maximum_select_fusion.refs_1_.refs_2_), custom_call_target="tpu_custom_call" | custom-call | tf_op jit(solution)/shard_map/pallas_call | solution.py:448
  133.5 17.1 %shard_map.52 = f32[192,1024]{1,0:T(8,128)} custom-call(f32[2,2,640,128]{3,2,1,0:T(8,128)S(1)} %reverse_select_fusion.refs_0_, f32[2,2,512,128]{3,2,1,0:T(8,128)S(1)} %reverse_select_fusion.1.refs_1_, f32[192,1024]{1,0:T(8,128)S(1)} %maximum_select_fusion.refs_1_.refs_2_, f32[192,512]{1,0:T(8,128)S(1)} %get-tuple-element.52.refs_3_, ...), custom_call_target="tpu_custom_call" | custom-call | tf_op jit(solution)/shard_map/pallas_call | solution.py:454
  (54 shorter events, 1.1 us)
Async XLA Ops:
  0.0 9.8 %copy-start = (f32[384,512]{1,0:T(8,128)S(1)}, f32[384,512]{1,0:T(8,128)}, u32[]{:S(2)}) copy-start(f32[384,512]{1,0:T(8,128)} %refs_3_.1) | copy-start | bytes 2359300
  1.0 9.7 %collective-permute-start = (f32[128,512]{1,0:T(8,128)S(1)}, f32[128,512]{1,0:T(8,128)S(1)}, u32[]{:S(2)}, u32[]{:S(2)}) collective-permute-start(f32[128,512]{1,0:T(8,128)S(1)} %slice.36), channel_id=1, source_target_pairs={{2,0},{4,2},{6,4},{8,6},{10,8},{12,10},{14,12},{16,14},{18,16},{20... | collective-permute-start | bytes 786440 | tf_op jit(solution)/shard_map/ppermute | solution.py:116
  6.6 1.2 copy-start.1
  7.8 0.7 copy-start.2
  11.1 8.5 %collective-permute-start.1 = (f32[128,512]{1,0:T(8,128)S(1)}, f32[128,512]{1,0:T(8,128)S(1)}, u32[]{:S(2)}, u32[]{:S(2)}) collective-permute-start(f32[128,512]{1,0:T(8,128)S(1)} %get-tuple-element.34), channel_id=1, source_target_pairs={{30,0},{0,2},{2,4},{4,6},{6,8},{8,10},{10,12},{12,14},{14,16},{16,... | collective-permute-start | bytes 786440 | tf_op jit(solution)/shard_map/ppermute | solution.py:116
  11.2 8.5 %collective-permute-start.2 = (f32[128,512]{1,0:T(8,128)S(1)}, f32[128,512]{1,0:T(8,128)S(1)}, u32[]{:S(2)}, u32[]{:S(2)}) collective-permute-start(f32[128,512]{1,0:T(8,128)S(1)} %get-tuple-element.35), channel_id=1, source_target_pairs={{2,0},{4,2},{6,4},{8,6},{10,8},{12,10},{14,12},{16,14},{18,16},{20... | collective-permute-start | bytes 786440 | tf_op jit(solution)/shard_map/ppermute | solution.py:116
  20.1 8.8 %collective-permute-start.3 = (f32[128,512]{1,0:T(8,128)S(1)}, f32[128,512]{1,0:T(8,128)S(1)}, u32[]{:S(2)}, u32[]{:S(2)}) collective-permute-start(f32[128,512]{1,0:T(8,128)S(1)} %get-tuple-element.39), channel_id=1, source_target_pairs={{30,0},{0,2},{2,4},{4,6},{6,8},{8,10},{10,12},{12,14},{14,16},{16,... | collective-permute-start | bytes 786440 | tf_op jit(solution)/shard_map/ppermute | solution.py:116
  20.1 8.7 %collective-permute-start.4 = (f32[128,512]{1,0:T(8,128)S(1)}, f32[128,512]{1,0:T(8,128)S(1)}, u32[]{:S(2)}, u32[]{:S(2)}) collective-permute-start(f32[128,512]{1,0:T(8,128)S(1)} %get-tuple-element.40), channel_id=1, source_target_pairs={{2,0},{4,2},{6,4},{8,6},{10,8},{12,10},{14,12},{16,14},{18,16},{20... | collective-permute-start | bytes 786440 | tf_op jit(solution)/shard_map/ppermute | solution.py:116
  29.2 8.7 %collective-permute-start.5 = (f32[128,512]{1,0:T(8,128)S(1)}, f32[128,512]{1,0:T(8,128)S(1)}, u32[]{:S(2)}, u32[]{:S(2)}) collective-permute-start(f32[128,512]{1,0:T(8,128)S(1)} %get-tuple-element.44), channel_id=1, source_target_pairs={{30,0},{0,2},{2,4},{4,6},{6,8},{8,10},{10,12},{12,14},{14,16},{16,... | collective-permute-start | bytes 786440 | tf_op jit(solution)/shard_map/ppermute | solution.py:116
  29.3 8.6 %collective-permute-start.6 = (f32[128,512]{1,0:T(8,128)S(1)}, f32[128,512]{1,0:T(8,128)S(1)}, u32[]{:S(2)}, u32[]{:S(2)}) collective-permute-start(f32[128,512]{1,0:T(8,128)S(1)} %get-tuple-element.45), channel_id=1, source_target_pairs={{2,0},{4,2},{6,4},{8,6},{10,8},{12,10},{14,12},{16,14},{18,16},{20... | collective-permute-start | bytes 786440 | tf_op jit(solution)/shard_map/ppermute | solution.py:116
  38.3 8.6 %collective-permute-start.7 = (f32[128,512]{1,0:T(8,128)S(1)}, f32[128,512]{1,0:T(8,128)S(1)}, u32[]{:S(2)}, u32[]{:S(2)}) collective-permute-start(f32[128,512]{1,0:T(8,128)S(1)} %get-tuple-element.49), channel_id=1, source_target_pairs={{30,0},{0,2},{2,4},{4,6},{6,8},{8,10},{10,12},{12,14},{14,16},{16,... | collective-permute-start | bytes 786440 | tf_op jit(solution)/shard_map/ppermute | solution.py:116
  38.4 8.5 %collective-permute-start.8 = (f32[128,512]{1,0:T(8,128)S(1)}, f32[128,512]{1,0:T(8,128)S(1)}, u32[]{:S(2)}, u32[]{:S(2)}) collective-permute-start(f32[128,512]{1,0:T(8,128)S(1)} %get-tuple-element.50), channel_id=1, source_target_pairs={{2,0},{4,2},{6,4},{8,6},{10,8},{12,10},{14,12},{16,14},{18,16},{20... | collective-permute-start | bytes 786440 | tf_op jit(solution)/shard_map/ppermute | solution.py:116
  47.2 8.6 %collective-permute-start.9 = (f32[128,512]{1,0:T(8,128)S(1)}, f32[128,512]{1,0:T(8,128)S(1)}, u32[]{:S(2)}, u32[]{:S(2)}) collective-permute-start(f32[128,512]{1,0:T(8,128)S(1)} %shard_map.48), channel_id=1, source_target_pairs={{30,0},{0,2},{2,4},{4,6},{6,8},{8,10},{10,12},{12,14},{14,16},{16,... | collective-permute-start | bytes 786440 | tf_op jit(solution)/shard_map/ppermute | solution.py:116
  47.9 12.1 %collective-permute-start.11 = (f32[256,512]{1,0:T(8,128)S(1)}, f32[256,512]{1,0:T(8,128)S(1)}, u32[]{:S(2)}, u32[]{:S(2)}) collective-permute-start(f32[256,512]{1,0:T(8,128)S(1)} %slice.46), channel_id=1, source_target_pairs={{0,1},{1,0},{2,3},{3,2},{4,5},{5,4},{6,7},{7,6},{8,9},{9,8},{10,11... | collective-permute-start | bytes 1572872 | tf_op jit(solution)/shard_map/ppermute | solution.py:200
  55.9 5.4 %copy-start.3 = (f32[128,512]{1,0:T(8,128)}, f32[128,512]{1,0:T(8,128)S(1)}, u32[]{:S(2)}) copy-start(f32[128,512]{1,0:T(8,128)S(1)} %slice_add_fusion) | copy-start | bytes 786436
  55.9 6.9 %collective-permute-start.10 = (f32[128,512]{1,0:T(8,128)S(1)}, f32[128,512]{1,0:T(8,128)S(1)}, u32[]{:S(2)}, u32[]{:S(2)}) collective-permute-start(f32[128,512]{1,0:T(8,128)S(1)} %slice_add_fusion), channel_id=1, source_target_pairs={{0,1},{1,0},{2,3},{3,2},{4,5},{5,4},{6,7},{7,6},{8,9},{9,8},{10,11... | collective-permute-start | bytes 786440 | tf_op jit(solution)/shard_map/ppermute | solution.py:200
  64.7 3.6 %copy-start.4 = (f32[128,512]{1,0:T(8,128)S(1)}, f32[128,512]{1,0:T(8,128)}, u32[]{:S(2)}) copy-start(f32[128,512]{1,0:T(8,128)} %copy-done.3) | copy-start | bytes 786436
  64.7 2.3 %collective-permute-start.12 = (f32[1152,128]{1,0:T(8,128)}, f32[1152,128]{1,0:T(8,128)}, u32[]{:S(2)}, u32[]{:S(2)}) collective-permute-start(f32[1152,128]{1,0:T(8,128)} %dynamic-slice_bitcast_fusion), channel_id=1, source_target_pairs={{0,2},{2,0},{4,6},{6,4},{8,10},{10,8},{12,14},{14,12},{16,18},{18,... | collective-permute-start | bytes 1769480 | tf_op jit(solution)/shard_map/ppermute | solution.py:200
  68.3 9.1 %collective-permute-start.13 = (f32[576,128]{1,0:T(8,128)S(1)}, f32[576,128]{1,0:T(8,128)S(1)}, u32[]{:S(2)}, u32[]{:S(2)}) collective-permute-start(f32[576,128]{1,0:T(8,128)S(1)} %dynamic-slice_bitcast_fusion.1), channel_id=1, source_target_pairs={{0,4},{2,6},{4,0},{6,2},{8,12},{10,14},{12,8},{14,10},{16,20},{18,... | collective-permute-start | bytes 884744 | tf_op jit(solution)/shard_map/ppermute | solution.py:200
  77.4 11.4 %collective-permute-start.16 = (f32[144,128]{1,0:T(8,128)S(1)}, f32[144,128]{1,0:T(8,128)S(1)}, u32[]{:S(2)}, u32[]{:S(2)}) collective-permute-start(f32[144,128]{1,0:T(8,128)S(1)} %get-tuple-element.56), channel_id=1, source_target_pairs={{0,24},{2,26},{4,28},{6,30},{8,16},{10,18},{12,20},{14,22},{16,8},... | collective-permute-start | bytes 221192 | tf_op jit(solution)/shard_map/ppermute | solution.py:200
  86.2 5.3 %collective-permute-start.15 = (f32[144,128]{1,0:T(8,128)S(1)}, f32[144,128]{1,0:T(8,128)S(1)}, u32[]{:S(2)}, u32[]{:S(2)}) collective-permute-start(f32[144,128]{1,0:T(8,128)S(1)} %get-tuple-element.57), channel_id=1, source_target_pairs={{0,16},{2,18},{4,20},{6,22},{8,24},{10,26},{12,28},{14,30},{16,0},... | collective-permute-start | bytes 221192 | tf_op jit(solution)/shard_map/ppermute | solution.py:200
  86.2 5.7 %collective-permute-start.14 = (f32[144,128]{1,0:T(8,128)S(1)}, f32[144,128]{1,0:T(8,128)S(1)}, u32[]{:S(2)}, u32[]{:S(2)}) collective-permute-start(f32[144,128]{1,0:T(8,128)S(1)} %get-tuple-element.55), channel_id=1, source_target_pairs={{0,8},{2,10},{4,12},{6,14},{8,0},{10,2},{12,4},{14,6},{16,24},{18,... | collective-permute-start | bytes 221192 | tf_op jit(solution)/shard_map/ppermute | solution.py:200
  91.9 6.4 %collective-permute-start.25 = (f32[64,128]{1,0:T(8,128)S(1)}, f32[64,128]{1,0:T(8,128)S(1)}, u32[]{:S(2)}, u32[]{:S(2)}) collective-permute-start(f32[64,128]{1,0:T(8,128)S(1)} %get-tuple-element.59), channel_id=1, source_target_pairs={{0,24},{2,26},{4,28},{6,30},{8,16},{10,18},{12,20},{14,22},{16,8},... | collective-permute-start | bytes 98312 | tf_op jit(solution)/shard_map/ppermute | solution.py:200
  94.0 6.8 %collective-permute-start.24 = (f32[64,128]{1,0:T(8,128)S(1)}, f32[64,128]{1,0:T(8,128)S(1)}, u32[]{:S(2)}, u32[]{:S(2)}) collective-permute-start(f32[64,128]{1,0:T(8,128)S(1)} %get-tuple-element.59), channel_id=1, source_target_pairs={{0,16},{2,18},{4,20},{6,22},{8,24},{10,26},{12,28},{14,30},{16,0},... | collective-permute-start | bytes 98312 | tf_op jit(solution)/shard_map/ppermute | solution.py:200
  94.4 6.4 %collective-permute-start.23 = (f32[64,128]{1,0:T(8,128)S(1)}, f32[64,128]{1,0:T(8,128)S(1)}, u32[]{:S(2)}, u32[]{:S(2)}) collective-permute-start(f32[64,128]{1,0:T(8,128)S(1)} %get-tuple-element.59), channel_id=1, source_target_pairs={{0,8},{2,10},{4,12},{6,14},{8,0},{10,2},{12,4},{14,6},{16,24},{18,... | collective-permute-start | bytes 98312 | tf_op jit(solution)/shard_map/ppermute | solution.py:200
  96.4 5.9 %collective-permute-start.19 = (f32[80,128]{1,0:T(8,128)S(1)}, f32[80,128]{1,0:T(8,128)S(1)}, u32[]{:S(2)}, u32[]{:S(2)}) collective-permute-start(f32[80,128]{1,0:T(8,128)S(1)} %get-tuple-element.61), channel_id=1, source_target_pairs={{0,24},{2,26},{4,28},{6,30},{8,16},{10,18},{12,20},{14,22},{16,8},... | collective-permute-start | bytes 122888 | tf_op jit(solution)/shard_map/ppermute | solution.py:200
  98.4 4.9 %collective-permute-start.18 = (f32[80,128]{1,0:T(8,128)S(1)}, f32[80,128]{1,0:T(8,128)S(1)}, u32[]{:S(2)}, u32[]{:S(2)}) collective-permute-start(f32[80,128]{1,0:T(8,128)S(1)} %get-tuple-element.61), channel_id=1, source_target_pairs={{0,16},{2,18},{4,20},{6,22},{8,24},{10,26},{12,28},{14,30},{16,0},... | collective-permute-start | bytes 122888 | tf_op jit(solution)/shard_map/ppermute | solution.py:200
  98.4 4.9 %collective-permute-start.17 = (f32[80,128]{1,0:T(8,128)S(1)}, f32[80,128]{1,0:T(8,128)S(1)}, u32[]{:S(2)}, u32[]{:S(2)}) collective-permute-start(f32[80,128]{1,0:T(8,128)S(1)} %get-tuple-element.61), channel_id=1, source_target_pairs={{0,8},{2,10},{4,12},{6,14},{8,0},{10,2},{12,4},{14,6},{16,24},{18,... | collective-permute-start | bytes 122888 | tf_op jit(solution)/shard_map/ppermute | solution.py:200
  100.9 5.1 %collective-permute-start.26 = (f32[256,128]{1,0:T(8,128)S(1)}, f32[256,128]{1,0:T(8,128)S(1)}, u32[]{:S(2)}, u32[]{:S(2)}) collective-permute-start(f32[256,128]{1,0:T(8,128)S(1)} %bitcast.73), channel_id=1, source_target_pairs={{0,4},{2,6},{4,0},{6,2},{8,12},{10,14},{12,8},{14,10},{16,20},{18,... | collective-permute-start | bytes 393224 | tf_op jit(solution)/shard_map/ppermute | solution.py:200
  103.3 5.4 %collective-permute-start.20 = (f32[320,128]{1,0:T(8,128)S(1)}, f32[320,128]{1,0:T(8,128)S(1)}, u32[]{:S(2)}, u32[]{:S(2)}) collective-permute-start(f32[320,128]{1,0:T(8,128)S(1)} %bitcast.69), channel_id=1, source_target_pairs={{0,4},{2,6},{4,0},{6,2},{8,12},{10,14},{12,8},{14,10},{16,20},{18,... | collective-permute-start | bytes 491528 | tf_op jit(solution)/shard_map/ppermute | solution.py:200
  106.1 7.8 %collective-permute-start.27 = (f32[512,128]{1,0:T(8,128)S(1)}, f32[512,128]{1,0:T(8,128)S(1)}, u32[]{:S(2)}, u32[]{:S(2)}) collective-permute-start(f32[512,128]{1,0:T(8,128)S(1)} %bitcast.66), channel_id=1, source_target_pairs={{0,1},{1,0},{2,3},{3,2},{4,5},{5,4},{6,7},{7,6},{8,9},{9,8},{10,11... | collective-permute-start | bytes 786440 | tf_op jit(solution)/shard_map/ppermute | solution.py:200
  108.8 8.6 %collective-permute-start.21 = (f32[640,128]{1,0:T(8,128)S(1)}, f32[640,128]{1,0:T(8,128)S(1)}, u32[]{:S(2)}, u32[]{:S(2)}) collective-permute-start(f32[640,128]{1,0:T(8,128)S(1)} %bitcast.62), channel_id=1, source_target_pairs={{0,1},{1,0},{2,3},{3,2},{4,5},{5,4},{6,7},{7,6},{8,9},{9,8},{10,11... | collective-permute-start | bytes 983048 | tf_op jit(solution)/shard_map/ppermute | solution.py:200
  113.9 3.7 %collective-permute-start.28 = (f32[2,512,128]{2,1,0:T(8,128)S(1)}, f32[2,512,128]{2,1,0:T(8,128)S(1)}, u32[]{:S(2)}, u32[]{:S(2)}) collective-permute-start(f32[2,512,128]{2,1,0:T(8,128)S(1)} %reverse_select_fusion.3), channel_id=1, source_target_pairs={{0,2},{2,0},{4,6},{6,4},{8,10},{10,8},{12,14},{14,12},{16,18},{18,... | collective-permute-start | bytes 1572872 | tf_op jit(solution)/shard_map/ppermute | solution.py:200
  117.5 2.2 %collective-permute-start.22 = (f32[2,640,128]{2,1,0:T(8,128)S(1)}, f32[2,640,128]{2,1,0:T(8,128)S(1)}, u32[]{:S(2)}, u32[]{:S(2)}) collective-permute-start(f32[2,640,128]{2,1,0:T(8,128)S(1)} %reverse_select_fusion.2), channel_id=1, source_target_pairs={{0,2},{2,0},{4,6},{6,4},{8,10},{10,8},{12,14},{14,12},{16,18},{18,... | collective-permute-start | bytes 1966088 | tf_op jit(solution)/shard_map/ppermute | solution.py:200

commit v6 on v5

--- a/solution.py
+++ b/solution.py
@@ -183,16 +183,29 @@
     half_gram(mine_ref[halo:, :], other_ref[...], second_ref[0], out_ref, None)
 
 
-def high_gram_kernel(pieces, second_ref, part_ref, top_ref, other_ref, base_ref, out_ref, all_ref):
+def high_gram_kernel(pieces, flag_ref, part_ref, top_ref, other_ref, base_ref, keep_ref, send_ref, all_ref):
     halo = top_ref.shape[0]
-    half_gram(part_ref[:halo, :] + top_ref[...], other_ref[...], second_ref[0], all_ref, base_ref)
+    half_gram(part_ref[:halo, :] + top_ref[...], other_ref[...], flag_ref[1], all_ref, base_ref)
     panels = top_ref.shape[1] // LANES
     total = all_ref.shape[0]
     cut = LANES * panels * (panels + 1) // 2
     a, b, piece = cut // pieces, (total - cut) // pieces, total // pieces
-    for i in range(pieces):
-        out_ref[i * piece : i * piece + a, :] = all_ref[i * a : (i + 1) * a, :]
-        out_ref[i * piece + a : (i + 1) * piece, :] = all_ref[cut + i * b : cut + (i + 1) * b, :]
+
+    def put(out_ref, first):
+        for at in range(pieces // 2):
+            i = first + at
+            out_ref[at * piece : at * piece + a, :] = all_ref[i * a : (i + 1) * a, :]
+            out_ref[at * piece + a : (at + 1) * piece, :] = all_ref[cut + i * b : cut + (i + 1) * b, :]
+
+    @pl.when(flag_ref[0] == 0)
+    def _():
+        put(keep_ref, 0)
+        put(send_ref, pieces // 2)
+
+    @pl.when(flag_ref[0] == 1)
+    def _():
+        put(keep_ref, pieces // 2)
+        put(send_ref, 0)
 
 
 def exchanged(block, axis, mask):
@@ -381,6 +394,13 @@
     return ref[part, second, at * LANES : (at + 1) * LANES, :]
 
 
+def cross_block(ref, second, at):
+    rows = ref.shape[3] // LANES
+    part, at = divmod(at, ref.shape[1] * rows)
+    piece, at = divmod(at, rows)
+    return ref[part, piece, second, at * LANES : (at + 1) * LANES, :]
+
+
 def triangle_block(ref, second, row, col, panels):
     return quarter_block(ref, second, sum(panels - p for p in range(col)) + row - col)
 
@@ -411,7 +431,7 @@
         blocks = []
         for r in range(panels):
             second, inner = divmod(r, half)
-            blocks.append(quarter_block(cross_ref, second, p * half + inner))
+            blocks.append(cross_block(cross_ref, second, p * half + inner))
         solve = jnp.concatenate(blocks, axis=0) * scale
         for k in range(p):
             pair = left_ref[:size, 2 * k * LANES : 2 * (k + 1) * LANES]
@@ -424,13 +444,13 @@
         weight = jnp.concatenate(
             [weights(mine[:, 2 * k * LANES : 2 * (k + 1) * LANES]) for k in range(panels)], axis=1
         )
-        drop = folded(left_ref[...], weight)
+        drop = folded(left_ref[p * LANES :, :], weight)
         for r in range(panels):
             block = jnp.zeros((LANES, LANES), F32)
             if r >= p:
-                block = triangle_block(tri_ref, 1, r, p, panels) * scale - drop[r * LANES : (r + 1) * LANES]
+                block = triangle_block(tri_ref, 1, r, p, panels) * scale - drop[(r - p) * LANES : (r - p + 1) * LANES]
             work_ref[p, r * LANES : (r + 1) * LANES, :] = block
-        work_ref[p, size:, :] = rows_ref[:, size + p * LANES : size + (p + 1) * LANES] - drop[size:]
+        work_ref[p, size:, :] = rows_ref[:, size + p * LANES : size + (p + 1) * LANES] - drop[size - p * LANES :]
     factor_panels(work_ref, new_pair_ref, new_weight_ref, inverse_ref)
     out_ref[:, :size] = done_ref[...]
     for p in range(panels):
@@ -477,12 +497,17 @@
     low = exchanged(part[halo:], "orb", 1)
     gram = low_gram(flag, part, low, halo, packed)
     high = exchanged(part[:halo] + top, "orb", 1)
-    gram = high_gram(flag, part, top, high, gram)
     dom = bits("dom")
     stages = dom if len(dom) < 4 else dom[:-2] + [("dom", dom[-2][1], 4)]
-    gram = scattered(gram, stages)
+    flags = jnp.stack([rank(*stages[0]), second])
+    keep, send = high_gram(flags, part, top, high, gram)
+    gram = scattered(keep + exchanged(send, "dom", stages[0][1]), stages[1:])
     cut = LANES * panels * (panels + 1) // 2 // lax.axis_size("dom")
-    tri, cross = [everywhere(piece, stages) for piece in (gram[:cut], gram[cut:])]
+    orb = ("orb", 1, 2)
+    tri = everywhere(gram[:cut], stages[:0:-1] + [orb, stages[0]])
+    cross = everywhere(gram[cut:], stages[:1:-1] + [orb, stages[1], stages[0]])
+    tri = tri.reshape(2, 2, -1, LANES)
+    cross = cross.reshape(2, stages[1][2], 2, -1, LANES)
     mine = jnp.concatenate([part[:halo] + top, part[halo:]], axis=0).reshape(2, own // 2, cols)
     other = jnp.concatenate([high, low], axis=0).reshape(2, own // 2, cols)
     mine = jnp.where(second == 0, mine[0], mine[1])
@@ -494,9 +519,9 @@
 
 
 def everywhere(block, stages):
-    for stage in reversed(stages[1:]):
+    for stage in stages:
         block = gathered(block, stage).reshape(-1, LANES)
-    return gathered(gathered(block, ("orb", 1, 2)), stages[0])
+    return block
 
 
 def with_flag(body, out_shape, count, scratch=()):
@@ -515,9 +540,10 @@
     return with_flag(kernel, f32(packed, LANES), 2)(flag, part, low)
 
 
-def high_gram(flag, part, top, high, gram):
+def high_gram(flags, part, top, high, gram):
     kernel = lambda *refs: high_gram_kernel(lax.axis_size("dom"), *refs)
-    return with_flag(kernel, f32(*gram.shape), 4, [pltpu.VMEM(gram.shape, F32)])(flag, part, top, high, gram)
+    outs = [f32(gram.shape[0] // 2, LANES)] * 2
+    return with_flag(kernel, outs, 4, [pltpu.VMEM(gram.shape, F32)])(flags, part, top, high, gram)
 
 
 def body(orbitals, cell_mats, cell_map):
@@ -529,9 +555,10 @@
     panels = cols // LANES
     two = (
         lax.axis_size("orb") == 2
-        and lax.axis_size("dom") > 1
+        and lax.axis_size("dom") > 2
         and cols % (2 * LANES) == 0
         and (LANES * panels * (panels + 1) // 2) % lax.axis_size("dom") == 0
+        and panels * panels // 2 % 4 == 0
         and (LANES * panels * panels // 2) % lax.axis_size("dom") == 0
     )
     return (two_orb if two else any_orb)(part, top, 1.0 / node_total)

time: 151 us -> 149 us (0.987)
  no operation moved by 1% of the time
where the time goes in v6:
time: 149 us
  starting transfers between devices  51.7 us (35%)
  waiting for transfers between devices  47.2 us (32%)
  Pallas kernels  44.1 us (30%)
  local copies, waits for them, and re-layouts  3.07 us (2%)
  other arithmetic  2.15 us (1%)
    ppermute x19, waiting for transfers between devices, exchanged(): return lax.ppermute(block, axis, route)  30.7 us
    ppermute x19, starting transfers between devices, exchanged(): return lax.ppermute(block, axis, route)  27.8 us
    ppermute x10, starting transfers between devices, shifted(): return lax.ppermute(block, axis, route)  24 us
    pallas_call x1, Pallas kernels, factor_halves(): kernel_call(lambda *refs: second_kernel(scale, *refs), f32(count, width),...  16.7 us
    ppermute x10, waiting for transfers between devices, shifted(): return lax.ppermute(block, axis, route)  16.4 us
    pallas_call x1, Pallas kernels, factor_halves(): kernel_call(lambda *refs: first_kernel(scale, *refs), [f32(count, size),...  13.7 us
    pallas_call x5, Pallas kernels, filtered_columns(): got = kernel_call(rest, outs)(*matrix, applied, vec, *arrived, *before)  6.67 us
  transfers between devices with their start and end apart: 29, of which 18 were waited for; matrix products, arithmetic and copies ran while one was open for 1% of the time, Pallas kernels for 7%

profile of v6, /device:TPU:0, one launch (start us, length us, event | category | flops | bytes accessed | tf_op | source)
XLA Modules:
  0.0 148.8 jit_solution(15957555309664649405)
XLA Ops:
  0.0 1.0 slice.36
  1.0 5.5 %collective-permute-start = (f32[128,512]{1,0:T(8,128)S(1)}, f32[128,512]{1,0:T(8,128)S(1)}, u32[]{:S(2)}, u32[]{:S(2)}) collective-permute-start(f32[128,512]{1,0:T(8,128)S(1)} %slice.36), channel_id=1, source_target_pairs={{2,0},{4,2},{6,4},{8,6},{10,8},{12,10},{14,12},{16,14},{18,16},{20... | collective-permute-start | bytes 786440 | tf_op jit(solution)/shard_map/ppermute | solution.py:116
  6.6 1.2 copy-done.1
  7.8 0.7 copy-done.2
  8.5 1.3 shard_map.37
  9.8 1.0 shard_map.38.refs_2_
  10.8 0.4 shard_map.40
  11.2 4.5 %collective-permute-start.2 = (f32[128,512]{1,0:T(8,128)S(1)}, f32[128,512]{1,0:T(8,128)S(1)}, u32[]{:S(2)}, u32[]{:S(2)}) collective-permute-start(f32[128,512]{1,0:T(8,128)S(1)} %get-tuple-element.37), channel_id=1, source_target_pairs={{2,0},{4,2},{6,4},{8,6},{10,8},{12,10},{14,12},{16,14},{18,16},{20... | collective-permute-start | bytes 786440 | tf_op jit(solution)/shard_map/ppermute | solution.py:116
  15.6 1.5 %shard_map.39 = (f32[512,512]{1,0:T(8,128)S(1)}, f32[512,512]{1,0:T(8,128)S(1)}, f32[512,512]{1,0:T(8,128)S(1)}) custom-call(bf16[512,512]{1,0:T(8,128)(2,1)S(1)} %get-tuple-element.32.hi_ref.refs_0_, bf16[512,512]{1,0:T(8,128)(2,1)S(1)} %get-tuple-element.33.lo_ref.refs_1_, f32[512,512]{1,0:T(8,128)S(1)} %shard_map.38.refs_2_, f32[384,512]{1,0:T(8,128)S(1)} %copy-done, ...), custom_call_target="tpu_custom_call" | custom-call | tf_op jit(solution)/shard_map/pallas_call | solution.py:135
  17.2 2.5 %collective-permute-done.1.refs_4_.refs_3_ = f32[128,512]{1,0:T(8,128)S(1)} collective-permute-done((f32[128,512]{1,0:T(8,128)S(1)}, f32[128,512]{1,0:T(8,128)S(1)}, u32[]{:S(2)}, u32[]{:S(2)}) %collective-permute-start.1) | collective-permute-done | bytes 262176 | tf_op jit(solution)/shard_map/ppermute | solution.py:116
  19.7 0.4 shard_map.42
  20.1 4.6 %collective-permute-start.4 = (f32[128,512]{1,0:T(8,128)S(1)}, f32[128,512]{1,0:T(8,128)S(1)}, u32[]{:S(2)}, u32[]{:S(2)}) collective-permute-start(f32[128,512]{1,0:T(8,128)S(1)} %get-tuple-element.42), channel_id=1, source_target_pairs={{2,0},{4,2},{6,4},{8,6},{10,8},{12,10},{14,12},{16,14},{18,16},{20... | collective-permute-start | bytes 786440 | tf_op jit(solution)/shard_map/ppermute | solution.py:116
  24.7 1.5 %shard_map.41 = (f32[512,512]{1,0:T(8,128)S(1)}, f32[512,512]{1,0:T(8,128)S(1)}, f32[512,512]{1,0:T(8,128)S(1)}) custom-call(bf16[512,512]{1,0:T(8,128)(2,1)S(1)} %get-tuple-element.32.hi_ref.refs_0_, bf16[512,512]{1,0:T(8,128)(2,1)S(1)} %get-tuple-element.33.lo_ref.refs_1_, f32[512,512]{1,0:T(8,128)S(1)} %get-tuple-element.34.refs_2_, ...), custom_call_target="tpu_custom_call" | custom-call | tf_op jit(solution)/shard_map/pallas_call | solution.py:135
  26.3 2.5 %collective-permute-done.3.refs_4_.refs_3_ = f32[128,512]{1,0:T(8,128)S(1)} collective-permute-done((f32[128,512]{1,0:T(8,128)S(1)}, f32[128,512]{1,0:T(8,128)S(1)}, u32[]{:S(2)}, u32[]{:S(2)}) %collective-permute-start.3) | collective-permute-done | bytes 262176 | tf_op jit(solution)/shard_map/ppermute | solution.py:116
  28.8 0.4 shard_map.44
  29.3 4.6 %collective-permute-start.6 = (f32[128,512]{1,0:T(8,128)S(1)}, f32[128,512]{1,0:T(8,128)S(1)}, u32[]{:S(2)}, u32[]{:S(2)}) collective-permute-start(f32[128,512]{1,0:T(8,128)S(1)} %get-tuple-element.47), channel_id=1, source_target_pairs={{2,0},{4,2},{6,4},{8,6},{10,8},{12,10},{14,12},{16,14},{18,16},{20... | collective-permute-start | bytes 786440 | tf_op jit(solution)/shard_map/ppermute | solution.py:116
  33.9 1.5 %shard_map.43 = (f32[512,512]{1,0:T(8,128)S(1)}, f32[512,512]{1,0:T(8,128)S(1)}, f32[512,512]{1,0:T(8,128)S(1)}) custom-call(bf16[512,512]{1,0:T(8,128)(2,1)S(1)} %get-tuple-element.32.hi_ref.refs_0_, bf16[512,512]{1,0:T(8,128)(2,1)S(1)} %get-tuple-element.33.lo_ref.refs_1_, f32[512,512]{1,0:T(8,128)S(1)} %get-tuple-element.39.refs_2_, ...), custom_call_target="tpu_custom_call" | custom-call | tf_op jit(solution)/shard_map/pallas_call | solution.py:135
  35.4 2.5 %collective-permute-done.5.refs_4_.refs_3_ = f32[128,512]{1,0:T(8,128)S(1)} collective-permute-done((f32[128,512]{1,0:T(8,128)S(1)}, f32[128,512]{1,0:T(8,128)S(1)}, u32[]{:S(2)}, u32[]{:S(2)}) %collective-permute-start.5) | collective-permute-done | bytes 262176 | tf_op jit(solution)/shard_map/ppermute | solution.py:116
  37.9 0.4 shard_map.46
  38.4 4.6 %collective-permute-start.8 = (f32[128,512]{1,0:T(8,128)S(1)}, f32[128,512]{1,0:T(8,128)S(1)}, u32[]{:S(2)}, u32[]{:S(2)}) collective-permute-start(f32[128,512]{1,0:T(8,128)S(1)} %get-tuple-element.52), channel_id=1, source_target_pairs={{2,0},{4,2},{6,4},{8,6},{10,8},{12,10},{14,12},{16,14},{18,16},{20... | collective-permute-start | bytes 786440 | tf_op jit(solution)/shard_map/ppermute | solution.py:116
  43.0 1.5 %shard_map.45 = (f32[512,512]{1,0:T(8,128)S(1)}, f32[512,512]{1,0:T(8,128)S(1)}, f32[512,512]{1,0:T(8,128)S(1)}) custom-call(bf16[512,512]{1,0:T(8,128)(2,1)S(1)} %get-tuple-element.32.hi_ref.refs_0_, bf16[512,512]{1,0:T(8,128)(2,1)S(1)} %get-tuple-element.33.lo_ref.refs_1_, f32[512,512]{1,0:T(8,128)S(1)} %get-tuple-element.44.refs_2_, ...), custom_call_target="tpu_custom_call" | custom-call | tf_op jit(solution)/shard_map/pallas_call | solution.py:135
  44.5 2.4 %collective-permute-done.7.refs_4_.refs_3_ = f32[128,512]{1,0:T(8,128)S(1)} collective-permute-done((f32[128,512]{1,0:T(8,128)S(1)}, f32[128,512]{1,0:T(8,128)S(1)}, u32[]{:S(2)}, u32[]{:S(2)}) %collective-permute-start.7) | collective-permute-done | bytes 262176 | tf_op jit(solution)/shard_map/ppermute | solution.py:116
  46.9 0.3 shard_map.48
  47.3 0.5 shard_map.47.refs_1_
  47.9 1.6 %collective-permute-start.11 = (f32[256,512]{1,0:T(8,128)S(1)}, f32[256,512]{1,0:T(8,128)S(1)}, u32[]{:S(2)}, u32[]{:S(2)}) collective-permute-start(f32[256,512]{1,0:T(8,128)S(1)} %slice.46), channel_id=1, source_target_pairs={{0,1},{1,0},{2,3},{3,2},{4,5},{5,4},{6,7},{7,6},{8,9},{9,8},{10,11... | collective-permute-start | bytes 1572872 | tf_op jit(solution)/shard_map/ppermute | solution.py:213
  49.5 6.4 %collective-permute-done.9.refs_2_ = f32[128,512]{1,0:T(8,128)S(1)} collective-permute-done((f32[128,512]{1,0:T(8,128)S(1)}, f32[128,512]{1,0:T(8,128)S(1)}, u32[]{:S(2)}, u32[]{:S(2)}) %collective-permute-start.9) | collective-permute-done | bytes 262176 | tf_op jit(solution)/shard_map/ppermute | solution.py:116
  55.9 1.6 %collective-permute-start.10 = (f32[128,512]{1,0:T(8,128)S(1)}, f32[128,512]{1,0:T(8,128)S(1)}, u32[]{:S(2)}, u32[]{:S(2)}) collective-permute-start(f32[128,512]{1,0:T(8,128)S(1)} %slice_add_fusion), channel_id=1, source_target_pairs={{0,1},{1,0},{2,3},{3,2},{4,5},{5,4},{6,7},{7,6},{8,9},{9,8},{10,11... | collective-permute-start | bytes 786440 | tf_op jit(solution)/shard_map/ppermute | solution.py:213
  57.5 0.1 pad_add_fusion.refs_0_
  57.5 2.4 %collective-permute-done.11.refs_2_ = f32[256,512]{1,0:T(8,128)S(1)} collective-permute-done((f32[256,512]{1,0:T(8,128)S(1)}, f32[256,512]{1,0:T(8,128)S(1)}, u32[]{:S(2)}, u32[]{:S(2)}) %collective-permute-start.11) | collective-permute-done | bytes 524320 | tf_op jit(solution)/shard_map/ppermute | solution.py:213
  60.0 1.3 shard_map.49.refs_4_
  61.3 1.4 collective-permute-done.10.refs_3_
  62.8 1.7 %shard_map.50 = (f32[1152,128]{1,0:T(8,128)S(1)}, f32[1152,128]{1,0:T(8,128)S(1)}) custom-call(s32[2]{0:T(128)S(1)} %pad_add_fusion.refs_0_, f32[384,512]{1,0:T(8,128)S(1)} %shard_map.47.refs_1_, f32[128,512]{1,0:T(8,128)S(1)} %collective-permute-done.9.refs_2_, f32[128,512]{1,0:T(8,128)S(1)} %collective-permute-done.10.refs_3_, ...), custom_call_target="tpu_custom_call" | custom-call | tf_op jit(solution)/shard_map/pallas_call | solution.py:546
  64.4 0.1 collective-permute-start.12
  64.6 2.1 %collective-permute-done.12 = f32[1152,128]{1,0:T(8,128)} collective-permute-done((f32[1152,128]{1,0:T(8,128)S(1)}, f32[1152,128]{1,0:T(8,128)}, u32[]{:S(2)}, u32[]{:S(2)}) %collective-permute-start.12) | collective-permute-done | bytes 589856 | tf_op jit(solution)/shard_map/ppermute | solution.py:213
  66.6 1.1 add.68
  67.8 0.1 collective-permute-start.13
  68.0 9.0 %collective-permute-done.13 = f32[576,128]{1,0:T(8,128)S(1)} collective-permute-done((f32[576,128]{1,0:T(8,128)S(1)}, f32[576,128]{1,0:T(8,128)S(1)}, u32[]{:S(2)}, u32[]{:S(2)}) %collective-permute-start.13) | collective-permute-done | bytes 294944 | tf_op jit(solution)/shard_map/ppermute | solution.py:213
  77.0 8.8 %collective-permute-start.16 = (f32[144,128]{1,0:T(8,128)S(1)}, f32[144,128]{1,0:T(8,128)S(1)}, u32[]{:S(2)}, u32[]{:S(2)}) collective-permute-start(f32[144,128]{1,0:T(8,128)S(1)} %get-tuple-element.60), channel_id=1, source_target_pairs={{0,24},{2,26},{4,28},{6,30},{8,16},{10,18},{12,20},{14,22},{16,8},... | collective-permute-start | bytes 221192 | tf_op jit(solution)/shard_map/ppermute | solution.py:213
  85.8 0.6 collective-permute-start.14
  86.5 1.9 %collective-permute-done.16 = f32[144,128]{1,0:T(8,128)S(1)} collective-permute-done((f32[144,128]{1,0:T(8,128)S(1)}, f32[144,128]{1,0:T(8,128)S(1)}, u32[]{:S(2)}, u32[]{:S(2)}) %collective-permute-start.16) | collective-permute-done | bytes 73760 | tf_op jit(solution)/shard_map/ppermute | solution.py:213
  88.4 2.6 %collective-permute-done.15 = f32[144,128]{1,0:T(8,128)S(1)} collective-permute-done((f32[144,128]{1,0:T(8,128)S(1)}, f32[144,128]{1,0:T(8,128)S(1)}, u32[]{:S(2)}, u32[]{:S(2)}) %collective-permute-start.15) | collective-permute-done | bytes 73760 | tf_op jit(solution)/shard_map/ppermute | solution.py:213
  91.0 0.4 collective-permute-done.14
  91.5 2.0 %collective-permute-start.25 = (f32[64,128]{1,0:T(8,128)S(1)}, f32[64,128]{1,0:T(8,128)S(1)}, u32[]{:S(2)}, u32[]{:S(2)}) collective-permute-start(f32[64,128]{1,0:T(8,128)S(1)} %get-tuple-element.63), channel_id=1, source_target_pairs={{0,24},{2,26},{4,28},{6,30},{8,16},{10,18},{12,20},{14,22},{16,8},... | collective-permute-start | bytes 98312 | tf_op jit(solution)/shard_map/ppermute | solution.py:213
  93.5 0.5 collective-permute-start.24
  94.0 2.0 %collective-permute-start.23 = (f32[64,128]{1,0:T(8,128)S(1)}, f32[64,128]{1,0:T(8,128)S(1)}, u32[]{:S(2)}, u32[]{:S(2)}) collective-permute-start(f32[64,128]{1,0:T(8,128)S(1)} %get-tuple-element.63), channel_id=1, source_target_pairs={{0,8},{2,10},{4,12},{6,14},{8,0},{10,2},{12,4},{14,6},{16,24},{18,... | collective-permute-start | bytes 98312 | tf_op jit(solution)/shard_map/ppermute | solution.py:213
  96.0 2.0 %collective-permute-start.19 = (f32[80,128]{1,0:T(8,128)S(1)}, f32[80,128]{1,0:T(8,128)S(1)}, u32[]{:S(2)}, u32[]{:S(2)}) collective-permute-start(f32[80,128]{1,0:T(8,128)S(1)} %get-tuple-element.65), channel_id=1, source_target_pairs={{0,24},{2,26},{4,28},{6,30},{8,16},{10,18},{12,20},{14,22},{16,8},... | collective-permute-start | bytes 122888 | tf_op jit(solution)/shard_map/ppermute | solution.py:213
  97.9 2.4 %collective-permute-start.17 = (f32[80,128]{1,0:T(8,128)S(1)}, f32[80,128]{1,0:T(8,128)S(1)}, u32[]{:S(2)}, u32[]{:S(2)}) collective-permute-start(f32[80,128]{1,0:T(8,128)S(1)} %get-tuple-element.65), channel_id=1, source_target_pairs={{0,8},{2,10},{4,12},{6,14},{8,0},{10,2},{12,4},{14,6},{16,24},{18,... | collective-permute-start | bytes 122888 | tf_op jit(solution)/shard_map/ppermute | solution.py:213
  100.4 1.6 %collective-permute-start.26 = (f32[256,128]{1,0:T(8,128)S(1)}, f32[256,128]{1,0:T(8,128)S(1)}, u32[]{:S(2)}, u32[]{:S(2)}) collective-permute-start(f32[256,128]{1,0:T(8,128)S(1)} %bitcast.76), channel_id=1, source_target_pairs={{0,1},{1,0},{2,3},{3,2},{4,5},{5,4},{6,7},{7,6},{8,9},{9,8},{10,11... | collective-permute-start | bytes 393224 | tf_op jit(solution)/shard_map/ppermute | solution.py:213
  102.0 0.8 collective-permute-done.18
  102.9 1.4 collective-permute-start.20
  104.3 1.1 collective-permute-done.26
  105.5 1.4 collective-permute-start.27
  106.9 1.8 %collective-permute-done.20 = f32[320,128]{1,0:T(8,128)S(1)} collective-permute-done((f32[320,128]{1,0:T(8,128)S(1)}, f32[320,128]{1,0:T(8,128)S(1)}, u32[]{:S(2)}, u32[]{:S(2)}) %collective-permute-start.20) | collective-permute-done | bytes 163872 | tf_op jit(solution)/shard_map/ppermute | solution.py:213
  108.8 1.6 %collective-permute-start.21 = (f32[640,128]{1,0:T(8,128)S(1)}, f32[640,128]{1,0:T(8,128)S(1)}, u32[]{:S(2)}, u32[]{:S(2)}) collective-permute-start(f32[640,128]{1,0:T(8,128)S(1)} %bitcast.65), channel_id=1, source_target_pairs={{0,1},{1,0},{2,3},{3,2},{4,5},{5,4},{6,7},{7,6},{8,9},{9,8},{10,11... | collective-permute-start | bytes 983048 | tf_op jit(solution)/shard_map/ppermute | solution.py:213
  110.4 1.6 %collective-permute-done.27 = f32[512,128]{1,0:T(8,128)S(1)} collective-permute-done((f32[512,128]{1,0:T(8,128)S(1)}, f32[512,128]{1,0:T(8,128)S(1)}, u32[]{:S(2)}, u32[]{:S(2)}) %collective-permute-start.27) | collective-permute-done | bytes 262176 | tf_op jit(solution)/shard_map/ppermute | solution.py:213
  112.0 0.1 collective-permute-start.28
  112.1 3.8 %collective-permute-done.21 = f32[640,128]{1,0:T(8,128)S(1)} collective-permute-done((f32[640,128]{1,0:T(8,128)S(1)}, f32[640,128]{1,0:T(8,128)S(1)}, u32[]{:S(2)}, u32[]{:S(2)}) %collective-permute-start.21) | collective-permute-done | bytes 327712 | tf_op jit(solution)/shard_map/ppermute | solution.py:213
  116.2 0.1 maximum_select_fusion.refs_1_.refs_2_
  116.3 0.1 reverse_select_fusion.1
  116.4 1.8 %collective-permute-done.22 = f32[1280,128]{1,0:T(8,128)S(1)} collective-permute-done((f32[1280,128]{1,0:T(8,128)S(1)}, f32[1280,128]{1,0:T(8,128)S(1)}, u32[]{:S(2)}, u32[]{:S(2)}) %collective-permute-start.22) | collective-permute-done | bytes 655392 | tf_op jit(solution)/shard_map/ppermute | solution.py:213
  118.2 0.1 pad_maximum_fusion
  118.3 0.1 reverse_select_fusion
  118.4 13.7 %shard_map.51 = (f32[192,512]{1,0:T(8,128)S(1)}, bf16[4,704,256]{2,1,0:T(8,128)(2,1)S(1)}, bf16[4,256,256]{2,1,0:T(8,128)(2,1)S(1)}) custom-call(f32[2,2,640,128]{3,2,1,0:T(8,128)S(1)} %bitcast.56, f32[192,1024]{1,0:T(8,128)S(1)} %maximum_select_fusion.refs_1_.refs_2_), custom_call_target="tpu_custom_call" | custom-call | tf_op jit(solution)/shard_map/pallas_call | solution.py:468
  132.1 16.7 %shard_map.52 = f32[192,1024]{1,0:T(8,128)} custom-call(f32[2,2,640,128]{3,2,1,0:T(8,128)S(1)} %bitcast.57, f32[2,2,2,256,128]{4,3,2,1,0:T(8,128)S(1)} %bitcast.58, f32[192,1024]{1,0:T(8,128)S(1)} %maximum_select_fusion.refs_1_.refs_2_, f32[192,512]{1,0:T(8,128)S(1)} %get-tuple-element.56.refs_3_, bf16[4,704,256]{2,1,0:T(8,128)(2,1)S(1)} %get-tuple-element.57.refs_4_, ...), custom_call_target="tpu_custom_call" | custom-call | tf_op jit(solution)/shard_map/pallas_call | solution.py:474
  (52 shorter events, 1.1 us)
Async XLA Ops:
  0.0 9.8 %copy-start = (f32[384,512]{1,0:T(8,128)S(1)}, f32[384,512]{1,0:T(8,128)}, u32[]{:S(2)}) copy-start(f32[384,512]{1,0:T(8,128)} %refs_3_.1) | copy-start | bytes 2359300
  1.0 9.7 %collective-permute-start = (f32[128,512]{1,0:T(8,128)S(1)}, f32[128,512]{1,0:T(8,128)S(1)}, u32[]{:S(2)}, u32[]{:S(2)}) collective-permute-start(f32[128,512]{1,0:T(8,128)S(1)} %slice.36), channel_id=1, source_target_pairs={{2,0},{4,2},{6,4},{8,6},{10,8},{12,10},{14,12},{16,14},{18,16},{20... | collective-permute-start | bytes 786440 | tf_op jit(solution)/shard_map/ppermute | solution.py:116
  6.6 1.2 copy-start.1
  7.8 0.7 copy-start.2
  11.1 8.5 %collective-permute-start.1 = (f32[128,512]{1,0:T(8,128)S(1)}, f32[128,512]{1,0:T(8,128)S(1)}, u32[]{:S(2)}, u32[]{:S(2)}) collective-permute-start(f32[128,512]{1,0:T(8,128)S(1)} %get-tuple-element.36), channel_id=1, source_target_pairs={{30,0},{0,2},{2,4},{4,6},{6,8},{8,10},{10,12},{12,14},{14,16},{16,... | collective-permute-start | bytes 786440 | tf_op jit(solution)/shard_map/ppermute | solution.py:116
  11.2 8.5 %collective-permute-start.2 = (f32[128,512]{1,0:T(8,128)S(1)}, f32[128,512]{1,0:T(8,128)S(1)}, u32[]{:S(2)}, u32[]{:S(2)}) collective-permute-start(f32[128,512]{1,0:T(8,128)S(1)} %get-tuple-element.37), channel_id=1, source_target_pairs={{2,0},{4,2},{6,4},{8,6},{10,8},{12,10},{14,12},{16,14},{18,16},{20... | collective-permute-start | bytes 786440 | tf_op jit(solution)/shard_map/ppermute | solution.py:116
  20.1 8.8 %collective-permute-start.3 = (f32[128,512]{1,0:T(8,128)S(1)}, f32[128,512]{1,0:T(8,128)S(1)}, u32[]{:S(2)}, u32[]{:S(2)}) collective-permute-start(f32[128,512]{1,0:T(8,128)S(1)} %get-tuple-element.41), channel_id=1, source_target_pairs={{30,0},{0,2},{2,4},{4,6},{6,8},{8,10},{10,12},{12,14},{14,16},{16,... | collective-permute-start | bytes 786440 | tf_op jit(solution)/shard_map/ppermute | solution.py:116
  20.1 8.7 %collective-permute-start.4 = (f32[128,512]{1,0:T(8,128)S(1)}, f32[128,512]{1,0:T(8,128)S(1)}, u32[]{:S(2)}, u32[]{:S(2)}) collective-permute-start(f32[128,512]{1,0:T(8,128)S(1)} %get-tuple-element.42), channel_id=1, source_target_pairs={{2,0},{4,2},{6,4},{8,6},{10,8},{12,10},{14,12},{16,14},{18,16},{20... | collective-permute-start | bytes 786440 | tf_op jit(solution)/shard_map/ppermute | solution.py:116
  29.2 8.7 %collective-permute-start.5 = (f32[128,512]{1,0:T(8,128)S(1)}, f32[128,512]{1,0:T(8,128)S(1)}, u32[]{:S(2)}, u32[]{:S(2)}) collective-permute-start(f32[128,512]{1,0:T(8,128)S(1)} %get-tuple-element.46), channel_id=1, source_target_pairs={{30,0},{0,2},{2,4},{4,6},{6,8},{8,10},{10,12},{12,14},{14,16},{16,... | collective-permute-start | bytes 786440 | tf_op jit(solution)/shard_map/ppermute | solution.py:116
  29.3 8.6 %collective-permute-start.6 = (f32[128,512]{1,0:T(8,128)S(1)}, f32[128,512]{1,0:T(8,128)S(1)}, u32[]{:S(2)}, u32[]{:S(2)}) collective-permute-start(f32[128,512]{1,0:T(8,128)S(1)} %get-tuple-element.47), channel_id=1, source_target_pairs={{2,0},{4,2},{6,4},{8,6},{10,8},{12,10},{14,12},{16,14},{18,16},{20... | collective-permute-start | bytes 786440 | tf_op jit(solution)/shard_map/ppermute | solution.py:116
  38.3 8.6 %collective-permute-start.7 = (f32[128,512]{1,0:T(8,128)S(1)}, f32[128,512]{1,0:T(8,128)S(1)}, u32[]{:S(2)}, u32[]{:S(2)}) collective-permute-start(f32[128,512]{1,0:T(8,128)S(1)} %get-tuple-element.51), channel_id=1, source_target_pairs={{30,0},{0,2},{2,4},{4,6},{6,8},{8,10},{10,12},{12,14},{14,16},{16,... | collective-permute-start | bytes 786440 | tf_op jit(solution)/shard_map/ppermute | solution.py:116
  38.4 8.5 %collective-permute-start.8 = (f32[128,512]{1,0:T(8,128)S(1)}, f32[128,512]{1,0:T(8,128)S(1)}, u32[]{:S(2)}, u32[]{:S(2)}) collective-permute-start(f32[128,512]{1,0:T(8,128)S(1)} %get-tuple-element.52), channel_id=1, source_target_pairs={{2,0},{4,2},{6,4},{8,6},{10,8},{12,10},{14,12},{16,14},{18,16},{20... | collective-permute-start | bytes 786440 | tf_op jit(solution)/shard_map/ppermute | solution.py:116
  47.2 8.6 %collective-permute-start.9 = (f32[128,512]{1,0:T(8,128)S(1)}, f32[128,512]{1,0:T(8,128)S(1)}, u32[]{:S(2)}, u32[]{:S(2)}) collective-permute-start(f32[128,512]{1,0:T(8,128)S(1)} %shard_map.48), channel_id=1, source_target_pairs={{30,0},{0,2},{2,4},{4,6},{6,8},{8,10},{10,12},{12,14},{14,16},{16,... | collective-permute-start | bytes 786440 | tf_op jit(solution)/shard_map/ppermute | solution.py:116
  47.9 12.1 %collective-permute-start.11 = (f32[256,512]{1,0:T(8,128)S(1)}, f32[256,512]{1,0:T(8,128)S(1)}, u32[]{:S(2)}, u32[]{:S(2)}) collective-permute-start(f32[256,512]{1,0:T(8,128)S(1)} %slice.46), channel_id=1, source_target_pairs={{0,1},{1,0},{2,3},{3,2},{4,5},{5,4},{6,7},{7,6},{8,9},{9,8},{10,11... | collective-permute-start | bytes 1572872 | tf_op jit(solution)/shard_map/ppermute | solution.py:213
  55.9 5.4 %copy-start.3 = (f32[128,512]{1,0:T(8,128)}, f32[128,512]{1,0:T(8,128)S(1)}, u32[]{:S(2)}) copy-start(f32[128,512]{1,0:T(8,128)S(1)} %slice_add_fusion) | copy-start | bytes 786436
  55.9 6.9 %collective-permute-start.10 = (f32[128,512]{1,0:T(8,128)S(1)}, f32[128,512]{1,0:T(8,128)S(1)}, u32[]{:S(2)}, u32[]{:S(2)}) collective-permute-start(f32[128,512]{1,0:T(8,128)S(1)} %slice_add_fusion), channel_id=1, source_target_pairs={{0,1},{1,0},{2,3},{3,2},{4,5},{5,4},{6,7},{7,6},{8,9},{9,8},{10,11... | collective-permute-start | bytes 786440 | tf_op jit(solution)/shard_map/ppermute | solution.py:213
  64.4 2.2 %collective-permute-start.12 = (f32[1152,128]{1,0:T(8,128)S(1)}, f32[1152,128]{1,0:T(8,128)}, u32[]{:S(2)}, u32[]{:S(2)}) collective-permute-start(f32[1152,128]{1,0:T(8,128)S(1)} %get-tuple-element.55), channel_id=1, source_target_pairs={{0,2},{2,0},{4,6},{6,4},{8,10},{10,8},{12,14},{14,12},{16,18},{18,... | collective-permute-start | bytes 1769480 | tf_op jit(solution)/shard_map/ppermute | solution.py:213
  67.8 18.7 %copy-start.4 = (f32[128,512]{1,0:T(8,128)S(1)}, f32[128,512]{1,0:T(8,128)}, u32[]{:S(2)}) copy-start(f32[128,512]{1,0:T(8,128)} %copy-done.3) | copy-start | bytes 786436
  67.8 9.1 %collective-permute-start.13 = (f32[576,128]{1,0:T(8,128)S(1)}, f32[576,128]{1,0:T(8,128)S(1)}, u32[]{:S(2)}, u32[]{:S(2)}) collective-permute-start(f32[576,128]{1,0:T(8,128)S(1)} %dynamic-slice_bitcast_fusion), channel_id=1, source_target_pairs={{0,4},{2,6},{4,0},{6,2},{8,12},{10,14},{12,8},{14,10},{16,20},{18,... | collective-permute-start | bytes 884744 | tf_op jit(solution)/shard_map/ppermute | solution.py:213
  77.0 11.4 %collective-permute-start.16 = (f32[144,128]{1,0:T(8,128)S(1)}, f32[144,128]{1,0:T(8,128)S(1)}, u32[]{:S(2)}, u32[]{:S(2)}) collective-permute-start(f32[144,128]{1,0:T(8,128)S(1)} %get-tuple-element.60), channel_id=1, source_target_pairs={{0,24},{2,26},{4,28},{6,30},{8,16},{10,18},{12,20},{14,22},{16,8},... | collective-permute-start | bytes 221192 | tf_op jit(solution)/shard_map/ppermute | solution.py:213
  85.8 5.3 %collective-permute-start.15 = (f32[144,128]{1,0:T(8,128)S(1)}, f32[144,128]{1,0:T(8,128)S(1)}, u32[]{:S(2)}, u32[]{:S(2)}) collective-permute-start(f32[144,128]{1,0:T(8,128)S(1)} %get-tuple-element.61), channel_id=1, source_target_pairs={{0,16},{2,18},{4,20},{6,22},{8,24},{10,26},{12,28},{14,30},{16,0},... | collective-permute-start | bytes 221192 | tf_op jit(solution)/shard_map/ppermute | solution.py:213
  85.8 5.7 %collective-permute-start.14 = (f32[144,128]{1,0:T(8,128)S(1)}, f32[144,128]{1,0:T(8,128)S(1)}, u32[]{:S(2)}, u32[]{:S(2)}) collective-permute-start(f32[144,128]{1,0:T(8,128)S(1)} %get-tuple-element.59), channel_id=1, source_target_pairs={{0,8},{2,10},{4,12},{6,14},{8,0},{10,2},{12,4},{14,6},{16,24},{18,... | collective-permute-start | bytes 221192 | tf_op jit(solution)/shard_map/ppermute | solution.py:213
  91.5 6.4 %collective-permute-start.25 = (f32[64,128]{1,0:T(8,128)S(1)}, f32[64,128]{1,0:T(8,128)S(1)}, u32[]{:S(2)}, u32[]{:S(2)}) collective-permute-start(f32[64,128]{1,0:T(8,128)S(1)} %get-tuple-element.63), channel_id=1, source_target_pairs={{0,24},{2,26},{4,28},{6,30},{8,16},{10,18},{12,20},{14,22},{16,8},... | collective-permute-start | bytes 98312 | tf_op jit(solution)/shard_map/ppermute | solution.py:213
  93.5 6.8 %collective-permute-start.24 = (f32[64,128]{1,0:T(8,128)S(1)}, f32[64,128]{1,0:T(8,128)S(1)}, u32[]{:S(2)}, u32[]{:S(2)}) collective-permute-start(f32[64,128]{1,0:T(8,128)S(1)} %get-tuple-element.63), channel_id=1, source_target_pairs={{0,16},{2,18},{4,20},{6,22},{8,24},{10,26},{12,28},{14,30},{16,0},... | collective-permute-start | bytes 98312 | tf_op jit(solution)/shard_map/ppermute | solution.py:213
  94.0 6.4 %collective-permute-start.23 = (f32[64,128]{1,0:T(8,128)S(1)}, f32[64,128]{1,0:T(8,128)S(1)}, u32[]{:S(2)}, u32[]{:S(2)}) collective-permute-start(f32[64,128]{1,0:T(8,128)S(1)} %get-tuple-element.63), channel_id=1, source_target_pairs={{0,8},{2,10},{4,12},{6,14},{8,0},{10,2},{12,4},{14,6},{16,24},{18,... | collective-permute-start | bytes 98312 | tf_op jit(solution)/shard_map/ppermute | solution.py:213
  96.0 6.1 %collective-permute-start.19 = (f32[80,128]{1,0:T(8,128)S(1)}, f32[80,128]{1,0:T(8,128)S(1)}, u32[]{:S(2)}, u32[]{:S(2)}) collective-permute-start(f32[80,128]{1,0:T(8,128)S(1)} %get-tuple-element.65), channel_id=1, source_target_pairs={{0,24},{2,26},{4,28},{6,30},{8,16},{10,18},{12,20},{14,22},{16,8},... | collective-permute-start | bytes 122888 | tf_op jit(solution)/shard_map/ppermute | solution.py:213
  97.9 4.9 %collective-permute-start.18 = (f32[80,128]{1,0:T(8,128)S(1)}, f32[80,128]{1,0:T(8,128)S(1)}, u32[]{:S(2)}, u32[]{:S(2)}) collective-permute-start(f32[80,128]{1,0:T(8,128)S(1)} %get-tuple-element.65), channel_id=1, source_target_pairs={{0,16},{2,18},{4,20},{6,22},{8,24},{10,26},{12,28},{14,30},{16,0},... | collective-permute-start | bytes 122888 | tf_op jit(solution)/shard_map/ppermute | solution.py:213
  97.9 4.9 %collective-permute-start.17 = (f32[80,128]{1,0:T(8,128)S(1)}, f32[80,128]{1,0:T(8,128)S(1)}, u32[]{:S(2)}, u32[]{:S(2)}) collective-permute-start(f32[80,128]{1,0:T(8,128)S(1)} %get-tuple-element.65), channel_id=1, source_target_pairs={{0,8},{2,10},{4,12},{6,14},{8,0},{10,2},{12,4},{14,6},{16,24},{18,... | collective-permute-start | bytes 122888 | tf_op jit(solution)/shard_map/ppermute | solution.py:213
  100.4 5.0 %collective-permute-start.26 = (f32[256,128]{1,0:T(8,128)S(1)}, f32[256,128]{1,0:T(8,128)S(1)}, u32[]{:S(2)}, u32[]{:S(2)}) collective-permute-start(f32[256,128]{1,0:T(8,128)S(1)} %bitcast.76), channel_id=1, source_target_pairs={{0,1},{1,0},{2,3},{3,2},{4,5},{5,4},{6,7},{7,6},{8,9},{9,8},{10,11... | collective-permute-start | bytes 393224 | tf_op jit(solution)/shard_map/ppermute | solution.py:213
  102.9 5.8 %collective-permute-start.20 = (f32[320,128]{1,0:T(8,128)S(1)}, f32[320,128]{1,0:T(8,128)S(1)}, u32[]{:S(2)}, u32[]{:S(2)}) collective-permute-start(f32[320,128]{1,0:T(8,128)S(1)} %bitcast.72), channel_id=1, source_target_pairs={{0,4},{2,6},{4,0},{6,2},{8,12},{10,14},{12,8},{14,10},{16,20},{18,... | collective-permute-start | bytes 491528 | tf_op jit(solution)/shard_map/ppermute | solution.py:213
  105.5 6.4 %collective-permute-start.27 = (f32[512,128]{1,0:T(8,128)S(1)}, f32[512,128]{1,0:T(8,128)S(1)}, u32[]{:S(2)}, u32[]{:S(2)}) collective-permute-start(f32[512,128]{1,0:T(8,128)S(1)} %bitcast.69), channel_id=1, source_target_pairs={{0,4},{2,6},{4,0},{6,2},{8,12},{10,14},{12,8},{14,10},{16,20},{18,... | collective-permute-start | bytes 786440 | tf_op jit(solution)/shard_map/ppermute | solution.py:213
  108.8 7.1 %collective-permute-start.21 = (f32[640,128]{1,0:T(8,128)S(1)}, f32[640,128]{1,0:T(8,128)S(1)}, u32[]{:S(2)}, u32[]{:S(2)}) collective-permute-start(f32[640,128]{1,0:T(8,128)S(1)} %bitcast.65), channel_id=1, source_target_pairs={{0,1},{1,0},{2,3},{3,2},{4,5},{5,4},{6,7},{7,6},{8,9},{9,8},{10,11... | collective-permute-start | bytes 983048 | tf_op jit(solution)/shard_map/ppermute | solution.py:213
  112.0 4.2 %collective-permute-start.28 = (f32[1024,128]{1,0:T(8,128)S(1)}, f32[1024,128]{1,0:T(8,128)S(1)}, u32[]{:S(2)}, u32[]{:S(2)}) collective-permute-start(f32[1024,128]{1,0:T(8,128)S(1)} %bitcast.63), channel_id=1, source_target_pairs={{0,2},{2,0},{4,6},{6,4},{8,10},{10,8},{12,14},{14,12},{16,18},{18,... | collective-permute-start | bytes 1572872 | tf_op jit(solution)/shard_map/ppermute | solution.py:213
  116.0 2.2 %collective-permute-start.22 = (f32[1280,128]{1,0:T(8,128)S(1)}, f32[1280,128]{1,0:T(8,128)S(1)}, u32[]{:S(2)}, u32[]{:S(2)}) collective-permute-start(f32[1280,128]{1,0:T(8,128)S(1)} %bitcast.59), channel_id=1, source_target_pairs={{0,2},{2,0},{4,6},{6,4},{8,10},{10,8},{12,14},{14,12},{16,18},{18,... | collective-permute-start | bytes 1966088 | tf_op jit(solution)/shard_map/ppermute | solution.py:213

commit v7 on v6

--- a/solution.py
+++ b/solution.py
@@ -343,11 +343,18 @@
     def panel(p, carry):
         mine = pl.ds(pl.multiple_of(p * LANES, LANES), LANES)
 
-        def update(k, inner):
-            work_ref[p] = work_ref[p] - folded(pair_ref[k], weights(pair_ref[k, mine, :]))
-            return inner
-
-        lax.fori_loop(0, p, update, 0)
+        for c in range(1, work_ref.shape[0]):
+
+            @pl.when(p == c)
+            def _(c=c):
+                first = c * LANES
+                value = work_ref[c, first:, :]
+                for k in range(c):
+                    value = value - folded(
+                        pair_ref[k, first:, :], weights(pair_ref[k, first : first + LANES, :])
+                    )
+                work_ref[c, first:, :] = value
+
         inverse_factor(work_ref[p, mine, :], inverse_ref)
         weight = weights(pair_of(inverse_ref[...]))
         solved = folded(pair_of(work_ref[p]), weight)

time: 149 us -> 147 us (0.987)
  Pallas kernels: 44.1 us -> 42.5 us
where the time goes in v7:
time: 147 us
  starting transfers between devices  51.7 us (35%)
  waiting for transfers between devices  47.2 us (32%)
  Pallas kernels  42.5 us (29%)
  local copies, waits for them, and re-layouts  3.07 us (2%)
  other arithmetic  2.15 us (1%)
    ppermute x19, waiting for transfers between devices, exchanged(): return lax.ppermute(block, axis, route)  30.7 us
    ppermute x19, starting transfers between devices, exchanged(): return lax.ppermute(block, axis, route)  27.8 us
    ppermute x10, starting transfers between devices, shifted(): return lax.ppermute(block, axis, route)  24 us
    ppermute x10, waiting for transfers between devices, shifted(): return lax.ppermute(block, axis, route)  16.4 us
    pallas_call x1, Pallas kernels, factor_halves(): kernel_call(lambda *refs: second_kernel(scale, *refs), f32(count, width),...  15.9 us
    pallas_call x1, Pallas kernels, factor_halves(): kernel_call(lambda *refs: first_kernel(scale, *refs), [f32(count, size),...  12.9 us
    pallas_call x5, Pallas kernels, filtered_columns(): got = kernel_call(rest, outs)(*matrix, applied, vec, *arrived, *before)  6.67 us
  transfers between devices with their start and end apart: 29, of which 18 were waited for; matrix products, arithmetic and copies ran while one was open for 1% of the time, Pallas kernels for 7%

profile of v7, /device:TPU:0, one launch (start us, length us, event | category | flops | bytes accessed | tf_op | source)
XLA Modules:
  0.0 147.2 jit_solution(14648982058786058341)
XLA Ops:
  0.0 1.0 slice.36
  1.0 5.5 %collective-permute-start = (f32[128,512]{1,0:T(8,128)S(1)}, f32[128,512]{1,0:T(8,128)S(1)}, u32[]{:S(2)}, u32[]{:S(2)}) collective-permute-start(f32[128,512]{1,0:T(8,128)S(1)} %slice.36), channel_id=1, source_target_pairs={{2,0},{4,2},{6,4},{8,6},{10,8},{12,10},{14,12},{16,14},{18,16},{20... | collective-permute-start | bytes 786440 | tf_op jit(solution)/shard_map/ppermute | solution.py:116
  6.6 1.2 copy-done.1
  7.8 0.7 copy-done.2
  8.5 1.3 shard_map.37
  9.8 1.0 shard_map.38.refs_2_
  10.8 0.4 shard_map.40
  11.2 4.5 %collective-permute-start.2 = (f32[128,512]{1,0:T(8,128)S(1)}, f32[128,512]{1,0:T(8,128)S(1)}, u32[]{:S(2)}, u32[]{:S(2)}) collective-permute-start(f32[128,512]{1,0:T(8,128)S(1)} %get-tuple-element.37), channel_id=1, source_target_pairs={{2,0},{4,2},{6,4},{8,6},{10,8},{12,10},{14,12},{16,14},{18,16},{20... | collective-permute-start | bytes 786440 | tf_op jit(solution)/shard_map/ppermute | solution.py:116
  15.6 1.5 %shard_map.39 = (f32[512,512]{1,0:T(8,128)S(1)}, f32[512,512]{1,0:T(8,128)S(1)}, f32[512,512]{1,0:T(8,128)S(1)}) custom-call(bf16[512,512]{1,0:T(8,128)(2,1)S(1)} %get-tuple-element.32.hi_ref.refs_0_, bf16[512,512]{1,0:T(8,128)(2,1)S(1)} %get-tuple-element.33.lo_ref.refs_1_, f32[512,512]{1,0:T(8,128)S(1)} %shard_map.38.refs_2_, f32[384,512]{1,0:T(8,128)S(1)} %copy-done, ...), custom_call_target="tpu_custom_call" | custom-call | tf_op jit(solution)/shard_map/pallas_call | solution.py:135
  17.2 2.5 %collective-permute-done.1.refs_4_.refs_3_ = f32[128,512]{1,0:T(8,128)S(1)} collective-permute-done((f32[128,512]{1,0:T(8,128)S(1)}, f32[128,512]{1,0:T(8,128)S(1)}, u32[]{:S(2)}, u32[]{:S(2)}) %collective-permute-start.1) | collective-permute-done | bytes 262176 | tf_op jit(solution)/shard_map/ppermute | solution.py:116
  19.7 0.4 shard_map.42
  20.1 4.6 %collective-permute-start.4 = (f32[128,512]{1,0:T(8,128)S(1)}, f32[128,512]{1,0:T(8,128)S(1)}, u32[]{:S(2)}, u32[]{:S(2)}) collective-permute-start(f32[128,512]{1,0:T(8,128)S(1)} %get-tuple-element.42), channel_id=1, source_target_pairs={{2,0},{4,2},{6,4},{8,6},{10,8},{12,10},{14,12},{16,14},{18,16},{20... | collective-permute-start | bytes 786440 | tf_op jit(solution)/shard_map/ppermute | solution.py:116
  24.7 1.5 %shard_map.41 = (f32[512,512]{1,0:T(8,128)S(1)}, f32[512,512]{1,0:T(8,128)S(1)}, f32[512,512]{1,0:T(8,128)S(1)}) custom-call(bf16[512,512]{1,0:T(8,128)(2,1)S(1)} %get-tuple-element.32.hi_ref.refs_0_, bf16[512,512]{1,0:T(8,128)(2,1)S(1)} %get-tuple-element.33.lo_ref.refs_1_, f32[512,512]{1,0:T(8,128)S(1)} %get-tuple-element.34.refs_2_, ...), custom_call_target="tpu_custom_call" | custom-call | tf_op jit(solution)/shard_map/pallas_call | solution.py:135
  26.3 2.5 %collective-permute-done.3.refs_4_.refs_3_ = f32[128,512]{1,0:T(8,128)S(1)} collective-permute-done((f32[128,512]{1,0:T(8,128)S(1)}, f32[128,512]{1,0:T(8,128)S(1)}, u32[]{:S(2)}, u32[]{:S(2)}) %collective-permute-start.3) | collective-permute-done | bytes 262176 | tf_op jit(solution)/shard_map/ppermute | solution.py:116
  28.8 0.4 shard_map.44
  29.3 4.6 %collective-permute-start.6 = (f32[128,512]{1,0:T(8,128)S(1)}, f32[128,512]{1,0:T(8,128)S(1)}, u32[]{:S(2)}, u32[]{:S(2)}) collective-permute-start(f32[128,512]{1,0:T(8,128)S(1)} %get-tuple-element.47), channel_id=1, source_target_pairs={{2,0},{4,2},{6,4},{8,6},{10,8},{12,10},{14,12},{16,14},{18,16},{20... | collective-permute-start | bytes 786440 | tf_op jit(solution)/shard_map/ppermute | solution.py:116
  33.9 1.5 %shard_map.43 = (f32[512,512]{1,0:T(8,128)S(1)}, f32[512,512]{1,0:T(8,128)S(1)}, f32[512,512]{1,0:T(8,128)S(1)}) custom-call(bf16[512,512]{1,0:T(8,128)(2,1)S(1)} %get-tuple-element.32.hi_ref.refs_0_, bf16[512,512]{1,0:T(8,128)(2,1)S(1)} %get-tuple-element.33.lo_ref.refs_1_, f32[512,512]{1,0:T(8,128)S(1)} %get-tuple-element.39.refs_2_, ...), custom_call_target="tpu_custom_call" | custom-call | tf_op jit(solution)/shard_map/pallas_call | solution.py:135
  35.4 2.5 %collective-permute-done.5.refs_4_.refs_3_ = f32[128,512]{1,0:T(8,128)S(1)} collective-permute-done((f32[128,512]{1,0:T(8,128)S(1)}, f32[128,512]{1,0:T(8,128)S(1)}, u32[]{:S(2)}, u32[]{:S(2)}) %collective-permute-start.5) | collective-permute-done | bytes 262176 | tf_op jit(solution)/shard_map/ppermute | solution.py:116
  37.9 0.4 shard_map.46
  38.4 4.6 %collective-permute-start.8 = (f32[128,512]{1,0:T(8,128)S(1)}, f32[128,512]{1,0:T(8,128)S(1)}, u32[]{:S(2)}, u32[]{:S(2)}) collective-permute-start(f32[128,512]{1,0:T(8,128)S(1)} %get-tuple-element.52), channel_id=1, source_target_pairs={{2,0},{4,2},{6,4},{8,6},{10,8},{12,10},{14,12},{16,14},{18,16},{20... | collective-permute-start | bytes 786440 | tf_op jit(solution)/shard_map/ppermute | solution.py:116
  43.0 1.5 %shard_map.45 = (f32[512,512]{1,0:T(8,128)S(1)}, f32[512,512]{1,0:T(8,128)S(1)}, f32[512,512]{1,0:T(8,128)S(1)}) custom-call(bf16[512,512]{1,0:T(8,128)(2,1)S(1)} %get-tuple-element.32.hi_ref.refs_0_, bf16[512,512]{1,0:T(8,128)(2,1)S(1)} %get-tuple-element.33.lo_ref.refs_1_, f32[512,512]{1,0:T(8,128)S(1)} %get-tuple-element.44.refs_2_, ...), custom_call_target="tpu_custom_call" | custom-call | tf_op jit(solution)/shard_map/pallas_call | solution.py:135
  44.5 2.4 %collective-permute-done.7.refs_4_.refs_3_ = f32[128,512]{1,0:T(8,128)S(1)} collective-permute-done((f32[128,512]{1,0:T(8,128)S(1)}, f32[128,512]{1,0:T(8,128)S(1)}, u32[]{:S(2)}, u32[]{:S(2)}) %collective-permute-start.7) | collective-permute-done | bytes 262176 | tf_op jit(solution)/shard_map/ppermute | solution.py:116
  46.9 0.3 shard_map.48
  47.3 0.5 shard_map.47.refs_1_
  47.9 1.6 %collective-permute-start.11 = (f32[256,512]{1,0:T(8,128)S(1)}, f32[256,512]{1,0:T(8,128)S(1)}, u32[]{:S(2)}, u32[]{:S(2)}) collective-permute-start(f32[256,512]{1,0:T(8,128)S(1)} %slice.46), channel_id=1, source_target_pairs={{0,1},{1,0},{2,3},{3,2},{4,5},{5,4},{6,7},{7,6},{8,9},{9,8},{10,11... | collective-permute-start | bytes 1572872 | tf_op jit(solution)/shard_map/ppermute | solution.py:213
  49.5 6.4 %collective-permute-done.9.refs_2_ = f32[128,512]{1,0:T(8,128)S(1)} collective-permute-done((f32[128,512]{1,0:T(8,128)S(1)}, f32[128,512]{1,0:T(8,128)S(1)}, u32[]{:S(2)}, u32[]{:S(2)}) %collective-permute-start.9) | collective-permute-done | bytes 262176 | tf_op jit(solution)/shard_map/ppermute | solution.py:116
  55.9 1.6 %collective-permute-start.10 = (f32[128,512]{1,0:T(8,128)S(1)}, f32[128,512]{1,0:T(8,128)S(1)}, u32[]{:S(2)}, u32[]{:S(2)}) collective-permute-start(f32[128,512]{1,0:T(8,128)S(1)} %slice_add_fusion), channel_id=1, source_target_pairs={{0,1},{1,0},{2,3},{3,2},{4,5},{5,4},{6,7},{7,6},{8,9},{9,8},{10,11... | collective-permute-start | bytes 786440 | tf_op jit(solution)/shard_map/ppermute | solution.py:213
  57.5 0.1 pad_add_fusion.refs_0_
  57.5 2.4 %collective-permute-done.11.refs_2_ = f32[256,512]{1,0:T(8,128)S(1)} collective-permute-done((f32[256,512]{1,0:T(8,128)S(1)}, f32[256,512]{1,0:T(8,128)S(1)}, u32[]{:S(2)}, u32[]{:S(2)}) %collective-permute-start.11) | collective-permute-done | bytes 524320 | tf_op jit(solution)/shard_map/ppermute | solution.py:213
  60.0 1.3 shard_map.49.refs_4_
  61.3 1.4 collective-permute-done.10.refs_3_
  62.8 1.7 %shard_map.50 = (f32[1152,128]{1,0:T(8,128)S(1)}, f32[1152,128]{1,0:T(8,128)S(1)}) custom-call(s32[2]{0:T(128)S(1)} %pad_add_fusion.refs_0_, f32[384,512]{1,0:T(8,128)S(1)} %shard_map.47.refs_1_, f32[128,512]{1,0:T(8,128)S(1)} %collective-permute-done.9.refs_2_, f32[128,512]{1,0:T(8,128)S(1)} %collective-permute-done.10.refs_3_, ...), custom_call_target="tpu_custom_call" | custom-call | tf_op jit(solution)/shard_map/pallas_call | solution.py:553
  64.4 0.1 collective-permute-start.12
  64.6 2.1 %collective-permute-done.12 = f32[1152,128]{1,0:T(8,128)} collective-permute-done((f32[1152,128]{1,0:T(8,128)S(1)}, f32[1152,128]{1,0:T(8,128)}, u32[]{:S(2)}, u32[]{:S(2)}) %collective-permute-start.12) | collective-permute-done | bytes 589856 | tf_op jit(solution)/shard_map/ppermute | solution.py:213
  66.6 1.1 add.68
  67.8 0.1 collective-permute-start.13
  68.0 9.0 %collective-permute-done.13 = f32[576,128]{1,0:T(8,128)S(1)} collective-permute-done((f32[576,128]{1,0:T(8,128)S(1)}, f32[576,128]{1,0:T(8,128)S(1)}, u32[]{:S(2)}, u32[]{:S(2)}) %collective-permute-start.13) | collective-permute-done | bytes 294944 | tf_op jit(solution)/shard_map/ppermute | solution.py:213
  77.0 8.8 %collective-permute-start.16 = (f32[144,128]{1,0:T(8,128)S(1)}, f32[144,128]{1,0:T(8,128)S(1)}, u32[]{:S(2)}, u32[]{:S(2)}) collective-permute-start(f32[144,128]{1,0:T(8,128)S(1)} %get-tuple-element.60), channel_id=1, source_target_pairs={{0,24},{2,26},{4,28},{6,30},{8,16},{10,18},{12,20},{14,22},{16,8},... | collective-permute-start | bytes 221192 | tf_op jit(solution)/shard_map/ppermute | solution.py:213
  85.8 0.6 collective-permute-start.14
  86.5 1.9 %collective-permute-done.16 = f32[144,128]{1,0:T(8,128)S(1)} collective-permute-done((f32[144,128]{1,0:T(8,128)S(1)}, f32[144,128]{1,0:T(8,128)S(1)}, u32[]{:S(2)}, u32[]{:S(2)}) %collective-permute-start.16) | collective-permute-done | bytes 73760 | tf_op jit(solution)/shard_map/ppermute | solution.py:213
  88.4 2.6 %collective-permute-done.15 = f32[144,128]{1,0:T(8,128)S(1)} collective-permute-done((f32[144,128]{1,0:T(8,128)S(1)}, f32[144,128]{1,0:T(8,128)S(1)}, u32[]{:S(2)}, u32[]{:S(2)}) %collective-permute-start.15) | collective-permute-done | bytes 73760 | tf_op jit(solution)/shard_map/ppermute | solution.py:213
  91.0 0.4 collective-permute-done.14
  91.5 2.0 %collective-permute-start.25 = (f32[64,128]{1,0:T(8,128)S(1)}, f32[64,128]{1,0:T(8,128)S(1)}, u32[]{:S(2)}, u32[]{:S(2)}) collective-permute-start(f32[64,128]{1,0:T(8,128)S(1)} %get-tuple-element.63), channel_id=1, source_target_pairs={{0,24},{2,26},{4,28},{6,30},{8,16},{10,18},{12,20},{14,22},{16,8},... | collective-permute-start | bytes 98312 | tf_op jit(solution)/shard_map/ppermute | solution.py:213
  93.5 0.5 collective-permute-start.24
  94.0 2.0 %collective-permute-start.23 = (f32[64,128]{1,0:T(8,128)S(1)}, f32[64,128]{1,0:T(8,128)S(1)}, u32[]{:S(2)}, u32[]{:S(2)}) collective-permute-start(f32[64,128]{1,0:T(8,128)S(1)} %get-tuple-element.63), channel_id=1, source_target_pairs={{0,8},{2,10},{4,12},{6,14},{8,0},{10,2},{12,4},{14,6},{16,24},{18,... | collective-permute-start | bytes 98312 | tf_op jit(solution)/shard_map/ppermute | solution.py:213
  96.0 2.0 %collective-permute-start.19 = (f32[80,128]{1,0:T(8,128)S(1)}, f32[80,128]{1,0:T(8,128)S(1)}, u32[]{:S(2)}, u32[]{:S(2)}) collective-permute-start(f32[80,128]{1,0:T(8,128)S(1)} %get-tuple-element.65), channel_id=1, source_target_pairs={{0,24},{2,26},{4,28},{6,30},{8,16},{10,18},{12,20},{14,22},{16,8},... | collective-permute-start | bytes 122888 | tf_op jit(solution)/shard_map/ppermute | solution.py:213
  97.9 2.4 %collective-permute-start.17 = (f32[80,128]{1,0:T(8,128)S(1)}, f32[80,128]{1,0:T(8,128)S(1)}, u32[]{:S(2)}, u32[]{:S(2)}) collective-permute-start(f32[80,128]{1,0:T(8,128)S(1)} %get-tuple-element.65), channel_id=1, source_target_pairs={{0,8},{2,10},{4,12},{6,14},{8,0},{10,2},{12,4},{14,6},{16,24},{18,... | collective-permute-start | bytes 122888 | tf_op jit(solution)/shard_map/ppermute | solution.py:213
  100.4 1.6 %collective-permute-start.26 = (f32[256,128]{1,0:T(8,128)S(1)}, f32[256,128]{1,0:T(8,128)S(1)}, u32[]{:S(2)}, u32[]{:S(2)}) collective-permute-start(f32[256,128]{1,0:T(8,128)S(1)} %bitcast.76), channel_id=1, source_target_pairs={{0,1},{1,0},{2,3},{3,2},{4,5},{5,4},{6,7},{7,6},{8,9},{9,8},{10,11... | collective-permute-start | bytes 393224 | tf_op jit(solution)/shard_map/ppermute | solution.py:213
  102.0 0.8 collective-permute-done.18
  102.9 1.4 collective-permute-start.20
  104.3 1.1 collective-permute-done.26
  105.5 1.4 collective-permute-start.27
  106.9 1.8 %collective-permute-done.20 = f32[320,128]{1,0:T(8,128)S(1)} collective-permute-done((f32[320,128]{1,0:T(8,128)S(1)}, f32[320,128]{1,0:T(8,128)S(1)}, u32[]{:S(2)}, u32[]{:S(2)}) %collective-permute-start.20) | collective-permute-done | bytes 163872 | tf_op jit(solution)/shard_map/ppermute | solution.py:213
  108.8 1.6 %collective-permute-start.21 = (f32[640,128]{1,0:T(8,128)S(1)}, f32[640,128]{1,0:T(8,128)S(1)}, u32[]{:S(2)}, u32[]{:S(2)}) collective-permute-start(f32[640,128]{1,0:T(8,128)S(1)} %bitcast.65), channel_id=1, source_target_pairs={{0,1},{1,0},{2,3},{3,2},{4,5},{5,4},{6,7},{7,6},{8,9},{9,8},{10,11... | collective-permute-start | bytes 983048 | tf_op jit(solution)/shard_map/ppermute | solution.py:213
  110.4 1.6 %collective-permute-done.27 = f32[512,128]{1,0:T(8,128)S(1)} collective-permute-done((f32[512,128]{1,0:T(8,128)S(1)}, f32[512,128]{1,0:T(8,128)S(1)}, u32[]{:S(2)}, u32[]{:S(2)}) %collective-permute-start.27) | collective-permute-done | bytes 262176 | tf_op jit(solution)/shard_map/ppermute | solution.py:213
  112.0 0.1 collective-permute-start.28
  112.1 3.8 %collective-permute-done.21 = f32[640,128]{1,0:T(8,128)S(1)} collective-permute-done((f32[640,128]{1,0:T(8,128)S(1)}, f32[640,128]{1,0:T(8,128)S(1)}, u32[]{:S(2)}, u32[]{:S(2)}) %collective-permute-start.21) | collective-permute-done | bytes 327712 | tf_op jit(solution)/shard_map/ppermute | solution.py:213
  116.2 0.1 maximum_select_fusion.refs_1_.refs_2_
  116.3 0.1 reverse_select_fusion.1
  116.4 1.8 %collective-permute-done.22 = f32[1280,128]{1,0:T(8,128)S(1)} collective-permute-done((f32[1280,128]{1,0:T(8,128)S(1)}, f32[1280,128]{1,0:T(8,128)S(1)}, u32[]{:S(2)}, u32[]{:S(2)}) %collective-permute-start.22) | collective-permute-done | bytes 655392 | tf_op jit(solution)/shard_map/ppermute | solution.py:213
  118.2 0.1 pad_maximum_fusion
  118.3 0.1 reverse_select_fusion
  118.4 12.9 %shard_map.51 = (f32[192,512]{1,0:T(8,128)S(1)}, bf16[4,704,256]{2,1,0:T(8,128)(2,1)S(1)}, bf16[4,256,256]{2,1,0:T(8,128)(2,1)S(1)}) custom-call(f32[2,2,640,128]{3,2,1,0:T(8,128)S(1)} %bitcast.56, f32[192,1024]{1,0:T(8,128)S(1)} %maximum_select_fusion.refs_1_.refs_2_), custom_call_target="tpu_custom_call" | custom-call | tf_op jit(solution)/shard_map/pallas_call | solution.py:475
  131.3 15.9 %shard_map.52 = f32[192,1024]{1,0:T(8,128)} custom-call(f32[2,2,640,128]{3,2,1,0:T(8,128)S(1)} %bitcast.57, f32[2,2,2,256,128]{4,3,2,1,0:T(8,128)S(1)} %bitcast.58, f32[192,1024]{1,0:T(8,128)S(1)} %maximum_select_fusion.refs_1_.refs_2_, f32[192,512]{1,0:T(8,128)S(1)} %get-tuple-element.56.refs_3_, bf16[4,704,256]{2,1,0:T(8,128)(2,1)S(1)} %get-tuple-element.57.refs_4_, ...), custom_call_target="tpu_custom_call" | custom-call | tf_op jit(solution)/shard_map/pallas_call | solution.py:481
  (52 shorter events, 1.1 us)
Async XLA Ops:
  0.0 9.8 %copy-start = (f32[384,512]{1,0:T(8,128)S(1)}, f32[384,512]{1,0:T(8,128)}, u32[]{:S(2)}) copy-start(f32[384,512]{1,0:T(8,128)} %refs_3_.1) | copy-start | bytes 2359300
  1.0 9.7 %collective-permute-start = (f32[128,512]{1,0:T(8,128)S(1)}, f32[128,512]{1,0:T(8,128)S(1)}, u32[]{:S(2)}, u32[]{:S(2)}) collective-permute-start(f32[128,512]{1,0:T(8,128)S(1)} %slice.36), channel_id=1, source_target_pairs={{2,0},{4,2},{6,4},{8,6},{10,8},{12,10},{14,12},{16,14},{18,16},{20... | collective-permute-start | bytes 786440 | tf_op jit(solution)/shard_map/ppermute | solution.py:116
  6.6 1.2 copy-start.1
  7.8 0.7 copy-start.2
  11.1 8.5 %collective-permute-start.1 = (f32[128,512]{1,0:T(8,128)S(1)}, f32[128,512]{1,0:T(8,128)S(1)}, u32[]{:S(2)}, u32[]{:S(2)}) collective-permute-start(f32[128,512]{1,0:T(8,128)S(1)} %get-tuple-element.36), channel_id=1, source_target_pairs={{30,0},{0,2},{2,4},{4,6},{6,8},{8,10},{10,12},{12,14},{14,16},{16,... | collective-permute-start | bytes 786440 | tf_op jit(solution)/shard_map/ppermute | solution.py:116
  11.2 8.5 %collective-permute-start.2 = (f32[128,512]{1,0:T(8,128)S(1)}, f32[128,512]{1,0:T(8,128)S(1)}, u32[]{:S(2)}, u32[]{:S(2)}) collective-permute-start(f32[128,512]{1,0:T(8,128)S(1)} %get-tuple-element.37), channel_id=1, source_target_pairs={{2,0},{4,2},{6,4},{8,6},{10,8},{12,10},{14,12},{16,14},{18,16},{20... | collective-permute-start | bytes 786440 | tf_op jit(solution)/shard_map/ppermute | solution.py:116
  20.1 8.8 %collective-permute-start.3 = (f32[128,512]{1,0:T(8,128)S(1)}, f32[128,512]{1,0:T(8,128)S(1)}, u32[]{:S(2)}, u32[]{:S(2)}) collective-permute-start(f32[128,512]{1,0:T(8,128)S(1)} %get-tuple-element.41), channel_id=1, source_target_pairs={{30,0},{0,2},{2,4},{4,6},{6,8},{8,10},{10,12},{12,14},{14,16},{16,... | collective-permute-start | bytes 786440 | tf_op jit(solution)/shard_map/ppermute | solution.py:116
  20.1 8.7 %collective-permute-start.4 = (f32[128,512]{1,0:T(8,128)S(1)}, f32[128,512]{1,0:T(8,128)S(1)}, u32[]{:S(2)}, u32[]{:S(2)}) collective-permute-start(f32[128,512]{1,0:T(8,128)S(1)} %get-tuple-element.42), channel_id=1, source_target_pairs={{2,0},{4,2},{6,4},{8,6},{10,8},{12,10},{14,12},{16,14},{18,16},{20... | collective-permute-start | bytes 786440 | tf_op jit(solution)/shard_map/ppermute | solution.py:116
  29.2 8.7 %collective-permute-start.5 = (f32[128,512]{1,0:T(8,128)S(1)}, f32[128,512]{1,0:T(8,128)S(1)}, u32[]{:S(2)}, u32[]{:S(2)}) collective-permute-start(f32[128,512]{1,0:T(8,128)S(1)} %get-tuple-element.46), channel_id=1, source_target_pairs={{30,0},{0,2},{2,4},{4,6},{6,8},{8,10},{10,12},{12,14},{14,16},{16,... | collective-permute-start | bytes 786440 | tf_op jit(solution)/shard_map/ppermute | solution.py:116
  29.3 8.6 %collective-permute-start.6 = (f32[128,512]{1,0:T(8,128)S(1)}, f32[128,512]{1,0:T(8,128)S(1)}, u32[]{:S(2)}, u32[]{:S(2)}) collective-permute-start(f32[128,512]{1,0:T(8,128)S(1)} %get-tuple-element.47), channel_id=1, source_target_pairs={{2,0},{4,2},{6,4},{8,6},{10,8},{12,10},{14,12},{16,14},{18,16},{20... | collective-permute-start | bytes 786440 | tf_op jit(solution)/shard_map/ppermute | solution.py:116
  38.3 8.6 %collective-permute-start.7 = (f32[128,512]{1,0:T(8,128)S(1)}, f32[128,512]{1,0:T(8,128)S(1)}, u32[]{:S(2)}, u32[]{:S(2)}) collective-permute-start(f32[128,512]{1,0:T(8,128)S(1)} %get-tuple-element.51), channel_id=1, source_target_pairs={{30,0},{0,2},{2,4},{4,6},{6,8},{8,10},{10,12},{12,14},{14,16},{16,... | collective-permute-start | bytes 786440 | tf_op jit(solution)/shard_map/ppermute | solution.py:116
  38.4 8.5 %collective-permute-start.8 = (f32[128,512]{1,0:T(8,128)S(1)}, f32[128,512]{1,0:T(8,128)S(1)}, u32[]{:S(2)}, u32[]{:S(2)}) collective-permute-start(f32[128,512]{1,0:T(8,128)S(1)} %get-tuple-element.52), channel_id=1, source_target_pairs={{2,0},{4,2},{6,4},{8,6},{10,8},{12,10},{14,12},{16,14},{18,16},{20... | collective-permute-start | bytes 786440 | tf_op jit(solution)/shard_map/ppermute | solution.py:116
  47.2 8.6 %collective-permute-start.9 = (f32[128,512]{1,0:T(8,128)S(1)}, f32[128,512]{1,0:T(8,128)S(1)}, u32[]{:S(2)}, u32[]{:S(2)}) collective-permute-start(f32[128,512]{1,0:T(8,128)S(1)} %shard_map.48), channel_id=1, source_target_pairs={{30,0},{0,2},{2,4},{4,6},{6,8},{8,10},{10,12},{12,14},{14,16},{16,... | collective-permute-start | bytes 786440 | tf_op jit(solution)/shard_map/ppermute | solution.py:116
  47.9 12.1 %collective-permute-start.11 = (f32[256,512]{1,0:T(8,128)S(1)}, f32[256,512]{1,0:T(8,128)S(1)}, u32[]{:S(2)}, u32[]{:S(2)}) collective-permute-start(f32[256,512]{1,0:T(8,128)S(1)} %slice.46), channel_id=1, source_target_pairs={{0,1},{1,0},{2,3},{3,2},{4,5},{5,4},{6,7},{7,6},{8,9},{9,8},{10,11... | collective-permute-start | bytes 1572872 | tf_op jit(solution)/shard_map/ppermute | solution.py:213
  55.9 5.4 %copy-start.3 = (f32[128,512]{1,0:T(8,128)}, f32[128,512]{1,0:T(8,128)S(1)}, u32[]{:S(2)}) copy-start(f32[128,512]{1,0:T(8,128)S(1)} %slice_add_fusion) | copy-start | bytes 786436
  55.9 6.9 %collective-permute-start.10 = (f32[128,512]{1,0:T(8,128)S(1)}, f32[128,512]{1,0:T(8,128)S(1)}, u32[]{:S(2)}, u32[]{:S(2)}) collective-permute-start(f32[128,512]{1,0:T(8,128)S(1)} %slice_add_fusion), channel_id=1, source_target_pairs={{0,1},{1,0},{2,3},{3,2},{4,5},{5,4},{6,7},{7,6},{8,9},{9,8},{10,11... | collective-permute-start | bytes 786440 | tf_op jit(solution)/shard_map/ppermute | solution.py:213
  64.4 2.2 %collective-permute-start.12 = (f32[1152,128]{1,0:T(8,128)S(1)}, f32[1152,128]{1,0:T(8,128)}, u32[]{:S(2)}, u32[]{:S(2)}) collective-permute-start(f32[1152,128]{1,0:T(8,128)S(1)} %get-tuple-element.55), channel_id=1, source_target_pairs={{0,2},{2,0},{4,6},{6,4},{8,10},{10,8},{12,14},{14,12},{16,18},{18,... | collective-permute-start | bytes 1769480 | tf_op jit(solution)/shard_map/ppermute | solution.py:213
  67.8 18.7 %copy-start.4 = (f32[128,512]{1,0:T(8,128)S(1)}, f32[128,512]{1,0:T(8,128)}, u32[]{:S(2)}) copy-start(f32[128,512]{1,0:T(8,128)} %copy-done.3) | copy-start | bytes 786436
  67.8 9.1 %collective-permute-start.13 = (f32[576,128]{1,0:T(8,128)S(1)}, f32[576,128]{1,0:T(8,128)S(1)}, u32[]{:S(2)}, u32[]{:S(2)}) collective-permute-start(f32[576,128]{1,0:T(8,128)S(1)} %dynamic-slice_bitcast_fusion), channel_id=1, source_target_pairs={{0,4},{2,6},{4,0},{6,2},{8,12},{10,14},{12,8},{14,10},{16,20},{18,... | collective-permute-start | bytes 884744 | tf_op jit(solution)/shard_map/ppermute | solution.py:213
  77.0 11.4 %collective-permute-start.16 = (f32[144,128]{1,0:T(8,128)S(1)}, f32[144,128]{1,0:T(8,128)S(1)}, u32[]{:S(2)}, u32[]{:S(2)}) collective-permute-start(f32[144,128]{1,0:T(8,128)S(1)} %get-tuple-element.60), channel_id=1, source_target_pairs={{0,24},{2,26},{4,28},{6,30},{8,16},{10,18},{12,20},{14,22},{16,8},... | collective-permute-start | bytes 221192 | tf_op jit(solution)/shard_map/ppermute | solution.py:213
  85.8 5.3 %collective-permute-start.15 = (f32[144,128]{1,0:T(8,128)S(1)}, f32[144,128]{1,0:T(8,128)S(1)}, u32[]{:S(2)}, u32[]{:S(2)}) collective-permute-start(f32[144,128]{1,0:T(8,128)S(1)} %get-tuple-element.61), channel_id=1, source_target_pairs={{0,16},{2,18},{4,20},{6,22},{8,24},{10,26},{12,28},{14,30},{16,0},... | collective-permute-start | bytes 221192 | tf_op jit(solution)/shard_map/ppermute | solution.py:213
  85.8 5.7 %collective-permute-start.14 = (f32[144,128]{1,0:T(8,128)S(1)}, f32[144,128]{1,0:T(8,128)S(1)}, u32[]{:S(2)}, u32[]{:S(2)}) collective-permute-start(f32[144,128]{1,0:T(8,128)S(1)} %get-tuple-element.59), channel_id=1, source_target_pairs={{0,8},{2,10},{4,12},{6,14},{8,0},{10,2},{12,4},{14,6},{16,24},{18,... | collective-permute-start | bytes 221192 | tf_op jit(solution)/shard_map/ppermute | solution.py:213
  91.5 6.4 %collective-permute-start.25 = (f32[64,128]{1,0:T(8,128)S(1)}, f32[64,128]{1,0:T(8,128)S(1)}, u32[]{:S(2)}, u32[]{:S(2)}) collective-permute-start(f32[64,128]{1,0:T(8,128)S(1)} %get-tuple-element.63), channel_id=1, source_target_pairs={{0,24},{2,26},{4,28},{6,30},{8,16},{10,18},{12,20},{14,22},{16,8},... | collective-permute-start | bytes 98312 | tf_op jit(solution)/shard_map/ppermute | solution.py:213
  93.5 6.8 %collective-permute-start.24 = (f32[64,128]{1,0:T(8,128)S(1)}, f32[64,128]{1,0:T(8,128)S(1)}, u32[]{:S(2)}, u32[]{:S(2)}) collective-permute-start(f32[64,128]{1,0:T(8,128)S(1)} %get-tuple-element.63), channel_id=1, source_target_pairs={{0,16},{2,18},{4,20},{6,22},{8,24},{10,26},{12,28},{14,30},{16,0},... | collective-permute-start | bytes 98312 | tf_op jit(solution)/shard_map/ppermute | solution.py:213
  94.0 6.4 %collective-permute-start.23 = (f32[64,128]{1,0:T(8,128)S(1)}, f32[64,128]{1,0:T(8,128)S(1)}, u32[]{:S(2)}, u32[]{:S(2)}) collective-permute-start(f32[64,128]{1,0:T(8,128)S(1)} %get-tuple-element.63), channel_id=1, source_target_pairs={{0,8},{2,10},{4,12},{6,14},{8,0},{10,2},{12,4},{14,6},{16,24},{18,... | collective-permute-start | bytes 98312 | tf_op jit(solution)/shard_map/ppermute | solution.py:213
  96.0 6.1 %collective-permute-start.19 = (f32[80,128]{1,0:T(8,128)S(1)}, f32[80,128]{1,0:T(8,128)S(1)}, u32[]{:S(2)}, u32[]{:S(2)}) collective-permute-start(f32[80,128]{1,0:T(8,128)S(1)} %get-tuple-element.65), channel_id=1, source_target_pairs={{0,24},{2,26},{4,28},{6,30},{8,16},{10,18},{12,20},{14,22},{16,8},... | collective-permute-start | bytes 122888 | tf_op jit(solution)/shard_map/ppermute | solution.py:213
  97.9 4.9 %collective-permute-start.18 = (f32[80,128]{1,0:T(8,128)S(1)}, f32[80,128]{1,0:T(8,128)S(1)}, u32[]{:S(2)}, u32[]{:S(2)}) collective-permute-start(f32[80,128]{1,0:T(8,128)S(1)} %get-tuple-element.65), channel_id=1, source_target_pairs={{0,16},{2,18},{4,20},{6,22},{8,24},{10,26},{12,28},{14,30},{16,0},... | collective-permute-start | bytes 122888 | tf_op jit(solution)/shard_map/ppermute | solution.py:213
  97.9 4.9 %collective-permute-start.17 = (f32[80,128]{1,0:T(8,128)S(1)}, f32[80,128]{1,0:T(8,128)S(1)}, u32[]{:S(2)}, u32[]{:S(2)}) collective-permute-start(f32[80,128]{1,0:T(8,128)S(1)} %get-tuple-element.65), channel_id=1, source_target_pairs={{0,8},{2,10},{4,12},{6,14},{8,0},{10,2},{12,4},{14,6},{16,24},{18,... | collective-permute-start | bytes 122888 | tf_op jit(solution)/shard_map/ppermute | solution.py:213
  100.4 5.0 %collective-permute-start.26 = (f32[256,128]{1,0:T(8,128)S(1)}, f32[256,128]{1,0:T(8,128)S(1)}, u32[]{:S(2)}, u32[]{:S(2)}) collective-permute-start(f32[256,128]{1,0:T(8,128)S(1)} %bitcast.76), channel_id=1, source_target_pairs={{0,1},{1,0},{2,3},{3,2},{4,5},{5,4},{6,7},{7,6},{8,9},{9,8},{10,11... | collective-permute-start | bytes 393224 | tf_op jit(solution)/shard_map/ppermute | solution.py:213
  102.9 5.8 %collective-permute-start.20 = (f32[320,128]{1,0:T(8,128)S(1)}, f32[320,128]{1,0:T(8,128)S(1)}, u32[]{:S(2)}, u32[]{:S(2)}) collective-permute-start(f32[320,128]{1,0:T(8,128)S(1)} %bitcast.72), channel_id=1, source_target_pairs={{0,4},{2,6},{4,0},{6,2},{8,12},{10,14},{12,8},{14,10},{16,20},{18,... | collective-permute-start | bytes 491528 | tf_op jit(solution)/shard_map/ppermute | solution.py:213
  105.5 6.4 %collective-permute-start.27 = (f32[512,128]{1,0:T(8,128)S(1)}, f32[512,128]{1,0:T(8,128)S(1)}, u32[]{:S(2)}, u32[]{:S(2)}) collective-permute-start(f32[512,128]{1,0:T(8,128)S(1)} %bitcast.69), channel_id=1, source_target_pairs={{0,4},{2,6},{4,0},{6,2},{8,12},{10,14},{12,8},{14,10},{16,20},{18,... | collective-permute-start | bytes 786440 | tf_op jit(solution)/shard_map/ppermute | solution.py:213
  108.8 7.1 %collective-permute-start.21 = (f32[640,128]{1,0:T(8,128)S(1)}, f32[640,128]{1,0:T(8,128)S(1)}, u32[]{:S(2)}, u32[]{:S(2)}) collective-permute-start(f32[640,128]{1,0:T(8,128)S(1)} %bitcast.65), channel_id=1, source_target_pairs={{0,1},{1,0},{2,3},{3,2},{4,5},{5,4},{6,7},{7,6},{8,9},{9,8},{10,11... | collective-permute-start | bytes 983048 | tf_op jit(solution)/shard_map/ppermute | solution.py:213
  112.0 4.2 %collective-permute-start.28 = (f32[1024,128]{1,0:T(8,128)S(1)}, f32[1024,128]{1,0:T(8,128)S(1)}, u32[]{:S(2)}, u32[]{:S(2)}) collective-permute-start(f32[1024,128]{1,0:T(8,128)S(1)} %bitcast.63), channel_id=1, source_target_pairs={{0,2},{2,0},{4,6},{6,4},{8,10},{10,8},{12,14},{14,12},{16,18},{18,... | collective-permute-start | bytes 1572872 | tf_op jit(solution)/shard_map/ppermute | solution.py:213
  116.0 2.2 %collective-permute-start.22 = (f32[1280,128]{1,0:T(8,128)S(1)}, f32[1280,128]{1,0:T(8,128)S(1)}, u32[]{:S(2)}, u32[]{:S(2)}) collective-permute-start(f32[1280,128]{1,0:T(8,128)S(1)} %bitcast.59), channel_id=1, source_target_pairs={{0,2},{2,0},{4,6},{6,4},{8,10},{10,8},{12,14},{14,12},{16,18},{18,... | collective-permute-start | bytes 1966088 | tf_op jit(solution)/shard_map/ppermute | solution.py:213
